TPU v7x, 256 devices: a whole 4x4x8 slice. The times are simulated.
256 devices in a mesh: shot: 16 (over z_hi, y, core), dom: 16 (over x, z_lo).
Axes of the slice: x: 4, y: 4, z: 8 (z_hi: 2, z_lo: 4; z = z_hi * 4 + z_lo), core: 2. Of those that a mesh axis runs over, the one named last changes fastest.
Arguments:
- model_slab: float32 [256, 128, 128], P('dom'), may hold values from 0.0225 to 0.17
- wave_prev: float32 [16, 256, 128, 128], P('shot', 'dom'), may hold values from -6 to 6
- wave_now: float32 [16, 256, 128, 128], P('shot', 'dom'), may hold values from -6 to 6
- adjoint_next: float32 [16, 256, 128, 128], P('shot', 'dom'), may hold values from -6 to 6
- adjoint_now: float32 [16, 256, 128, 128], P('shot', 'dom'), may hold values from -6 to 6
- wavelet: float32 [16, 8], P('shot'), may hold values from -12 to 12
- source_cell: int32 [16], P('shot'), may hold values from 0 to 4194303
- receiver_cells: int32 [16, 256], P('shot'), may hold values from 0 to 4194303
- observed: float32 [16, 8, 256], P('shot'), may hold values from -6 to 6
Outputs:
- direction: float32 [256, 128, 128], P('dom')
- new_model: float32 [256, 128, 128], P('dom')
Inputs may be any that keep to these rules, and one draw needn't show every extreme that they name: `source_cell`: flat cell index x * 128 * 128 + y * 128 + z. `receiver_cells`: flat cell indices x * 128 * 128 + y * 128 + z; a cell may repeat.
All inputs are finite; a program needn't handle non-finite values. Where the computation divides by a largest or mean magnitude, that divisor is 1e-20 or more.
Results may differ from a plain program's by a relative error of at most 0.000025.
Values sent between devices are 32-bit elements; how exact they have to be, the bound alone decides.
No kernel may reach another device: no remote copies, remote signals or barrier semaphores. Data moves between devices by JAX's collectives and lax.ppermute only.
A program may use at most 192 MiB of HBM per device.

v0:
```python
import jax
import jax.numpy as jnp
from jax import lax
from jax.sharding import PartitionSpec as P

STEPS = 8


COEFFS = (8.0 / 5.0, -1.0 / 5.0, 8.0 / 315.0, -1.0 / 560.0)
CENTRE = -205.0 / 72.0
STEP_FRACTION = 0.1
EPSILON = 1e-06


def padded_2(cells, sides, width):
    for axis, dim in sides:
        count = lax.axis_size(axis)
        ends = count - 1
        head = lax.slice_in_dim(cells, 0, width, axis=dim)
        tail = lax.slice_in_dim(cells, cells.shape[dim] - width, cells.shape[dim], axis=dim)
        cells = jnp.concatenate(
            [
                lax.ppermute(tail, axis, [(i, (i + 1) % count) for i in range(ends)]),
                cells,
                lax.ppermute(head, axis, [((i + 1) % count, i) for i in range(ends)]),
            ],
            axis=dim,
        )
    return cells


def shifted(field, axis, offset):
    length = field.shape[axis]
    filler_shape = list(field.shape)
    filler_shape[axis] = abs(offset)
    filler = jnp.zeros(filler_shape, field.dtype)
    if offset > 0:
        return jnp.concatenate([lax.slice_in_dim(field, offset, length, axis=axis), filler], axis)
    return jnp.concatenate([filler, lax.slice_in_dim(field, 0, length + offset, axis=axis)], axis)


def laplace(padded):
    rows = padded.shape[0] - 8
    field = padded[4 : 4 + rows]
    total = 3.0 * CENTRE * field
    for index, weight in enumerate(COEFFS):
        offset = index + 1
        total = total + weight * (
            padded[4 + offset : 4 + offset + rows] + padded[4 - offset : 4 - offset + rows]
        )
    for axis in (1, 2):
        for index, weight in enumerate(COEFFS):
            offset = index + 1
            total = total + weight * (shifted(field, axis, offset) + shifted(field, axis, -offset))
    return total


def add_at(field, start_row, targets, amounts):
    count = field.size
    plane = field.shape[1] * field.shape[2]
    relative = targets - start_row * plane
    inside = (relative >= 0) & (relative < count)
    slots = jnp.clip(relative, 0, count - 1)
    values = jnp.where(inside, amounts, 0.0)
    return field.reshape(-1).at[slots].add(values).reshape(field.shape)


def on_device(
    model_slab,
    wave_prev,
    wave_now,
    adjoint_next,
    adjoint_now,
    wavelet,
    source_cell,
    receiver_cells,
    observed,
):
    shape = model_slab.shape
    rows = shape[0]
    cells = shape[0] * shape[1] * shape[2]
    own_row = lax.axis_index("dom") * rows
    first_cell = own_row * shape[1] * shape[2]
    source_one = source_cell[0]
    receivers = receiver_cells[0]
    receiver_local = receivers - first_cell
    receiver_inside = (receiver_local >= 0) & (receiver_local < cells)
    receiver_slots = jnp.clip(receiver_local, 0, cells - 1)
    images = []
    residuals = []
    gradient = jnp.zeros(shape, jnp.float32)
    older, current = (wave_prev[0], wave_now[0])
    for tick in range(STEPS):
        padded = padded_2(current, (("dom", 0),), 4)
        image = laplace(padded)
        newer = 2.0 * current - older + model_slab * image
        newer = add_at(newer, own_row, source_one, wavelet[0, tick])
        values = newer.reshape(-1)[receiver_slots] - observed[0, tick]
        residuals.append(jnp.where(receiver_inside, values, 0.0))
        images.append(image)
        older, current = (current, newer)
    later, present = (adjoint_next[0], adjoint_now[0])
    for tick in reversed(range(STEPS)):
        padded = padded_2(present, (("dom", 0),), 4)
        earlier = 2.0 * present - later + model_slab * laplace(padded)
        earlier = add_at(earlier, own_row, receivers, residuals[tick])
        gradient = gradient + earlier * images[tick]
        later, present = (present, earlier)
    total = lax.psum(gradient, "shot")
    peak = lax.pmax(jnp.max(jnp.abs(total)), "dom")
    direction = total / (peak + EPSILON)
    new_model = model_slab * (1.0 - STEP_FRACTION * direction)
    return (direction, new_model)


def solution(mesh):
    placed = (
        P("dom", None, None),
        P("shot", "dom", None, None),
        P("shot", "dom", None, None),
        P("shot", "dom", None, None),
        P("shot", "dom", None, None),
        P("shot", None),
        P("shot"),
        P("shot", None),
        P("shot", None, None),
    )
    return jax.shard_map(
        on_device,
        mesh=mesh,
        in_specs=placed,
        out_specs=(P("dom", None, None), P("dom", None, None)),
        check_vma=False,
    )
```

profile of v0, /device:TPU:0, one launch (start us, length us, event | category | flops | bytes accessed | tf_op | source)
XLA Modules:
  0.0 704.9 jit_solution(66041510398555331)
XLA Ops:
  10.5 5.3 collective-permute-start.1
  17.1 4.6 collective-permute-start.3
  54.4 9.5 %fusion.432 = (f32[16,128,128]{2,1,0:T(8,128)S(1)}, f32[16,128,128]{2,1,0:T(8,128)}) fusion(f32[1,16,128,128]{3,2,1,0:T(8,128)} %param.26, f32[16,128,128]{2,1,0:T(8,128)} %param.25, f32[1,16,128,128]{3,2,1,0:T(8,128)S(1)} %copy-done.9, f32[16,128,124]{2,1,0:T(8,128)} %get-tuple-element.385, f32[16,128,124]{2,1,0:T(8,128)} %get-tuple-element.384, ...), kind=kLoop, calls=%fused_computation.673 | loop fusion | flops 12845056 | bytes 23265280 | tf_op jit(solution)/shard_map/add | solution.py:96
  78.1 2.1 collective-permute-start.4
  80.7 7.3 %fusion.388 = f32[16,128,128]{2,1,0:T(8,128)S(1)} fusion(f32[16,128,128]{2,1,0:T(8,128)S(1)} %copy-done.13, f32[16,128,128]{2,1,0:T(8,128)S(1)} %bitcast.275, f32[4,128,128]{2,1,0:T(8,128)} %collective-permute-done.1, f32[4,128,128]{2,1,0:T(8,128)S(1)} %collective-permute-done, f32[1,16,128,128]{3,2,1,0:T(8,128)} %param.28, ...), kind=kLoop, calls=%fused_computation.596 | loop fusion | flops 12845056 | bytes 21168128 | tf_op jit(solution)/shard_map/add | solution.py:105
  89.6 5.6 collective-permute-done.4
  95.3 5.5 multiply_add_fusion.7
  104.7 3.9 collective-permute-start.7
  111.4 2.5 collective-permute-done.7
  113.9 10.0 %collective-permute-done.6 = f32[4,128,128]{2,1,0:T(8,128)S(1)} collective-permute-done((f32[4,128,128]{2,1,0:T(8,128)S(1)}, f32[4,128,128]{2,1,0:T(8,128)S(1)}, u32[]{:S(2)}, u32[]{:S(2)}) %collective-permute-start.6) | collective-permute-done | bytes 262176 | tf_op jit(solution)/shard_map/ppermute | solution.py:25
  123.9 7.4 %multiply_add_fusion.6 = (f32[16,128,128]{2,1,0:T(8,128)S(1)}, f32[16,128,128]{2,1,0:T(8,128)}) fusion(f32[16,128,128]{2,1,0:T(8,128)S(1)} %copy-done.14, f32[16,128,128]{2,1,0:T(8,128)S(1)} %bitcast.225, f32[16,128,128]{2,1,0:T(8,128)} %bitcast.235, f32[16,128,124]{2,1,0:T(8,128)S(1)} %get-tuple-element.349, f32[16,128,124]{2,1,0:T(8,128)S(1)} %get-tuple-element.348, ...), kind=kLoop, calls=%fused_computation.683 | loop fusion | flops 12845056 | bytes 22216704 | tf_op jit(solution)/shard_map/add | solution.py:96
  135.2 3.7 collective-permute-start.9
  144.2 9.8 %collective-permute-done.8 = f32[4,128,128]{2,1,0:T(8,128)S(1)} collective-permute-done((f32[4,128,128]{2,1,0:T(8,128)S(1)}, f32[4,128,128]{2,1,0:T(8,128)S(1)}, u32[]{:S(2)}, u32[]{:S(2)}) %collective-permute-start.8) | collective-permute-done | bytes 262176 | tf_op jit(solution)/shard_map/ppermute | solution.py:25
  154.0 5.4 multiply_add_fusion.5
  163.3 2.3 collective-permute-start.11
  168.4 2.9 collective-permute-done.11
  171.3 9.9 %collective-permute-done.10 = f32[4,128,128]{2,1,0:T(8,128)S(1)} collective-permute-done((f32[4,128,128]{2,1,0:T(8,128)S(1)}, f32[4,128,128]{2,1,0:T(8,128)S(1)}, u32[]{:S(2)}, u32[]{:S(2)}) %collective-permute-start.10) | collective-permute-done | bytes 262176 | tf_op jit(solution)/shard_map/ppermute | solution.py:25
  181.2 5.5 multiply_add_fusion.4
  188.2 10.2 %gather_fusion.3 = f32[256]{0:T(256)S(1)} fusion(f32[262144]{0:T(1024)} %fusion.437, s32[1024]{0:T(1024)S(1)} %pad_clamp_fusion), kind=kCustom, calls=%fused_computation.3 | custom fusion | bytes 3072 | tf_op jit(solution)/shard_map/gather | solution.py:98
  216.1 2.9 fusion.537
  219.4 6.0 collective-permute-done.12
  225.4 7.6 %multiply_add_fusion.3 = (f32[16,128,128]{2,1,0:T(8,128)S(1)}, f32[16,128,128]{2,1,0:T(8,128)}) fusion(f32[16,128,128]{2,1,0:T(8,128)S(1)} %copy-done.17, f32[16,128,128]{2,1,0:T(8,128)S(1)} %bitcast.203, f32[16,128,128]{2,1,0:T(8,128)} %bitcast.40, f32[16,128,124]{2,1,0:T(8,128)S(1)} %get-tuple-element.295, f32[16,128,124]{2,1,0:T(8,128)S(1)} %get-tuple-element.294, ...), kind=kLoop, calls=%fused_computation.680 | loop fusion | flops 12845056 | bytes 22216704 | tf_op jit(solution)/shard_map/add | solution.py:96
  237.1 2.5 collective-permute-start.15
  244.3 6.0 collective-permute-done.14
  250.4 5.5 multiply_add_fusion.2
  259.7 2.3 collective-permute-start.17
  266.6 6.4 collective-permute-done.16
  273.1 5.6 multiply_add_fusion.1
  280.1 10.1 %gather_fusion = f32[256]{0:T(256)S(1)} fusion(f32[262144]{0:T(1024)} %fusion.440, s32[1024]{0:T(1024)S(1)} %pad_clamp_fusion), kind=kCustom, calls=%fused_computation | custom fusion | bytes 3072 | tf_op jit(solution)/shard_map/gather | solution.py:98
  290.3 2.6 scatter_fusion
  294.9 2.1 collective-permute-start.19
  301.3 5.3 collective-permute-done.18
  306.6 3.6 fusion.170
  310.2 2.6 scatter_fusion.1
  314.8 2.3 collective-permute-start.21
  318.9 2.7 collective-permute-done.21
  321.6 5.6 collective-permute-done.20
  327.3 3.6 fusion.144
  330.8 2.6 scatter_fusion.2
  335.4 2.3 collective-permute-start.23
  339.7 2.7 collective-permute-done.23
  342.5 5.8 collective-permute-done.22
  348.3 4.3 fusion.118
  352.6 4.4 scatter_fusion.3
  360.3 2.3 collective-permute-start.25
  364.4 3.0 collective-permute-done.25
  367.4 5.9 collective-permute-done.24
  373.3 5.6 fusion.92
  378.9 4.4 scatter_fusion.4
  386.6 2.3 collective-permute-start.27
  393.7 5.9 collective-permute-done.26
  399.6 5.7 fusion.66
  405.3 4.4 scatter_fusion.5
  413.1 2.3 collective-permute-start.29
  420.2 5.8 collective-permute-done.28
  426.0 5.7 fusion.40
  431.7 4.4 scatter_fusion.6
  439.4 2.3 collective-permute-start.31
  446.6 6.1 collective-permute-done.30
  452.7 5.8 fusion.14
  458.5 4.5 scatter_fusion.7
  463.0 7.7 %multiply_add_fusion = f32[16,128,128]{2,1,0:T(8,128)} fusion(f32[16,128,128]{2,1,0:T(8,128)} %bitcast.277, f32[16,128,128]{2,1,0:T(8,128)} %get-tuple-element.115, f32[16,128,128]{2,1,0:T(8,128)} %bitcast.238, f32[16,128,128]{2,1,0:T(8,128)} %get-tuple-element.113, f32[16,128,128]{2,1,0:T(8,128)} %bitcast.171, f32[16,128,128]{2,1,0:T(8,128)} %get-tuple-element.111, ...), kind=kLoop, calls=%fused_computation.677 | loop fusion | flops 3932160 | bytes 17825792 | tf_op jit(solution)/shard_map/add | solution.py:107
  470.7 179.4 %all-reduce.258.cloned.1.call-done = f32[16,128,128]{2,1,0:T(8,128)} async-done(((f32[16,128,128]{2,1,0:T(8,128)}), f32[16,128,128]{2,1,0:T(8,128)}) %all-reduce.258.cloned.1.call-update) | async-done | bytes 1048592 | tf_op jit(solution)/shard_map/psum | solution.py:109
  652.1 43.5 %pmax.7 = f32[]{:T(128)} all-reduce(f32[]{:T(128)} %abs_reduce_fusion), channel_id=1, replica_groups=mesh['shot'=16,'dom'=16] {'dom'}, use_global_device_ids=true, to_apply=%region_10.11 | all-reduce | flops 1 | bytes 8 | tf_op jit(solution)/shard_map/pmax | solution.py:110
  (295 shorter events, 154.8 us)
Async XLA Ops:
  7.2 14.6 %copy-start.11 = (f32[1,16,128,128]{3,2,1,0:T(8,128)S(1)}, f32[1,16,128,128]{3,2,1,0:T(8,128)}, u32[]{:S(2)}) copy-start(f32[1,16,128,128]{3,2,1,0:T(8,128)} %param.29) | copy-start | bytes 3145732
  7.2 14.5 %copy-start.48 = (s32[1,256]{1,0:T(1,128)S(1)}, s32[1,256]{1,0:T(1,128)}, u32[]{:S(2)}) copy-start(s32[1,256]{1,0:T(1,128)} %param.32) | copy-start | bytes 3076
  7.2 642.9 %all-reduce.258.cloned.1.call-start = ((), (), s32[]{:S(2)}) async-start(), calls=%async_computation | async-start | bytes 2097152 | tf_op jit(solution)/shard_map/psum | solution.py:109
  9.2 71.3 %collective-permute-start = (f32[4,128,128]{2,1,0:T(8,128)}, f32[4,128,128]{2,1,0:T(8,128)S(1)}, u32[]{:S(2)}, u32[]{:S(2)}) collective-permute-start(f32[4,128,128]{2,1,0:T(8,128)} %get-tuple-element.402), channel_id=1, source_target_pairs={{1,0},{2,1},{3,2},{4,3},{5,4},{6,5},{7,6},{8,7},{9,8},{10,9},{11,1... | collective-permute-start | bytes 786440 | tf_op jit(solution)/shard_map/ppermute | solution.py:25
  10.5 70.0 %collective-permute-start.1 = (f32[4,128,128]{2,1,0:T(8,128)}, f32[4,128,128]{2,1,0:T(8,128)}, u32[]{:S(2)}, u32[]{:S(2)}) collective-permute-start(f32[4,128,128]{2,1,0:T(8,128)} %get-tuple-element.403), channel_id=1, source_target_pairs={{0,1},{1,2},{2,3},{3,4},{4,5},{5,6},{6,7},{7,8},{8,9},{9,10},{10,1... | collective-permute-start | bytes 786440 | tf_op jit(solution)/shard_map/ppermute | solution.py:23
  15.8 37.8 %collective-permute-start.2 = (f32[4,128,128]{2,1,0:T(8,128)S(1)}, f32[4,128,128]{2,1,0:T(8,128)S(1)}, u32[]{:S(2)}, u32[]{:S(2)}) collective-permute-start(f32[4,128,128]{2,1,0:T(8,128)S(1)} %get-tuple-element.368), channel_id=1, source_target_pairs={{1,0},{2,1},{3,2},{4,3},{5,4},{6,5},{7,6},{8,7},{9,8},{10,9},{11,1... | collective-permute-start | bytes 786440 | tf_op jit(solution)/shard_map/ppermute | solution.py:25
  17.1 36.5 %collective-permute-start.3 = (f32[4,128,128]{2,1,0:T(8,128)S(1)}, f32[4,128,128]{2,1,0:T(8,128)S(1)}, u32[]{:S(2)}, u32[]{:S(2)}) collective-permute-start(f32[4,128,128]{2,1,0:T(8,128)S(1)} %get-tuple-element.369), channel_id=1, source_target_pairs={{0,1},{1,2},{2,3},{3,4},{4,5},{5,6},{6,7},{7,8},{8,9},{9,10},{10,1... | collective-permute-start | bytes 786440 | tf_op jit(solution)/shard_map/ppermute | solution.py:23
  76.1 13.6 %collective-permute-start.5 = (f32[4,128,128]{2,1,0:T(8,128)}, f32[4,128,128]{2,1,0:T(8,128)S(1)}, u32[]{:S(2)}, u32[]{:S(2)}) collective-permute-start(f32[4,128,128]{2,1,0:T(8,128)} %bitcast.18), channel_id=1, source_target_pairs={{0,1},{1,2},{2,3},{3,4},{4,5},{5,6},{6,7},{7,8},{8,9},{9,10},{10,1... | collective-permute-start | bytes 786440 | tf_op jit(solution)/shard_map/ppermute | solution.py:23
  78.1 17.2 %collective-permute-start.4 = (f32[4,128,128]{2,1,0:T(8,128)}, f32[4,128,128]{2,1,0:T(8,128)S(1)}, u32[]{:S(2)}, u32[]{:S(2)}) collective-permute-start(f32[4,128,128]{2,1,0:T(8,128)} %bitcast.17), channel_id=1, source_target_pairs={{1,0},{2,1},{3,2},{4,3},{5,4},{6,5},{7,6},{8,7},{9,8},{10,9},{11,1... | collective-permute-start | bytes 786440 | tf_op jit(solution)/shard_map/ppermute | solution.py:25
  80.6 14.7 %copy-start.32 = (f32[16,125,128]{2,1,0:T(8,128)S(1)}, f32[16,125,128]{2,1,0:T(8,128)}, u32[]{:S(2)}) copy-start(f32[16,125,128]{2,1,0:T(8,128)} %get-tuple-element.357) | copy-start | bytes 3072004
  80.6 14.7 %copy-start.33 = (f32[16,128,126]{2,1,0:T(8,128)S(1)}, f32[16,128,126]{2,1,0:T(8,128)}, u32[]{:S(2)}) copy-start(f32[16,128,126]{2,1,0:T(8,128)} %get-tuple-element.362) | copy-start | bytes 3096580
  80.6 14.7 %copy-start.34 = (f32[16,128,126]{2,1,0:T(8,128)S(1)}, f32[16,128,126]{2,1,0:T(8,128)}, u32[]{:S(2)}) copy-start(f32[16,128,126]{2,1,0:T(8,128)} %get-tuple-element.363) | copy-start | bytes 3096580
  80.6 14.6 %copy-start.35 = (f32[16,126,128]{2,1,0:T(8,128)S(1)}, f32[16,126,128]{2,1,0:T(8,128)}, u32[]{:S(2)}) copy-start(f32[16,126,128]{2,1,0:T(8,128)} %get-tuple-element.354) | copy-start | bytes 3096580
  80.6 14.6 %copy-start.36 = (f32[16,126,128]{2,1,0:T(8,128)S(1)}, f32[16,126,128]{2,1,0:T(8,128)}, u32[]{:S(2)}) copy-start(f32[16,126,128]{2,1,0:T(8,128)} %get-tuple-element.355) | copy-start | bytes 3096580
  80.6 14.6 %copy-start.37 = (f32[16,124,128]{2,1,0:T(8,128)S(1)}, f32[16,124,128]{2,1,0:T(8,128)}, u32[]{:S(2)}) copy-start(f32[16,124,128]{2,1,0:T(8,128)} %get-tuple-element.358) | copy-start | bytes 3047428
  80.6 14.6 %copy-start.38 = (f32[16,124,128]{2,1,0:T(8,128)S(1)}, f32[16,124,128]{2,1,0:T(8,128)}, u32[]{:S(2)}) copy-start(f32[16,124,128]{2,1,0:T(8,128)} %get-tuple-element.359) | copy-start | bytes 3047428
  80.6 14.6 %copy-start.39 = (f32[16,127,128]{2,1,0:T(8,128)S(1)}, f32[16,127,128]{2,1,0:T(8,128)}, u32[]{:S(2)}) copy-start(f32[16,127,128]{2,1,0:T(8,128)} %get-tuple-element.352) | copy-start | bytes 3121156
  80.7 14.6 %copy-start.40 = (f32[16,127,128]{2,1,0:T(8,128)S(1)}, f32[16,127,128]{2,1,0:T(8,128)}, u32[]{:S(2)}) copy-start(f32[16,127,128]{2,1,0:T(8,128)} %get-tuple-element.353) | copy-start | bytes 3121156
  104.7 9.2 %collective-permute-start.7 = (f32[4,128,128]{2,1,0:T(8,128)S(1)}, f32[4,128,128]{2,1,0:T(8,128)S(1)}, u32[]{:S(2)}, u32[]{:S(2)}) collective-permute-start(f32[4,128,128]{2,1,0:T(8,128)S(1)} %bitcast.291), channel_id=1, source_target_pairs={{0,1},{1,2},{2,3},{3,4},{4,5},{5,6},{6,7},{7,8},{8,9},{9,10},{10,1... | collective-permute-start | bytes 786440 | tf_op jit(solution)/shard_map/ppermute | solution.py:23
  108.6 15.3 %copy-start.14 = (f32[16,128,128]{2,1,0:T(8,128)S(1)}, f32[16,128,128]{2,1,0:T(8,128)}, u32[]{:S(2)}) copy-start(f32[16,128,128]{2,1,0:T(8,128)} %param.25) | copy-start | bytes 3145732
  108.6 15.3 %collective-permute-start.6 = (f32[4,128,128]{2,1,0:T(8,128)S(1)}, f32[4,128,128]{2,1,0:T(8,128)S(1)}, u32[]{:S(2)}, u32[]{:S(2)}) collective-permute-start(f32[4,128,128]{2,1,0:T(8,128)S(1)} %bitcast.278), channel_id=1, source_target_pairs={{1,0},{2,1},{3,2},{4,3},{5,4},{6,5},{7,6},{8,7},{9,8},{10,9},{11,1... | collective-permute-start | bytes 786440 | tf_op jit(solution)/shard_map/ppermute | solution.py:25
  135.2 9.0 %collective-permute-start.9 = (f32[4,128,128]{2,1,0:T(8,128)S(1)}, f32[4,128,128]{2,1,0:T(8,128)S(1)}, u32[]{:S(2)}, u32[]{:S(2)}) collective-permute-start(f32[4,128,128]{2,1,0:T(8,128)S(1)} %bitcast.292), channel_id=1, source_target_pairs={{0,1},{1,2},{2,3},{3,4},{4,5},{5,6},{6,7},{7,8},{8,9},{9,10},{10,1... | collective-permute-start | bytes 786440 | tf_op jit(solution)/shard_map/ppermute | solution.py:23
  138.9 15.1 %copy-start.7 = (f32[262144]{0:T(1024)S(1)}, f32[262144]{0:T(1024)}, u32[]{:S(2)}) copy-start(f32[262144]{0:T(1024)} %copy-done.6) | copy-start | bytes 3145732
  138.9 15.1 %copy-start.15 = (f32[16,128,128]{2,1,0:T(8,128)S(1)}, f32[16,128,128]{2,1,0:T(8,128)}, u32[]{:S(2)}) copy-start(f32[16,128,128]{2,1,0:T(8,128)} %param.25) | copy-start | bytes 3145732
  138.9 15.1 %collective-permute-start.8 = (f32[4,128,128]{2,1,0:T(8,128)S(1)}, f32[4,128,128]{2,1,0:T(8,128)S(1)}, u32[]{:S(2)}, u32[]{:S(2)}) collective-permute-start(f32[4,128,128]{2,1,0:T(8,128)S(1)} %bitcast.279), channel_id=1, source_target_pairs={{1,0},{2,1},{3,2},{4,3},{5,4},{6,5},{7,6},{8,7},{9,8},{10,9},{11,1... | collective-permute-start | bytes 786440 | tf_op jit(solution)/shard_map/ppermute | solution.py:25
  163.3 8.0 %collective-permute-start.11 = (f32[4,128,128]{2,1,0:T(8,128)S(1)}, f32[4,128,128]{2,1,0:T(8,128)S(1)}, u32[]{:S(2)}, u32[]{:S(2)}) collective-permute-start(f32[4,128,128]{2,1,0:T(8,128)S(1)} %bitcast.293), channel_id=1, source_target_pairs={{0,1},{1,2},{2,3},{3,4},{4,5},{5,6},{6,7},{7,8},{8,9},{9,10},{10,1... | collective-permute-start | bytes 786440 | tf_op jit(solution)/shard_map/ppermute | solution.py:23
  165.7 15.5 %copy-start.16 = (f32[16,128,128]{2,1,0:T(8,128)S(1)}, f32[16,128,128]{2,1,0:T(8,128)}, u32[]{:S(2)}) copy-start(f32[16,128,128]{2,1,0:T(8,128)} %param.25) | copy-start | bytes 3145732
  165.7 15.5 %collective-permute-start.10 = (f32[4,128,128]{2,1,0:T(8,128)S(1)}, f32[4,128,128]{2,1,0:T(8,128)S(1)}, u32[]{:S(2)}, u32[]{:S(2)}) collective-permute-start(f32[4,128,128]{2,1,0:T(8,128)S(1)} %bitcast.280), channel_id=1, source_target_pairs={{1,0},{2,1},{3,2},{4,3},{5,4},{6,5},{7,6},{8,7},{9,8},{10,9},{11,1... | collective-permute-start | bytes 786440 | tf_op jit(solution)/shard_map/ppermute | solution.py:25
  212.6 6.8 collective-permute-start.13
  214.6 10.8 %copy-start.17 = (f32[16,128,128]{2,1,0:T(8,128)S(1)}, f32[16,128,128]{2,1,0:T(8,128)}, u32[]{:S(2)}) copy-start(f32[16,128,128]{2,1,0:T(8,128)} %param.25) | copy-start | bytes 3145732
  214.6 10.8 %collective-permute-start.12 = (f32[4,128,128]{2,1,0:T(8,128)S(1)}, f32[4,128,128]{2,1,0:T(8,128)S(1)}, u32[]{:S(2)}, u32[]{:S(2)}) collective-permute-start(f32[4,128,128]{2,1,0:T(8,128)S(1)} %bitcast.281), channel_id=1, source_target_pairs={{1,0},{2,1},{3,2},{4,3},{5,4},{6,5},{7,6},{8,7},{9,8},{10,9},{11,1... | collective-permute-start | bytes 786440 | tf_op jit(solution)/shard_map/ppermute | solution.py:25
  237.1 7.2 %collective-permute-start.15 = (f32[4,128,128]{2,1,0:T(8,128)S(1)}, f32[4,128,128]{2,1,0:T(8,128)S(1)}, u32[]{:S(2)}, u32[]{:S(2)}) collective-permute-start(f32[4,128,128]{2,1,0:T(8,128)S(1)} %bitcast.295), channel_id=1, source_target_pairs={{0,1},{1,2},{2,3},{3,4},{4,5},{5,6},{6,7},{7,8},{8,9},{9,10},{10,1... | collective-permute-start | bytes 786440 | tf_op jit(solution)/shard_map/ppermute | solution.py:23
  239.6 10.7 %copy-start.18 = (f32[16,128,128]{2,1,0:T(8,128)S(1)}, f32[16,128,128]{2,1,0:T(8,128)}, u32[]{:S(2)}) copy-start(f32[16,128,128]{2,1,0:T(8,128)} %param.25) | copy-start | bytes 3145732
  239.6 10.7 %collective-permute-start.14 = (f32[4,128,128]{2,1,0:T(8,128)S(1)}, f32[4,128,128]{2,1,0:T(8,128)S(1)}, u32[]{:S(2)}, u32[]{:S(2)}) collective-permute-start(f32[4,128,128]{2,1,0:T(8,128)S(1)} %bitcast.282), channel_id=1, source_target_pairs={{1,0},{2,1},{3,2},{4,3},{5,4},{6,5},{7,6},{8,7},{9,8},{10,9},{11,1... | collective-permute-start | bytes 786440 | tf_op jit(solution)/shard_map/ppermute | solution.py:25
  259.7 6.9 collective-permute-start.17
  262.0 11.0 %copy-start.19 = (f32[16,128,128]{2,1,0:T(8,128)S(1)}, f32[16,128,128]{2,1,0:T(8,128)}, u32[]{:S(2)}) copy-start(f32[16,128,128]{2,1,0:T(8,128)} %param.25) | copy-start | bytes 3145732
  262.1 11.0 %collective-permute-start.16 = (f32[4,128,128]{2,1,0:T(8,128)S(1)}, f32[4,128,128]{2,1,0:T(8,128)S(1)}, u32[]{:S(2)}, u32[]{:S(2)}) collective-permute-start(f32[4,128,128]{2,1,0:T(8,128)S(1)} %bitcast.283), channel_id=1, source_target_pairs={{1,0},{2,1},{3,2},{4,3},{5,4},{6,5},{7,6},{8,7},{9,8},{10,9},{11,1... | collective-permute-start | bytes 786440 | tf_op jit(solution)/shard_map/ppermute | solution.py:25
  294.9 6.4 collective-permute-start.19
  297.0 9.6 %copy-start.12 = (f32[1,16,128,128]{3,2,1,0:T(8,128)S(1)}, f32[1,16,128,128]{3,2,1,0:T(8,128)}, u32[]{:S(2)}) copy-start(f32[1,16,128,128]{3,2,1,0:T(8,128)} %param.29) | copy-start | bytes 3145732
  297.1 9.6 %copy-start.20 = (f32[16,128,128]{2,1,0:T(8,128)S(1)}, f32[16,128,128]{2,1,0:T(8,128)}, u32[]{:S(2)}) copy-start(f32[16,128,128]{2,1,0:T(8,128)} %param.25) | copy-start | bytes 3145732
  297.1 9.6 %collective-permute-start.18 = (f32[4,128,128]{2,1,0:T(8,128)S(1)}, f32[4,128,128]{2,1,0:T(8,128)S(1)}, u32[]{:S(2)}, u32[]{:S(2)}) collective-permute-start(f32[4,128,128]{2,1,0:T(8,128)S(1)} %bitcast.284), channel_id=1, source_target_pairs={{1,0},{2,1},{3,2},{4,3},{5,4},{6,5},{7,6},{8,7},{9,8},{10,9},{11,1... | collective-permute-start | bytes 786440 | tf_op jit(solution)/shard_map/ppermute | solution.py:25
  314.8 6.9 collective-permute-start.21
  317.1 10.2 %copy-start.21 = (f32[16,128,128]{2,1,0:T(8,128)S(1)}, f32[16,128,128]{2,1,0:T(8,128)}, u32[]{:S(2)}) copy-start(f32[16,128,128]{2,1,0:T(8,128)} %param.25) | copy-start | bytes 3145732
  317.1 10.2 %collective-permute-start.20 = (f32[4,128,128]{2,1,0:T(8,128)S(1)}, f32[4,128,128]{2,1,0:T(8,128)S(1)}, u32[]{:S(2)}, u32[]{:S(2)}) collective-permute-start(f32[4,128,128]{2,1,0:T(8,128)S(1)} %bitcast.285), channel_id=1, source_target_pairs={{1,0},{2,1},{3,2},{4,3},{5,4},{6,5},{7,6},{8,7},{9,8},{10,9},{11,1... | collective-permute-start | bytes 786440 | tf_op jit(solution)/shard_map/ppermute | solution.py:25
  335.4 7.0 collective-permute-start.23
  337.8 10.5 %copy-start.22 = (f32[16,128,128]{2,1,0:T(8,128)S(1)}, f32[16,128,128]{2,1,0:T(8,128)}, u32[]{:S(2)}) copy-start(f32[16,128,128]{2,1,0:T(8,128)} %param.25) | copy-start | bytes 3145732
  337.8 10.5 %collective-permute-start.22 = (f32[4,128,128]{2,1,0:T(8,128)S(1)}, f32[4,128,128]{2,1,0:T(8,128)S(1)}, u32[]{:S(2)}, u32[]{:S(2)}) collective-permute-start(f32[4,128,128]{2,1,0:T(8,128)S(1)} %bitcast.286), channel_id=1, source_target_pairs={{1,0},{2,1},{3,2},{4,3},{5,4},{6,5},{7,6},{8,7},{9,8},{10,9},{11,1... | collective-permute-start | bytes 786440 | tf_op jit(solution)/shard_map/ppermute | solution.py:25
  360.3 7.1 %collective-permute-start.25 = (f32[4,128,128]{2,1,0:T(8,128)S(1)}, f32[4,128,128]{2,1,0:T(8,128)S(1)}, u32[]{:S(2)}, u32[]{:S(2)}) collective-permute-start(f32[4,128,128]{2,1,0:T(8,128)S(1)} %bitcast.300), channel_id=1, source_target_pairs={{0,1},{1,2},{2,3},{3,4},{4,5},{5,6},{6,7},{7,8},{8,9},{9,10},{10,1... | collective-permute-start | bytes 786440 | tf_op jit(solution)/shard_map/ppermute | solution.py:23
  362.6 10.7 %copy-start.23 = (f32[16,128,128]{2,1,0:T(8,128)S(1)}, f32[16,128,128]{2,1,0:T(8,128)}, u32[]{:S(2)}) copy-start(f32[16,128,128]{2,1,0:T(8,128)} %param.25) | copy-start | bytes 3145732
  362.6 10.7 %collective-permute-start.24 = (f32[4,128,128]{2,1,0:T(8,128)S(1)}, f32[4,128,128]{2,1,0:T(8,128)}, u32[]{:S(2)}, u32[]{:S(2)}) collective-permute-start(f32[4,128,128]{2,1,0:T(8,128)S(1)} %bitcast.287), channel_id=1, source_target_pairs={{1,0},{2,1},{3,2},{4,3},{5,4},{6,5},{7,6},{8,7},{9,8},{10,9},{11,1... | collective-permute-start | bytes 786440 | tf_op jit(solution)/shard_map/ppermute | solution.py:25
  386.6 7.1 %collective-permute-start.27 = (f32[4,128,128]{2,1,0:T(8,128)S(1)}, f32[4,128,128]{2,1,0:T(8,128)S(1)}, u32[]{:S(2)}, u32[]{:S(2)}) collective-permute-start(f32[4,128,128]{2,1,0:T(8,128)S(1)} %bitcast.301), channel_id=1, source_target_pairs={{0,1},{1,2},{2,3},{3,4},{4,5},{5,6},{6,7},{7,8},{8,9},{9,10},{10,1... | collective-permute-start | bytes 786440 | tf_op jit(solution)/shard_map/ppermute | solution.py:23
  388.9 10.7 %copy-start.1 = (f32[262144]{0:T(1024)S(1)}, f32[262144]{0:T(1024)}, u32[]{:S(2)}) copy-start(f32[262144]{0:T(1024)} %scatter_fusion.3) | copy-start | bytes 3145732
  388.9 10.7 %copy-start.24 = (f32[16,128,128]{2,1,0:T(8,128)S(1)}, f32[16,128,128]{2,1,0:T(8,128)}, u32[]{:S(2)}) copy-start(f32[16,128,128]{2,1,0:T(8,128)} %param.25) | copy-start | bytes 3145732
  388.9 10.7 %collective-permute-start.26 = (f32[4,128,128]{2,1,0:T(8,128)S(1)}, f32[4,128,128]{2,1,0:T(8,128)}, u32[]{:S(2)}, u32[]{:S(2)}) collective-permute-start(f32[4,128,128]{2,1,0:T(8,128)S(1)} %bitcast.288), channel_id=1, source_target_pairs={{1,0},{2,1},{3,2},{4,3},{5,4},{6,5},{7,6},{8,7},{9,8},{10,9},{11,1... | collective-permute-start | bytes 786440 | tf_op jit(solution)/shard_map/ppermute | solution.py:25
  413.1 7.1 %collective-permute-start.29 = (f32[4,128,128]{2,1,0:T(8,128)S(1)}, f32[4,128,128]{2,1,0:T(8,128)S(1)}, u32[]{:S(2)}, u32[]{:S(2)}) collective-permute-start(f32[4,128,128]{2,1,0:T(8,128)S(1)} %bitcast.302), channel_id=1, source_target_pairs={{0,1},{1,2},{2,3},{3,4},{4,5},{5,6},{6,7},{7,8},{8,9},{9,10},{10,1... | collective-permute-start | bytes 786440 | tf_op jit(solution)/shard_map/ppermute | solution.py:23
  415.4 10.6 %copy-start.3 = (f32[262144]{0:T(1024)S(1)}, f32[262144]{0:T(1024)}, u32[]{:S(2)}) copy-start(f32[262144]{0:T(1024)} %scatter_fusion.4) | copy-start | bytes 3145732
  415.4 10.6 %copy-start.25 = (f32[16,128,128]{2,1,0:T(8,128)S(1)}, f32[16,128,128]{2,1,0:T(8,128)}, u32[]{:S(2)}) copy-start(f32[16,128,128]{2,1,0:T(8,128)} %param.25) | copy-start | bytes 3145732
  415.4 10.6 %collective-permute-start.28 = (f32[4,128,128]{2,1,0:T(8,128)S(1)}, f32[4,128,128]{2,1,0:T(8,128)}, u32[]{:S(2)}, u32[]{:S(2)}) collective-permute-start(f32[4,128,128]{2,1,0:T(8,128)S(1)} %bitcast.289), channel_id=1, source_target_pairs={{1,0},{2,1},{3,2},{4,3},{5,4},{6,5},{7,6},{8,7},{9,8},{10,9},{11,1... | collective-permute-start | bytes 786440 | tf_op jit(solution)/shard_map/ppermute | solution.py:25
  439.4 7.2 %collective-permute-start.31 = (f32[4,128,128]{2,1,0:T(8,128)S(1)}, f32[4,128,128]{2,1,0:T(8,128)S(1)}, u32[]{:S(2)}, u32[]{:S(2)}) collective-permute-start(f32[4,128,128]{2,1,0:T(8,128)S(1)} %bitcast.303), channel_id=1, source_target_pairs={{0,1},{1,2},{2,3},{3,4},{4,5},{5,6},{6,7},{7,8},{8,9},{9,10},{10,1... | collective-permute-start | bytes 786440 | tf_op jit(solution)/shard_map/ppermute | solution.py:23
  441.8 10.9 %copy-start.5 = (f32[262144]{0:T(1024)S(1)}, f32[262144]{0:T(1024)}, u32[]{:S(2)}) copy-start(f32[262144]{0:T(1024)} %scatter_fusion.5) | copy-start | bytes 3145732
  441.8 10.9 %copy-start.26 = (f32[16,128,128]{2,1,0:T(8,128)S(1)}, f32[16,128,128]{2,1,0:T(8,128)}, u32[]{:S(2)}) copy-start(f32[16,128,128]{2,1,0:T(8,128)} %param.25) | copy-start | bytes 3145732
  441.8 10.9 %collective-permute-start.30 = (f32[4,128,128]{2,1,0:T(8,128)S(1)}, f32[4,128,128]{2,1,0:T(8,128)}, u32[]{:S(2)}, u32[]{:S(2)}) collective-permute-start(f32[4,128,128]{2,1,0:T(8,128)S(1)} %bitcast.290), channel_id=1, source_target_pairs={{1,0},{2,1},{3,2},{4,3},{5,4},{6,5},{7,6},{8,7},{9,8},{10,9},{11,1... | collective-permute-start | bytes 786440 | tf_op jit(solution)/shard_map/ppermute | solution.py:25
  470.7 225.5 %copy-start.27 = (f32[16,128,128]{2,1,0:T(8,128)S(1)}, f32[16,128,128]{2,1,0:T(8,128)}, u32[]{:S(2)}) copy-start(f32[16,128,128]{2,1,0:T(8,128)} %param.25) | copy-start | bytes 3145732
  650.1 46.2 %copy-start.28 = (f32[16,128,128]{2,1,0:T(8,128)S(1)}, f32[16,128,128]{2,1,0:T(8,128)}, u32[]{:S(2)}) copy-start(f32[16,128,128]{2,1,0:T(8,128)} %all-reduce.258.cloned.1.call-done) | copy-start | bytes 3145732
  (18 other events, 73.9 us)
Sparse Core Ops, SparseCore 0:
  470.8 179.1 all-reduce.257
where the time goes:
time: 714 us; the launch traced here: 705 us
  waiting for transfers between devices  301 us (42%)
  other arithmetic  139 us (19%)
  local copies, waits for them, and re-layouts  130 us (18%)
  starting transfers between devices  68.9 us (10%)
  blocking collectives  43.5 us (6%)
  between operations  22.2 us (3%)
    psum x1, waiting for transfers between devices, on_device(): total = lax.psum(gradient, 'shot')  179 us
    ppermute x16, waiting for transfers between devices, padded_2(): lax.ppermute(head, axis, [((i + 1) % count, i) for i in range(ends)])  94.2 us
    slice x128, local copies, waits for them, and re-layouts, shifted(): lax.slice_in_dim(field, offset, length, axis=axis)  88.1 us
    add x8, other arithmetic, on_device(): newer = 2.0 * current - older + model_slab * image  51.9 us
    ppermute x16, starting transfers between devices, padded_2(): lax.ppermute(tail, axis, [(i, (i + 1) % count) for i in range(ends)])  44.5 us
    pmax x1, blocking collectives, on_device(): peak = lax.pmax(jnp.max(jnp.abs(total)), 'dom')  43.5 us
    add x8, other arithmetic, on_device(): earlier = 2.0 * present - later + model_slab * laplace(padded)  41.5 us
    scatter-add x16, other arithmetic, add_at(): return field.reshape(-1).at[slots].add(values).reshape(field.shape)  34.3 us
  transfers between devices with their start and end apart: 33, of which 28 were waited for; matrix products, arithmetic and copies ran while one was open for 10% of the time, Pallas kernels for 0%

commit v1 on v0

v1 whole, which is shorter than its diff:
```python
import functools
import jax
import jax.numpy as jnp
from jax import lax
from jax.experimental import pallas as pl
from jax.experimental.pallas import tpu as pltpu
from jax.sharding import PartitionSpec as P

STEPS = 8
COEFFS = (8.0 / 5.0, -1.0 / 5.0, 8.0 / 315.0, -1.0 / 560.0)
CENTRE = -205.0 / 72.0
STEP_FRACTION = 0.1
EPSILON = 1e-06
ROWS = 16
NY = 128
NZ = 128
REC = 256
EDGE = 4
MID = ROWS - 2 * EDGE
CHUNK = 32
VMEM = pl.BlockSpec(memory_space=pltpu.VMEM)
SMEM = pl.BlockSpec(memory_space=pltpu.SMEM)
LIMIT = 24 * 1024 * 1024


def planes(count):
    return jax.ShapeDtypeStruct((count, NY, NZ), jnp.float32)


def call(kernel, outs, scratch, specs, out_specs, flops, nbytes, name, aliases={}):
    return pl.pallas_call(
        kernel,
        out_shape=outs,
        in_specs=specs,
        out_specs=out_specs,
        scratch_shapes=scratch,
        input_output_aliases=aliases,
        compiler_params=pltpu.CompilerParams(vmem_limit_bytes=LIMIT),
        cost_estimate=pl.CostEstimate(flops=flops, transcendentals=0, bytes_accessed=nbytes),
        name=name,
    )


def sort_kernel(first_ref, receivers_ref, lists_ref):
    for region in range(3):
        lists_ref[region, REC] = 0

    def body(j, carry):
        plane = (receivers_ref[0, j] - first_ref[0]) >> 14
        inside = (plane >= 0) & (plane < ROWS)
        region = jnp.where(plane < EDGE, 0, jnp.where(plane < ROWS - EDGE, 1, 2))

        @pl.when(inside)
        def _():
            count = lists_ref[region, REC]
            lists_ref[region, count] = j
            lists_ref[region, REC] = count + 1

        return carry

    lax.fori_loop(0, REC, body, 0)


def where_of(cell, first):
    local = cell - first
    return local >> 14, (local >> 7) & 127, local & 127


def lanes_row():
    return lax.broadcasted_iota(jnp.int32, (1, NZ), 1)


def add_source(first_ref, source_ref, wavelet_ref, tick, ref, low, count):
    plane, row, lane = where_of(source_ref[0], first_ref[0])
    plane = plane - low

    @pl.when((plane >= 0) & (plane < count))
    def _():
        extra = jnp.where(lanes_row() == lane, wavelet_ref[0, tick], 0.0)
        spot = ref[plane, pl.ds(row, 1), :]
        ref[plane, pl.ds(row, 1), :] = spot + extra


def add_residuals(first_ref, receivers_ref, lists_ref, res_ref, ref, region, low):
    def body(i, carry):
        j = lists_ref[region, i]
        plane, row, lane = where_of(receivers_ref[0, j], first_ref[0])
        spot = ref[plane - low, pl.ds(row, 1), :]
        ref[plane - low, pl.ds(row, 1), :] = spot + res_ref[pl.ds(j, 1), :]
        return carry

    lax.fori_loop(0, lists_ref[region, REC], body, 0)


def take_residuals(first_ref, receivers_ref, lists_ref, observed_ref, tick, refs, res_ref):
    lows = (0, EDGE, ROWS - EDGE)
    for region in range(3):
        ref, low = refs[region], lows[region]

        def body(i, carry):
            j = lists_ref[region, i]
            plane, row, lane = where_of(receivers_ref[0, j], first_ref[0])
            spot = ref[plane - low, pl.ds(row, 1), :]
            value = spot - observed_ref[tick, j]
            res_ref[pl.ds(j, 1), :] = jnp.where(lanes_row() == lane, value, 0.0)
            return carry

        lax.fori_loop(0, lists_ref[region, REC], body, 0)


def fill_padded(pad_ref, lo_ref, mid_ref, hi_ref):
    zeros = jnp.zeros((8, NZ), jnp.float32)
    for i in range(EDGE):
        pad_ref[i] = jnp.zeros((NY + 16, NZ), jnp.float32)
        pad_ref[ROWS + EDGE + i] = jnp.zeros((NY + 16, NZ), jnp.float32)
    start = EDGE
    for ref, count in ((lo_ref, EDGE), (mid_ref, MID), (hi_ref, EDGE)):

        def body(i, carry, ref=ref, start=start):
            pad_ref[start + i, pl.ds(0, 8), :] = zeros
            pad_ref[start + i, pl.ds(NY + 8, 8), :] = zeros
            pad_ref[start + i, pl.ds(8, NY), :] = ref[i]
            return carry

        lax.fori_loop(0, count, body, 0)
        start += count


def laplace_rows(pad_ref, plane, row, lane_weights):
    at = plane + EDGE
    field = pad_ref[at, pl.ds(8 + row, CHUNK), :]
    total = (3.0 * CENTRE) * field
    for index, weight in enumerate(COEFFS):
        k = index + 1
        pair = pad_ref[at + k, pl.ds(8 + row, CHUNK), :] + pad_ref[at - k, pl.ds(8 + row, CHUNK), :]
        pair = pair + (pad_ref[at, pl.ds(8 + row + k, CHUNK), :] + pad_ref[at, pl.ds(8 + row - k, CHUNK), :])
        total = total + weight * pair
        total = total + lane_weights[2 * index] * pltpu.roll(field, NZ - k, 1)
        total = total + lane_weights[2 * index + 1] * pltpu.roll(field, k, 1)
    return field, total


def make_lane_weights():
    lane = lax.broadcasted_iota(jnp.int32, (CHUNK, NZ), 1)
    out = []
    for index, weight in enumerate(COEFFS):
        k = index + 1
        out.append(jnp.where(lane < NZ - k, weight, 0.0))
        out.append(jnp.where(lane >= k, weight, 0.0))
    return out


def own_kernel(forward, tick, has_extra, *refs):
    refs = list(refs)
    take = lambda n: [refs.pop(0) for _ in range(n)]
    first_ref, receivers_ref, lists_ref = take(3)
    if forward:
        source_ref, wavelet_ref = take(2)
    observed = take(1)[0] if (forward and tick > 0) or (not forward and tick == STEPS - 1) else None
    cur = take(3)
    old = take(3)
    model = take(3)
    if not forward:
        if tick == STEPS - 1:
            last = take(3)
        else:
            res_in = take(1)[0]
        if has_extra:
            image = take(3)
            grad_in = take(1)[0]
    next_mid, base_lo, base_hi = take(3)
    if forward:
        image_out = take(3)
        res_out = take(1)[0] if tick > 0 else None
    else:
        res_out = take(1)[0] if tick == STEPS - 1 else None
        grad_out = take(1)[0] if has_extra or tick == STEPS - 1 else None
    pad_ref = take(1)[0]

    fill_padded(pad_ref, *cur)
    weights = make_lane_weights()
    outs = (base_lo, next_mid, base_hi)
    low = 0
    for region, count in enumerate((EDGE, MID, EDGE)):

        def body(i, carry, region=region, low=low):
            for row in range(0, NY, CHUNK):
                field, total = laplace_rows(pad_ref, low + i, row, weights)
                rows = pl.ds(row, CHUNK)
                value = 2.0 * field - old[region][i, rows, :] + model[region][i, rows, :] * total
                outs[region][i, rows, :] = value
                if forward:
                    image_out[region][i, rows, :] = total
                elif has_extra:
                    grad_out[low + i, rows, :] = grad_in[low + i, rows, :] + field * image[region][i, rows, :]
                elif grad_out is not None:
                    grad_out[low + i, rows, :] = jnp.zeros((CHUNK, NZ), jnp.float32)
            return carry

        lax.fori_loop(0, count, body, 0)
        low += count

    if forward:
        add_source(first_ref, source_ref, wavelet_ref, tick, next_mid, EDGE, MID)
        if tick > 0:
            take_residuals(first_ref, receivers_ref, lists_ref, observed, tick - 1, cur, res_out)
    else:
        if tick == STEPS - 1:
            take_residuals(first_ref, receivers_ref, lists_ref, observed, tick, last, res_out)
            res_in = res_out
        add_residuals(first_ref, receivers_ref, lists_ref, res_in, next_mid, 1, EDGE)


def edge_kernel(forward, tick, *refs):
    refs = list(refs)
    take = lambda n: [refs.pop(0) for _ in range(n)]
    first_ref, receivers_ref, lists_ref = take(3)
    if forward:
        source_ref, wavelet_ref = take(2)
    before, after, base_lo, base_hi, model_lo, model_hi = take(6)
    if forward:
        part_lo, part_hi = take(2)
    else:
        res_ref = take(1)[0]
    next_lo, next_hi = take(2)
    if forward:
        image_lo, image_hi = take(2)

    def body(c, carry):
        rows = pl.ds(pl.multiple_of(c * CHUNK, CHUNK), CHUNK)
        low = [before[i, rows, :] for i in range(EDGE)]
        high = [after[i, rows, :] for i in range(EDGE)]
        for j in range(EDGE):
            extra = COEFFS[3] * low[j]
            for k in range(j + 1, 4):
                extra = extra + COEFFS[k - 1] * low[EDGE + j - k]
            next_lo[j, rows, :] = base_lo[j, rows, :] + model_lo[j, rows, :] * extra
            if forward:
                image_lo[j, rows, :] = part_lo[j, rows, :] + extra
            extra = COEFFS[3] * high[j]
            for k in range(EDGE - j, 4):
                extra = extra + COEFFS[k - 1] * high[j + k - EDGE]
            next_hi[j, rows, :] = base_hi[j, rows, :] + model_hi[j, rows, :] * extra
            if forward:
                image_hi[j, rows, :] = part_hi[j, rows, :] + extra
        return carry

    lax.fori_loop(0, NY // CHUNK, body, 0)
    if forward:
        add_source(first_ref, source_ref, wavelet_ref, tick, next_lo, 0, EDGE)
        add_source(first_ref, source_ref, wavelet_ref, tick, next_hi, ROWS - EDGE, EDGE)
    else:
        add_residuals(first_ref, receivers_ref, lists_ref, res_ref, next_lo, 0, 0)
        add_residuals(first_ref, receivers_ref, lists_ref, res_ref, next_hi, 2, ROWS - EDGE)


def swap(value, axis, pairs):
    return lax.ppermute(value, axis, pairs)


def shot_sum(grad):
    shot = lax.axis_index("shot")
    core = shot % 2
    y = (shot // 2) % 4
    other_core = [(k, k ^ 1) for k in range(16)]
    other_z = [(k, k ^ 8) for k in range(16)]

    def turn(r):
        return [(k, (k // 8) * 8 + ((k // 2 + r) % 4) * 2 + k % 2) for k in range(16)]

    keep = lax.dynamic_slice_in_dim(grad, core * 8, 8, 0)
    send = lax.dynamic_slice_in_dim(grad, (1 - core) * 8, 8, 0)
    half = keep + swap(send, "shot", other_core)
    parts = [lax.dynamic_slice_in_dim(half, ((y + r) % 4) * 2, 2, 0) for r in range(4)]
    got = [swap(parts[r], "shot", turn(r)) for r in (1, 2, 3)]
    part = parts[0] + got[0] + got[1] + got[2]
    part = part + swap(part, "shot", other_z)
    got = [part] + [swap(part, "shot", turn(r)) for r in (1, 2, 3)]
    half = jnp.zeros((8, NY, NZ), jnp.float32)
    for r in range(4):
        half = lax.dynamic_update_slice_in_dim(half, got[r], ((y - r) % 4) * 2, 0)
    other = swap(half, "shot", other_core)
    first = jnp.where(core == 0, half, other)
    second = jnp.where(core == 0, other, half)
    return jnp.concatenate([first, second])


def dom_max(value):
    value = jnp.broadcast_to(value, (8, 128))

    def along_x(r):
        return [(k, ((k // 4 + r) % 4) * 4 + k % 4) for k in range(16)]

    def along_z(r):
        return [(k, (k // 4) * 4 + (k + r) % 4) for k in range(16)]

    for turn in (along_x, along_z):
        got = [swap(value, "dom", turn(r)) for r in (1, 2, 3)]
        value = jnp.maximum(jnp.maximum(value, got[0]), jnp.maximum(got[1], got[2]))
    return value[0, 0]


def on_device(model_slab, wave_prev, wave_now, adjoint_next, adjoint_now, wavelet, source_cell, receiver_cells, observed):
    cut = lambda a: (a[:EDGE], a[EDGE : ROWS - EDGE], a[ROWS - EDGE :])
    up = [(i, i + 1) for i in range(15)]
    down = [(i + 1, i) for i in range(15)]
    first = (lax.axis_index("dom") * (ROWS * NY * NZ)).astype(jnp.int32).reshape(1)
    lists = call(
        sort_kernel,
        jax.ShapeDtypeStruct((3, REC + 128), jnp.int32),
        [],
        [SMEM, SMEM],
        SMEM,
        1000,
        4096,
        "sort_receivers",
    )(first, receiver_cells)
    observed = observed[0]
    where = (first, receiver_cells, lists)
    model = cut(model_slab)
    pad = [pltpu.VMEM((ROWS + 2 * EDGE, NY + 16, NZ), jnp.float32)]
    res_shape = jax.ShapeDtypeStruct((REC, NZ), jnp.float32)
    own_cost = dict(flops=ROWS * NY * NZ * 60, nbytes=8 * ROWS * NY * NZ * 4)
    edge_cost = dict(flops=2 * EDGE * NY * NZ * 10, nbytes=6 * EDGE * NY * NZ * 4)

    def halos(cur):
        return swap(cur[2], "dom", up), swap(cur[0], "dom", down)

    old, cur = cut(wave_prev[0]), cut(wave_now[0])
    images, residuals = [], []
    for tick in range(STEPS):
        before, after = halos(cur)
        extra = (observed,) if tick > 0 else ()
        outs = [planes(MID), planes(EDGE), planes(EDGE), planes(EDGE), planes(MID), planes(EDGE)]
        outs += [res_shape] if tick > 0 else []
        result = call(
            functools.partial(own_kernel, True, tick, False),
            outs,
            pad,
            [SMEM] * (5 + len(extra)) + [VMEM] * 9,
            [VMEM] * len(outs),
            name="own_forward",
            **own_cost,
        )(*where, source_cell, wavelet, *extra, *cur, *old, *model)
        mid, base_lo, base_hi, part_lo, image_mid, part_hi = result[:6]
        if tick > 0:
            residuals.append(result[6])
        low, high, image_lo, image_hi = call(
            functools.partial(edge_kernel, True, tick),
            [planes(EDGE)] * 4,
            [],
            [SMEM] * 5 + [VMEM] * 8,
            [VMEM] * 4,
            name="edge_forward",
            **edge_cost,
        )(*where, source_cell, wavelet, before, after, base_lo, base_hi, model[0], model[2], part_lo, part_hi)
        images.append((image_lo, image_mid, image_hi))
        old, cur = cur, (low, mid, high)
    last = cur
    old, cur = cut(adjoint_next[0]), cut(adjoint_now[0])
    grad = None
    for tick in reversed(range(STEPS)):
        before, after = halos(cur)
        top = tick == STEPS - 1
        extra = (observed,) if top else ()
        fields = last if top else (residuals[tick], *images[tick + 1], grad)
        outs = [planes(MID), planes(EDGE), planes(EDGE)]
        outs += [res_shape] if top else []
        outs += [planes(ROWS)]
        result = call(
            functools.partial(own_kernel, False, tick, not top),
            outs,
            pad,
            [SMEM] * (3 + len(extra)) + [VMEM] * (9 + len(fields)),
            [VMEM] * len(outs),
            name="own_adjoint",
            **own_cost,
        )(*where, *extra, *cur, *old, *model, *fields)
        mid, base_lo, base_hi = result[:3]
        if top:
            residuals.append(result[3])
        grad = result[-1]
        low, high = call(
            functools.partial(edge_kernel, False, tick),
            [planes(EDGE)] * 2,
            [],
            [SMEM] * 3 + [VMEM] * 7,
            [VMEM] * 2,
            name="edge_adjoint",
            **edge_cost,
        )(*where, before, after, base_lo, base_hi, model[0], model[2], residuals[tick])
        old, cur = cur, (low, mid, high)
    grad = grad + jnp.concatenate([a * b for a, b in zip(cur, images[0])])
    total = shot_sum(grad)
    peak = dom_max(jnp.max(jnp.abs(total)))
    direction = total / (peak + EPSILON)
    new_model = model_slab * (1.0 - STEP_FRACTION * direction)
    return direction, new_model


def solution(mesh):
    placed = (
        P("dom", None, None),
        P("shot", "dom", None, None),
        P("shot", "dom", None, None),
        P("shot", "dom", None, None),
        P("shot", "dom", None, None),
        P("shot", None),
        P("shot"),
        P("shot", None),
        P("shot", None, None),
    )
    return jax.shard_map(
        on_device,
        mesh=mesh,
        in_specs=placed,
        out_specs=(P("dom", None, None), P("dom", None, None)),
        check_vma=False,
    )
```

time: 714 us -> 314 us (0.44)
  waiting for transfers between devices: 301 us -> 105 us
  other arithmetic: 139 us -> 3.3 us
  local copies, waits for them, and re-layouts: 130 us -> 10.1 us
  Pallas kernels: 0 us -> 94 us
  blocking collectives: 43.5 us -> 0 us
  starting transfers between devices: 68.9 us -> 94.5 us
  between operations: 22.2 us -> 3.1 us
    psum x1 -> x0, waiting for transfers between devices: 179 us -> none  [on_device(): total = lax.psum(gradient, 'shot')]
    add x17 -> x3, other arithmetic: 101 us -> 0.2 us  [the longest x1 0.11 us: on_device(): grad = grad + jnp.concatenate([a * b for a, b in zip(cur, images[0])])]
    slice x146 -> x9, local copies, waits for them, and re-layouts: 97.6 us -> 3.22 us  [the longest x8 2.71 us: on_device(): cut = lambda a: (a[:EDGE], a[EDGE:ROWS - EDGE], a[ROWS - EDGE:])]
    pallas_call x0 -> x33, Pallas kernels: none -> 94 us  [the longest x8 36.3 us: on_device(): call(functools.partial(own_kernel, True, tick, False), outs, pad, [SMEM]...]
    pmax x1 -> x0, blocking collectives: 43.5 us -> none  [on_device(): peak = lax.pmax(jnp.max(jnp.abs(total)), 'dom')]
    scatter-add x16 -> x0, other arithmetic: 34.3 us -> none  [add_at(): return field.reshape(-1).at[slots].add(values).reshape(field.shape)]
    gather x8 -> x0, local copies, waits for them, and re-layouts: 30.6 us -> none  [on_device(): values = newer.reshape(-1)[receiver_slots] - observed[0, tick]]
    ppermute x32 -> x47, starting transfers between devices: 68.9 us -> 94.5 us  [swap(): return lax.ppermute(value, axis, pairs)]
  transfers between devices with their start and end apart: 33 -> 47, of which waited for: 28 -> 25; matrix products, arithmetic and copies ran while one was open for 10% -> 0% of each run, Pallas kernels for 0% -> 26%
where the time goes in v1:
time: 314 us; the launch traced here: 310 us
  waiting for transfers between devices  105 us (33%)
  starting transfers between devices  94.5 us (30%)
  Pallas kernels  94 us (30%)
  local copies, waits for them, and re-layouts  10.1 us (3%)
  other arithmetic  3.3 us (1%)
    ppermute x47, waiting for transfers between devices, swap(): return lax.ppermute(value, axis, pairs)  105 us
    ppermute x47, starting transfers between devices, swap(): return lax.ppermute(value, axis, pairs)  94.5 us
    pallas_call x8, Pallas kernels, on_device(): call(functools.partial(own_kernel, True, tick, False), outs, pad, [SMEM]...  36.3 us
    pallas_call x8, Pallas kernels, on_device(): call(functools.partial(own_kernel, False, tick, not top), outs, pad, [SME...  35.6 us
    pallas_call x8, Pallas kernels, on_device(): call(functools.partial(edge_kernel, False, tick), [planes(EDGE)] * 2, [],...  8.46 us
    pallas_call x1, Pallas kernels, on_device(): call(sort_kernel, jax.ShapeDtypeStruct((3, REC + 128), jnp.int32), [], [S...  6.89 us
    pallas_call x8, Pallas kernels, on_device(): call(functools.partial(edge_kernel, True, tick), [planes(EDGE)] * 4, [],...  6.71 us
  transfers between devices with their start and end apart: 47, of which 25 were waited for; matrix products, arithmetic and copies ran while one was open for 0% of the time, Pallas kernels for 26%

profile of v1, /device:TPU:0, one launch (start us, length us, event | category | flops | bytes accessed | tf_op | source)
XLA Modules:
  0.0 310.4 jit_solution(4537939679580219369)
XLA Ops:
  2.0 2.3 collective-permute-start.2
  6.4 6.9 %sort_receivers.1.refs_2_ = s32[3,384]{1,0:T(4,128)S(1)} custom-call(s32[1]{0:T(128)} %bitcast.first_ref.refs_0_, s32[1,256]{1,0:T(1,128)S(1)} %copy-done), custom_call_target="tpu_custom_call" | custom-call | flops 1000 | bytes 4096 | tf_op jit(solution)/shard_map/sort_receivers/pallas_call | solution.py:308
  15.7 4.2 %own_forward.8 = (f32[8,128,128]{2,1,0:T(8,128)S(1)}, f32[4,128,128]{2,1,0:T(8,128)S(1)}, f32[4,128,128]{2,1,0:T(8,128)S(1)}, f32[4,128,128]{2,1,0:T(8,128)S(1)}...) custom-call(s32[1]{0:T(128)} %bitcast.first_ref.refs_0_, s32[1,256]{1,0:T(1,128)S(1)} %copy-done, ...), custom_call_target="tpu_custom_call" | custom-call | flops 15728640 | bytes 8388608 | tf_op jit(solution)/shard_map/own_forward/pallas_call | solution.py:336
  21.5 4.5 %collective-permute-start.4 = (f32[4,128,128]{2,1,0:T(8,128)S(1)}, f32[4,128,128]{2,1,0:T(8,128)S(1)}, u32[]{:S(2)}, u32[]{:S(2)}) collective-permute-start(f32[4,128,128]{2,1,0:T(8,128)S(1)} %get-tuple-element.142.refs_8_.refs_11_), channel_id=1, source_target_pairs={{0,1},{1,2},{2,3},{3,4},{4,5},{5,6},{6,7},{7,8},{8,9},{9,10},{10,1... | collective-permute-start | bytes 786440 | tf_op jit(solution)/shard_map/ppermute | solution.py:258
  27.4 4.6 %own_forward.9 = (f32[8,128,128]{2,1,0:T(8,128)S(1)}, f32[4,128,128]{2,1,0:T(8,128)S(1)}, f32[4,128,128]{2,1,0:T(8,128)S(1)}, f32[4,128,128]{2,1,0:T(8,128)S(1)}...) custom-call(s32[1]{0:T(128)} %bitcast.first_ref.refs_0_, s32[1,256]{1,0:T(1,128)S(1)} %copy-done, ...), custom_call_target="tpu_custom_call" | custom-call | flops 15728640 | bytes 8388608 | tf_op jit(solution)/shard_map/own_forward/pallas_call | solution.py:336
  32.0 9.1 %collective-permute-done.5.refs_6_ = f32[4,128,128]{2,1,0:T(8,128)S(1)} collective-permute-done((f32[4,128,128]{2,1,0:T(8,128)S(1)}, f32[4,128,128]{2,1,0:T(8,128)S(1)}, u32[]{:S(2)}, u32[]{:S(2)}) %collective-permute-start.5) | collective-permute-done | bytes 262176 | tf_op jit(solution)/shard_map/ppermute | solution.py:258
  42.0 3.7 %collective-permute-start.6 = (f32[4,128,128]{2,1,0:T(8,128)S(1)}, f32[4,128,128]{2,1,0:T(8,128)S(1)}, u32[]{:S(2)}, u32[]{:S(2)}) collective-permute-start(f32[4,128,128]{2,1,0:T(8,128)S(1)} %get-tuple-element.149.refs_8_.refs_11_), channel_id=1, source_target_pairs={{0,1},{1,2},{2,3},{3,4},{4,5},{5,6},{6,7},{7,8},{8,9},{9,10},{10,1... | collective-permute-start | bytes 786440 | tf_op jit(solution)/shard_map/ppermute | solution.py:258
  47.0 4.6 %own_forward.10 = (f32[8,128,128]{2,1,0:T(8,128)S(1)}, f32[4,128,128]{2,1,0:T(8,128)S(1)}, f32[4,128,128]{2,1,0:T(8,128)S(1)}, f32[4,128,128]{2,1,0:T(8,128)S(1)...) custom-call(s32[1]{0:T(128)} %bitcast.first_ref.refs_0_, s32[1,256]{1,0:T(1,128)S(1)} %copy-done, ...), custom_call_target="tpu_custom_call" | custom-call | flops 15728640 | bytes 8388608 | tf_op jit(solution)/shard_map/own_forward/pallas_call | solution.py:336
  51.6 9.0 %collective-permute-done.7.refs_6_ = f32[4,128,128]{2,1,0:T(8,128)S(1)} collective-permute-done((f32[4,128,128]{2,1,0:T(8,128)S(1)}, f32[4,128,128]{2,1,0:T(8,128)S(1)}, u32[]{:S(2)}, u32[]{:S(2)}) %collective-permute-start.7) | collective-permute-done | bytes 262176 | tf_op jit(solution)/shard_map/ppermute | solution.py:258
  61.5 2.2 collective-permute-start.8
  65.0 4.6 %own_forward.11 = (f32[8,128,128]{2,1,0:T(8,128)S(1)}, f32[4,128,128]{2,1,0:T(8,128)S(1)}, f32[4,128,128]{2,1,0:T(8,128)S(1)}, f32[4,128,128]{2,1,0:T(8,128)S(1)...) custom-call(s32[1]{0:T(128)} %bitcast.first_ref.refs_0_, s32[1,256]{1,0:T(1,128)S(1)} %copy-done, ...), custom_call_target="tpu_custom_call" | custom-call | flops 15728640 | bytes 8388608 | tf_op jit(solution)/shard_map/own_forward/pallas_call | solution.py:336
  69.6 9.3 %collective-permute-done.9.refs_6_ = f32[4,128,128]{2,1,0:T(8,128)S(1)} collective-permute-done((f32[4,128,128]{2,1,0:T(8,128)S(1)}, f32[4,128,128]{2,1,0:T(8,128)S(1)}, u32[]{:S(2)}, u32[]{:S(2)}) %collective-permute-start.9) | collective-permute-done | bytes 262176 | tf_op jit(solution)/shard_map/ppermute | solution.py:258
  79.8 2.2 collective-permute-start.10
  83.3 4.6 %own_forward.12 = (f32[8,128,128]{2,1,0:T(8,128)S(1)}, f32[4,128,128]{2,1,0:T(8,128)S(1)}, f32[4,128,128]{2,1,0:T(8,128)S(1)}, f32[4,128,128]{2,1,0:T(8,128)S(1)...) custom-call(s32[1]{0:T(128)} %bitcast.first_ref.refs_0_, s32[1,256]{1,0:T(1,128)S(1)} %copy-done, ...), custom_call_target="tpu_custom_call" | custom-call | flops 15728640 | bytes 8388608 | tf_op jit(solution)/shard_map/own_forward/pallas_call | solution.py:336
  87.9 6.8 %collective-permute-done.11.refs_6_ = f32[4,128,128]{2,1,0:T(8,128)S(1)} collective-permute-done((f32[4,128,128]{2,1,0:T(8,128)S(1)}, f32[4,128,128]{2,1,0:T(8,128)S(1)}, u32[]{:S(2)}, u32[]{:S(2)}) %collective-permute-start.11) | collective-permute-done | bytes 262176 | tf_op jit(solution)/shard_map/ppermute | solution.py:258
  95.5 2.5 collective-permute-start.12
  99.3 4.6 %own_forward.13 = (f32[8,128,128]{2,1,0:T(8,128)S(1)}, f32[4,128,128]{2,1,0:T(8,128)S(1)}, f32[4,128,128]{2,1,0:T(8,128)S(1)}, f32[4,128,128]{2,1,0:T(8,128)S(1)...) custom-call(s32[1]{0:T(128)} %bitcast.first_ref.refs_0_, s32[1,256]{1,0:T(1,128)S(1)} %copy-done, ...), custom_call_target="tpu_custom_call" | custom-call | flops 15728640 | bytes 8388608 | tf_op jit(solution)/shard_map/own_forward/pallas_call | solution.py:336
  103.9 5.2 %collective-permute-done.13.refs_6_ = f32[4,128,128]{2,1,0:T(8,128)S(1)} collective-permute-done((f32[4,128,128]{2,1,0:T(8,128)S(1)}, f32[4,128,128]{2,1,0:T(8,128)S(1)}, u32[]{:S(2)}, u32[]{:S(2)}) %collective-permute-start.13) | collective-permute-done | bytes 262176 | tf_op jit(solution)/shard_map/ppermute | solution.py:258
  110.0 2.3 collective-permute-start.14
  113.8 4.6 %collective-permute-start = (f32[4,128,128]{2,1,0:T(8,128)S(1)}, f32[4,128,128]{2,1,0:T(8,128)S(1)}, u32[]{:S(2)}, u32[]{:S(2)}) collective-permute-start(f32[4,128,128]{2,1,0:T(8,128)S(1)} %get-tuple-element.295.refs_6_.refs_8_), channel_id=1, source_target_pairs={{0,1},{1,2},{2,3},{3,4},{4,5},{5,6},{6,7},{7,8},{8,9},{9,10},{10,1... | collective-permute-start | bytes 786440 | tf_op jit(solution)/shard_map/ppermute | solution.py:258
  119.6 4.6 %own_forward.14 = (f32[8,128,128]{2,1,0:T(8,128)S(1)}, f32[4,128,128]{2,1,0:T(8,128)S(1)}, f32[4,128,128]{2,1,0:T(8,128)S(1)}, f32[4,128,128]{2,1,0:T(8,128)S(1)...) custom-call(s32[1]{0:T(128)} %bitcast.first_ref.refs_0_, s32[1,256]{1,0:T(1,128)S(1)} %copy-done, ...), custom_call_target="tpu_custom_call" | custom-call | flops 15728640 | bytes 8388608 | tf_op jit(solution)/shard_map/own_forward/pallas_call | solution.py:336
  124.3 4.8 %collective-permute-done.15.refs_6_ = f32[4,128,128]{2,1,0:T(8,128)S(1)} collective-permute-done((f32[4,128,128]{2,1,0:T(8,128)S(1)}, f32[4,128,128]{2,1,0:T(8,128)S(1)}, u32[]{:S(2)}, u32[]{:S(2)}) %collective-permute-start.15) | collective-permute-done | bytes 262176 | tf_op jit(solution)/shard_map/ppermute | solution.py:258
  129.9 2.1 collective-permute-start.16
  133.4 4.6 %own_forward.15 = (f32[8,128,128]{2,1,0:T(8,128)S(1)}, f32[4,128,128]{2,1,0:T(8,128)S(1)}, f32[4,128,128]{2,1,0:T(8,128)S(1)}, f32[4,128,128]{2,1,0:T(8,128)S(1)...) custom-call(s32[1]{0:T(128)} %bitcast.first_ref.refs_0_, s32[1,256]{1,0:T(1,128)S(1)} %copy-done, ...), custom_call_target="tpu_custom_call" | custom-call | flops 15728640 | bytes 8388608 | tf_op jit(solution)/shard_map/own_forward/pallas_call | solution.py:336
  138.0 7.9 %collective-permute-done.17.refs_6_ = f32[4,128,128]{2,1,0:T(8,128)S(1)} collective-permute-done((f32[4,128,128]{2,1,0:T(8,128)S(1)}, f32[4,128,128]{2,1,0:T(8,128)S(1)}, u32[]{:S(2)}, u32[]{:S(2)}) %collective-permute-start.17) | collective-permute-done | bytes 262176 | tf_op jit(solution)/shard_map/ppermute | solution.py:258
  146.8 4.7 %own_adjoint.8 = (f32[8,128,128]{2,1,0:T(8,128)S(1)}, f32[4,128,128]{2,1,0:T(8,128)S(1)}, f32[4,128,128]{2,1,0:T(8,128)S(1)}, f32[256,128]{1,0:T(8,128)S(1)}, f32[16,128,128]{2,1,0:T(8,128)S(1)}) custom-call(s32[1]{0:T(128)} %bitcast.first_ref.refs_0_, s32[1,256]{1,0:T(1,128)S(1)} %copy-done, s32[3,384]{1,0:T(4,128)S(1)} %sort_receivers.1.refs_2_, ...), custom_call_target="tpu_custom_call" | custom-call | flops 15728640 | bytes 8388608 | tf_op jit(solution)/shard_map/own_adjoint/pallas_call | solution.py:370
  152.4 2.3 collective-permute-start.18
  156.0 4.4 %own_adjoint.9 = (f32[8,128,128]{2,1,0:T(8,128)S(1)}, f32[4,128,128]{2,1,0:T(8,128)S(1)}, f32[4,128,128]{2,1,0:T(8,128)S(1)}, f32[16,128,128]{2,1,0:T(8,128)S(1)}) custom-call(s32[1]{0:T(128)} %bitcast.first_ref.refs_0_, s32[1,256]{1,0:T(1,128)S(1)} %copy-done, s32[3,384]{1,0:T(4,128)S(1)} %sort_receivers.1.refs_2_, ...), custom_call_target="tpu_custom_call" | custom-call | flops 15728640 | bytes 8388608 | tf_op jit(solution)/shard_map/own_adjoint/pallas_call | solution.py:370
  160.4 5.7 %collective-permute-done.19.refs_4_ = f32[4,128,128]{2,1,0:T(8,128)S(1)} collective-permute-done((f32[4,128,128]{2,1,0:T(8,128)S(1)}, f32[4,128,128]{2,1,0:T(8,128)S(1)}, u32[]{:S(2)}, u32[]{:S(2)}) %collective-permute-start.19) | collective-permute-done | bytes 262176 | tf_op jit(solution)/shard_map/ppermute | solution.py:258
  167.0 2.3 collective-permute-start.20
  170.7 4.4 %own_adjoint.10 = (f32[8,128,128]{2,1,0:T(8,128)S(1)}, f32[4,128,128]{2,1,0:T(8,128)S(1)}, f32[4,128,128]{2,1,0:T(8,128)S(1)}, f32[16,128,128]{2,1,0:T(8,128)S(1)}) custom-call(s32[1]{0:T(128)} %bitcast.first_ref.refs_0_, s32[1,256]{1,0:T(1,128)S(1)} %copy-done, s32[3,384]{1,0:T(4,128)S(1)} %sort_receivers.1.refs_2_, ...), custom_call_target="tpu_custom_call" | custom-call | flops 15728640 | bytes 8388608 | tf_op jit(solution)/shard_map/own_adjoint/pallas_call | solution.py:370
  175.0 5.6 %collective-permute-done.21.refs_4_ = f32[4,128,128]{2,1,0:T(8,128)S(1)} collective-permute-done((f32[4,128,128]{2,1,0:T(8,128)S(1)}, f32[4,128,128]{2,1,0:T(8,128)S(1)}, u32[]{:S(2)}, u32[]{:S(2)}) %collective-permute-start.21) | collective-permute-done | bytes 262176 | tf_op jit(solution)/shard_map/ppermute | solution.py:258
  181.5 2.3 collective-permute-start.22
  185.2 4.4 %own_adjoint.11 = (f32[8,128,128]{2,1,0:T(8,128)S(1)}, f32[4,128,128]{2,1,0:T(8,128)S(1)}, f32[4,128,128]{2,1,0:T(8,128)S(1)}, f32[16,128,128]{2,1,0:T(8,128)S(1)}) custom-call(s32[1]{0:T(128)} %bitcast.first_ref.refs_0_, s32[1,256]{1,0:T(1,128)S(1)} %copy-done, s32[3,384]{1,0:T(4,128)S(1)} %sort_receivers.1.refs_2_, ...), custom_call_target="tpu_custom_call" | custom-call | flops 15728640 | bytes 8388608 | tf_op jit(solution)/shard_map/own_adjoint/pallas_call | solution.py:370
  189.5 5.7 %collective-permute-done.23.refs_4_ = f32[4,128,128]{2,1,0:T(8,128)S(1)} collective-permute-done((f32[4,128,128]{2,1,0:T(8,128)S(1)}, f32[4,128,128]{2,1,0:T(8,128)S(1)}, u32[]{:S(2)}, u32[]{:S(2)}) %collective-permute-start.23) | collective-permute-done | bytes 262176 | tf_op jit(solution)/shard_map/ppermute | solution.py:258
  196.2 2.3 collective-permute-start.24
  198.5 1.5 collective-permute-start.25
  200.0 4.3 %own_adjoint.12 = (f32[8,128,128]{2,1,0:T(8,128)S(1)}, f32[4,128,128]{2,1,0:T(8,128)S(1)}, f32[4,128,128]{2,1,0:T(8,128)S(1)}, f32[16,128,128]{2,1,0:T(8,128)S(1)}) custom-call(s32[1]{0:T(128)} %bitcast.first_ref.refs_0_, s32[1,256]{1,0:T(1,128)S(1)} %copy-done, s32[3,384]{1,0:T(4,128)S(1)} %sort_receivers.1.refs_2_, ...), custom_call_target="tpu_custom_call" | custom-call | flops 15728640 | bytes 8388608 | tf_op jit(solution)/shard_map/own_adjoint/pallas_call | solution.py:370
  204.3 5.5 %collective-permute-done.25.refs_4_ = f32[4,128,128]{2,1,0:T(8,128)S(1)} collective-permute-done((f32[4,128,128]{2,1,0:T(8,128)S(1)}, f32[4,128,128]{2,1,0:T(8,128)S(1)}, u32[]{:S(2)}, u32[]{:S(2)}) %collective-permute-start.25) | collective-permute-done | bytes 262176 | tf_op jit(solution)/shard_map/ppermute | solution.py:258
  210.8 2.3 collective-permute-start.26
  214.4 4.3 %own_adjoint.13 = (f32[8,128,128]{2,1,0:T(8,128)S(1)}, f32[4,128,128]{2,1,0:T(8,128)S(1)}, f32[4,128,128]{2,1,0:T(8,128)S(1)}, f32[16,128,128]{2,1,0:T(8,128)S(1)}) custom-call(s32[1]{0:T(128)} %bitcast.first_ref.refs_0_, s32[1,256]{1,0:T(1,128)S(1)} %copy-done, s32[3,384]{1,0:T(4,128)S(1)} %sort_receivers.1.refs_2_, ...), custom_call_target="tpu_custom_call" | custom-call | flops 15728640 | bytes 8388608 | tf_op jit(solution)/shard_map/own_adjoint/pallas_call | solution.py:370
  218.8 5.7 %collective-permute-done.27.refs_4_ = f32[4,128,128]{2,1,0:T(8,128)S(1)} collective-permute-done((f32[4,128,128]{2,1,0:T(8,128)S(1)}, f32[4,128,128]{2,1,0:T(8,128)S(1)}, u32[]{:S(2)}, u32[]{:S(2)}) %collective-permute-start.27) | collective-permute-done | bytes 262176 | tf_op jit(solution)/shard_map/ppermute | solution.py:258
  225.4 2.3 collective-permute-start.28
  229.0 4.3 %own_adjoint.14 = (f32[8,128,128]{2,1,0:T(8,128)S(1)}, f32[4,128,128]{2,1,0:T(8,128)S(1)}, f32[4,128,128]{2,1,0:T(8,128)S(1)}, f32[16,128,128]{2,1,0:T(8,128)S(1)}) custom-call(s32[1]{0:T(128)} %bitcast.first_ref.refs_0_, s32[1,256]{1,0:T(1,128)S(1)} %copy-done, s32[3,384]{1,0:T(4,128)S(1)} %sort_receivers.1.refs_2_, ...), custom_call_target="tpu_custom_call" | custom-call | flops 15728640 | bytes 8388608 | tf_op jit(solution)/shard_map/own_adjoint/pallas_call | solution.py:370
  233.4 5.7 %collective-permute-done.29.refs_4_ = f32[4,128,128]{2,1,0:T(8,128)S(1)} collective-permute-done((f32[4,128,128]{2,1,0:T(8,128)S(1)}, f32[4,128,128]{2,1,0:T(8,128)S(1)}, u32[]{:S(2)}, u32[]{:S(2)}) %collective-permute-start.29) | collective-permute-done | bytes 262176 | tf_op jit(solution)/shard_map/ppermute | solution.py:258
  239.1 1.7 edge_adjoint.14
  240.8 3.0 collective-permute-start.30
  249.1 4.8 %own_adjoint.15 = (f32[8,128,128]{2,1,0:T(8,128)S(1)}, f32[4,128,128]{2,1,0:T(8,128)S(1)}, f32[4,128,128]{2,1,0:T(8,128)S(1)}, f32[16,128,128]{2,1,0:T(8,128)S(1)}) custom-call(s32[1]{0:T(128)} %bitcast.first_ref.refs_0_, s32[1,256]{1,0:T(1,128)S(1)} %copy-done, s32[3,384]{1,0:T(4,128)S(1)} %sort_receivers.1.refs_2_, ...), custom_call_target="tpu_custom_call" | custom-call | flops 15728640 | bytes 8388608 | tf_op jit(solution)/shard_map/own_adjoint/pallas_call | solution.py:370
  256.9 1.8 collective-permute-done.32
  260.0 2.9 collective-permute-start.34
  262.9 1.7 collective-permute-start.35
  265.8 3.4 %collective-permute-done.34 = f32[2,128,128]{2,1,0:T(8,128)S(1)} collective-permute-done((f32[2,128,128]{2,1,0:T(8,128)S(1)}, f32[2,128,128]{2,1,0:T(8,128)S(1)}, u32[]{:S(2)}, u32[]{:S(2)}) %collective-permute-start.34) | collective-permute-done | bytes 131104 | tf_op jit(solution)/shard_map/ppermute | solution.py:258
  269.3 6.8 %collective-permute-start.36 = (f32[2,128,128]{2,1,0:T(8,128)S(1)}, f32[2,128,128]{2,1,0:T(8,128)S(1)}, u32[]{:S(2)}, u32[]{:S(2)}) collective-permute-start(f32[2,128,128]{2,1,0:T(8,128)S(1)} %add_add_fusion), channel_id=1, source_target_pairs={{0,128},{16,144},{32,160},{48,176},{64,192},{80,208},{96,224},{112... | collective-permute-start | bytes 393224 | tf_op jit(solution)/shard_map/ppermute | solution.py:258
  276.0 3.1 collective-permute-done.36
  279.1 1.6 collective-permute-start.37
  280.7 2.8 collective-permute-start.38
  283.5 2.5 collective-permute-start.39
  288.7 1.9 collective-permute-done.40
  292.0 3.7 %collective-permute-start.41 = (f32[8,128]{1,0:T(8,128)S(1)}, f32[8,128]{1,0:T(8,128)S(1)}, u32[]{:S(2)}, u32[]{:S(2)}) collective-permute-start(f32[8,128]{1,0:T(8,128)S(1)} %broadcast_in_dim.7), channel_id=1, source_target_pairs={{0,4},{1,5},{2,6},{3,7},{4,8},{5,9},{6,10},{7,11},{8,12},{9,13},{1... | collective-permute-start | bytes 12296 | tf_op jit(solution)/shard_map/ppermute | solution.py:258
  295.7 2.8 collective-permute-start.43
  298.5 2.3 collective-permute-done.42
  301.5 1.7 collective-permute-start.44
  303.2 2.5 collective-permute-start.46
  308.9 1.5 subtract_multiply_fusion
  (133 shorter events, 52.9 us)
Async XLA Ops:
  0.6 5.0 %copy-start.17 = (f32[1,16,128,128]{3,2,1,0:T(8,128)S(1)}, f32[1,16,128,128]{3,2,1,0:T(8,128)}, u32[]{:S(2)}) copy-start(f32[1,16,128,128]{3,2,1,0:T(8,128)} %param.11) | copy-start | bytes 3145732
  2.0 3.6 %copy-start.15 = (f32[16,128,128]{2,1,0:T(8,128)S(1)}, f32[16,128,128]{2,1,0:T(8,128)}, u32[]{:S(2)}) copy-start(f32[16,128,128]{2,1,0:T(8,128)} %param.9) | copy-start | bytes 3145732
  2.0 17.9 %collective-permute-start.2 = (f32[4,128,128]{2,1,0:T(8,128)S(1)}, f32[4,128,128]{2,1,0:T(8,128)S(1)}, u32[]{:S(2)}, u32[]{:S(2)}) collective-permute-start(f32[4,128,128]{2,1,0:T(8,128)S(1)} %get-tuple-element.293.refs_7_.refs_11_), channel_id=1, source_target_pairs={{0,1},{1,2},{2,3},{3,4},{4,5},{5,6},{6,7},{7,8},{8,9},{9,10},{10,1... | collective-permute-start | bytes 786440 | tf_op jit(solution)/shard_map/ppermute | solution.py:258
  4.3 15.7 %collective-permute-start.3 = (f32[4,128,128]{2,1,0:T(8,128)S(1)}, f32[4,128,128]{2,1,0:T(8,128)S(1)}, u32[]{:S(2)}, u32[]{:S(2)}) collective-permute-start(f32[4,128,128]{2,1,0:T(8,128)S(1)} %get-tuple-element.294.refs_5_.refs_9_), channel_id=1, source_target_pairs={{1,0},{2,1},{3,2},{4,3},{5,4},{6,5},{7,6},{8,7},{9,8},{10,9},{11,1... | collective-permute-start | bytes 786440 | tf_op jit(solution)/shard_map/ppermute | solution.py:258
  5.7 9.3 %copy-start.18 = (f32[1,16,128,128]{3,2,1,0:T(8,128)S(1)}, f32[1,16,128,128]{3,2,1,0:T(8,128)}, u32[]{:S(2)}) copy-start(f32[1,16,128,128]{3,2,1,0:T(8,128)} %param.10) | copy-start | bytes 3145732
  19.9 7.4 %copy-start.1 = (f32[1,8,256]{2,1,0:T(8,128)S(1)}, f32[1,8,256]{2,1,0:T(8,128)}, u32[]{:S(2)}) copy-start(f32[1,8,256]{2,1,0:T(8,128)} %param.17) | copy-start | bytes 24580
  21.5 10.5 %collective-permute-start.4 = (f32[4,128,128]{2,1,0:T(8,128)S(1)}, f32[4,128,128]{2,1,0:T(8,128)S(1)}, u32[]{:S(2)}, u32[]{:S(2)}) collective-permute-start(f32[4,128,128]{2,1,0:T(8,128)S(1)} %get-tuple-element.142.refs_8_.refs_11_), channel_id=1, source_target_pairs={{0,1},{1,2},{2,3},{3,4},{4,5},{5,6},{6,7},{7,8},{8,9},{9,10},{10,1... | collective-permute-start | bytes 786440 | tf_op jit(solution)/shard_map/ppermute | solution.py:258
  26.1 15.1 %collective-permute-start.5 = (f32[4,128,128]{2,1,0:T(8,128)S(1)}, f32[4,128,128]{2,1,0:T(8,128)S(1)}, u32[]{:S(2)}, u32[]{:S(2)}) collective-permute-start(f32[4,128,128]{2,1,0:T(8,128)S(1)} %get-tuple-element.143.refs_6_.refs_9_), channel_id=1, source_target_pairs={{1,0},{2,1},{3,2},{4,3},{5,4},{6,5},{7,6},{8,7},{9,8},{10,9},{11,1... | collective-permute-start | bytes 786440 | tf_op jit(solution)/shard_map/ppermute | solution.py:258
  32.0 10.0 %copy-start.4 = (f32[8,128,128]{2,1,0:T(8,128)}, f32[8,128,128]{2,1,0:T(8,128)S(1)}, u32[]{:S(2)}) copy-start(f32[8,128,128]{2,1,0:T(8,128)S(1)} %get-tuple-element.262.refs_14_) | copy-start | bytes 1572868
  42.0 9.6 %copy-start.10 = (f32[4,128,128]{2,1,0:T(8,128)}, f32[4,128,128]{2,1,0:T(8,128)S(1)}, u32[]{:S(2)}) copy-start(f32[4,128,128]{2,1,0:T(8,128)S(1)} %get-tuple-element.261.refs_13_) | copy-start | bytes 786436
  42.0 9.6 %copy-start.12 = (f32[4,128,128]{2,1,0:T(8,128)}, f32[4,128,128]{2,1,0:T(8,128)S(1)}, u32[]{:S(2)}) copy-start(f32[4,128,128]{2,1,0:T(8,128)S(1)} %get-tuple-element.263.refs_15_) | copy-start | bytes 786436
  42.0 9.6 %collective-permute-start.6 = (f32[4,128,128]{2,1,0:T(8,128)S(1)}, f32[4,128,128]{2,1,0:T(8,128)S(1)}, u32[]{:S(2)}, u32[]{:S(2)}) collective-permute-start(f32[4,128,128]{2,1,0:T(8,128)S(1)} %get-tuple-element.149.refs_8_.refs_11_), channel_id=1, source_target_pairs={{0,1},{1,2},{2,3},{3,4},{4,5},{5,6},{6,7},{7,8},{8,9},{9,10},{10,1... | collective-permute-start | bytes 786440 | tf_op jit(solution)/shard_map/ppermute | solution.py:258
  45.7 14.9 %collective-permute-start.7 = (f32[4,128,128]{2,1,0:T(8,128)S(1)}, f32[4,128,128]{2,1,0:T(8,128)S(1)}, u32[]{:S(2)}, u32[]{:S(2)}) collective-permute-start(f32[4,128,128]{2,1,0:T(8,128)S(1)} %get-tuple-element.150.refs_6_.refs_9_), channel_id=1, source_target_pairs={{1,0},{2,1},{3,2},{4,3},{5,4},{6,5},{7,6},{8,7},{9,8},{10,9},{11,1... | collective-permute-start | bytes 786440 | tf_op jit(solution)/shard_map/ppermute | solution.py:258
  61.5 8.1 %collective-permute-start.8 = (f32[4,128,128]{2,1,0:T(8,128)S(1)}, f32[4,128,128]{2,1,0:T(8,128)S(1)}, u32[]{:S(2)}, u32[]{:S(2)}) collective-permute-start(f32[4,128,128]{2,1,0:T(8,128)S(1)} %get-tuple-element.156.refs_8_.refs_11_), channel_id=1, source_target_pairs={{0,1},{1,2},{2,3},{3,4},{4,5},{5,6},{6,7},{7,8},{8,9},{9,10},{10,1... | collective-permute-start | bytes 786440 | tf_op jit(solution)/shard_map/ppermute | solution.py:258
  63.7 15.2 %collective-permute-start.9 = (f32[4,128,128]{2,1,0:T(8,128)S(1)}, f32[4,128,128]{2,1,0:T(8,128)S(1)}, u32[]{:S(2)}, u32[]{:S(2)}) collective-permute-start(f32[4,128,128]{2,1,0:T(8,128)S(1)} %get-tuple-element.157.refs_6_.refs_9_), channel_id=1, source_target_pairs={{1,0},{2,1},{3,2},{4,3},{5,4},{6,5},{7,6},{8,7},{9,8},{10,9},{11,1... | collective-permute-start | bytes 786440 | tf_op jit(solution)/shard_map/ppermute | solution.py:258
  79.8 8.1 %collective-permute-start.10 = (f32[4,128,128]{2,1,0:T(8,128)S(1)}, f32[4,128,128]{2,1,0:T(8,128)S(1)}, u32[]{:S(2)}, u32[]{:S(2)}) collective-permute-start(f32[4,128,128]{2,1,0:T(8,128)S(1)} %get-tuple-element.163.refs_8_.refs_11_), channel_id=1, source_target_pairs={{0,1},{1,2},{2,3},{3,4},{4,5},{5,6},{6,7},{7,8},{8,9},{9,10},{10,1... | collective-permute-start | bytes 786440 | tf_op jit(solution)/shard_map/ppermute | solution.py:258
  82.0 12.7 %collective-permute-start.11 = (f32[4,128,128]{2,1,0:T(8,128)S(1)}, f32[4,128,128]{2,1,0:T(8,128)S(1)}, u32[]{:S(2)}, u32[]{:S(2)}) collective-permute-start(f32[4,128,128]{2,1,0:T(8,128)S(1)} %get-tuple-element.164.refs_6_.refs_9_), channel_id=1, source_target_pairs={{1,0},{2,1},{3,2},{4,3},{5,4},{6,5},{7,6},{8,7},{9,8},{10,9},{11,1... | collective-permute-start | bytes 786440 | tf_op jit(solution)/shard_map/ppermute | solution.py:258
  95.5 8.4 %collective-permute-start.12 = (f32[4,128,128]{2,1,0:T(8,128)S(1)}, f32[4,128,128]{2,1,0:T(8,128)S(1)}, u32[]{:S(2)}, u32[]{:S(2)}) collective-permute-start(f32[4,128,128]{2,1,0:T(8,128)S(1)} %get-tuple-element.170.refs_8_.refs_11_), channel_id=1, source_target_pairs={{0,1},{1,2},{2,3},{3,4},{4,5},{5,6},{6,7},{7,8},{8,9},{9,10},{10,1... | collective-permute-start | bytes 786440 | tf_op jit(solution)/shard_map/ppermute | solution.py:258
  98.0 11.2 %collective-permute-start.13 = (f32[4,128,128]{2,1,0:T(8,128)S(1)}, f32[4,128,128]{2,1,0:T(8,128)S(1)}, u32[]{:S(2)}, u32[]{:S(2)}) collective-permute-start(f32[4,128,128]{2,1,0:T(8,128)S(1)} %get-tuple-element.171.refs_6_.refs_9_), channel_id=1, source_target_pairs={{1,0},{2,1},{3,2},{4,3},{5,4},{6,5},{7,6},{8,7},{9,8},{10,9},{11,1... | collective-permute-start | bytes 786440 | tf_op jit(solution)/shard_map/ppermute | solution.py:258
  109.1 4.5 %copy-start.19 = (f32[1,16,128,128]{3,2,1,0:T(8,128)S(1)}, f32[1,16,128,128]{3,2,1,0:T(8,128)}, u32[]{:S(2)}) copy-start(f32[1,16,128,128]{3,2,1,0:T(8,128)} %param.13) | copy-start | bytes 3145732
  109.2 4.5 %copy-start.20 = (f32[1,16,128,128]{3,2,1,0:T(8,128)S(1)}, f32[1,16,128,128]{3,2,1,0:T(8,128)}, u32[]{:S(2)}) copy-start(f32[1,16,128,128]{3,2,1,0:T(8,128)} %param.12) | copy-start | bytes 3145732
  110.0 14.2 %collective-permute-start.14 = (f32[4,128,128]{2,1,0:T(8,128)S(1)}, f32[4,128,128]{2,1,0:T(8,128)S(1)}, u32[]{:S(2)}, u32[]{:S(2)}) collective-permute-start(f32[4,128,128]{2,1,0:T(8,128)S(1)} %get-tuple-element.177.refs_8_.refs_11_), channel_id=1, source_target_pairs={{0,1},{1,2},{2,3},{3,4},{4,5},{5,6},{6,7},{7,8},{8,9},{9,10},{10,1... | collective-permute-start | bytes 786440 | tf_op jit(solution)/shard_map/ppermute | solution.py:258
  112.3 16.7 %collective-permute-start.15 = (f32[4,128,128]{2,1,0:T(8,128)S(1)}, f32[4,128,128]{2,1,0:T(8,128)S(1)}, u32[]{:S(2)}, u32[]{:S(2)}) collective-permute-start(f32[4,128,128]{2,1,0:T(8,128)S(1)} %get-tuple-element.178.refs_6_.refs_9_), channel_id=1, source_target_pairs={{1,0},{2,1},{3,2},{4,3},{5,4},{6,5},{7,6},{8,7},{9,8},{10,9},{11,1... | collective-permute-start | bytes 786440 | tf_op jit(solution)/shard_map/ppermute | solution.py:258
  113.8 37.7 %collective-permute-start = (f32[4,128,128]{2,1,0:T(8,128)S(1)}, f32[4,128,128]{2,1,0:T(8,128)S(1)}, u32[]{:S(2)}, u32[]{:S(2)}) collective-permute-start(f32[4,128,128]{2,1,0:T(8,128)S(1)} %get-tuple-element.295.refs_6_.refs_8_), channel_id=1, source_target_pairs={{0,1},{1,2},{2,3},{3,4},{4,5},{5,6},{6,7},{7,8},{8,9},{9,10},{10,1... | collective-permute-start | bytes 786440 | tf_op jit(solution)/shard_map/ppermute | solution.py:258
  118.3 33.2 %collective-permute-start.1 = (f32[4,128,128]{2,1,0:T(8,128)S(1)}, f32[4,128,128]{2,1,0:T(8,128)S(1)}, u32[]{:S(2)}, u32[]{:S(2)}) collective-permute-start(f32[4,128,128]{2,1,0:T(8,128)S(1)} %get-tuple-element.296.refs_4_.refs_6_), channel_id=1, source_target_pairs={{1,0},{2,1},{3,2},{4,3},{5,4},{6,5},{7,6},{8,7},{9,8},{10,9},{11,1... | collective-permute-start | bytes 786440 | tf_op jit(solution)/shard_map/ppermute | solution.py:258
  129.9 8.1 %collective-permute-start.16 = (f32[4,128,128]{2,1,0:T(8,128)S(1)}, f32[4,128,128]{2,1,0:T(8,128)S(1)}, u32[]{:S(2)}, u32[]{:S(2)}) collective-permute-start(f32[4,128,128]{2,1,0:T(8,128)S(1)} %get-tuple-element.184.refs_8_), channel_id=1, source_target_pairs={{0,1},{1,2},{2,3},{3,4},{4,5},{5,6},{6,7},{7,8},{8,9},{9,10},{10,1... | collective-permute-start | bytes 786440 | tf_op jit(solution)/shard_map/ppermute | solution.py:258
  132.0 13.9 %collective-permute-start.17 = (f32[4,128,128]{2,1,0:T(8,128)S(1)}, f32[4,128,128]{2,1,0:T(8,128)S(1)}, u32[]{:S(2)}, u32[]{:S(2)}) collective-permute-start(f32[4,128,128]{2,1,0:T(8,128)S(1)} %get-tuple-element.185.refs_6_), channel_id=1, source_target_pairs={{1,0},{2,1},{3,2},{4,3},{5,4},{6,5},{7,6},{8,7},{9,8},{10,9},{11,1... | collective-permute-start | bytes 786440 | tf_op jit(solution)/shard_map/ppermute | solution.py:258
  152.4 8.0 %collective-permute-start.18 = (f32[4,128,128]{2,1,0:T(8,128)S(1)}, f32[4,128,128]{2,1,0:T(8,128)S(1)}, u32[]{:S(2)}, u32[]{:S(2)}) collective-permute-start(f32[4,128,128]{2,1,0:T(8,128)S(1)} %get-tuple-element.197.refs_5_.refs_8_), channel_id=1, source_target_pairs={{0,1},{1,2},{2,3},{3,4},{4,5},{5,6},{6,7},{7,8},{8,9},{9,10},{10,1... | collective-permute-start | bytes 786440 | tf_op jit(solution)/shard_map/ppermute | solution.py:258
  154.7 11.4 %collective-permute-start.19 = (f32[4,128,128]{2,1,0:T(8,128)S(1)}, f32[4,128,128]{2,1,0:T(8,128)S(1)}, u32[]{:S(2)}, u32[]{:S(2)}) collective-permute-start(f32[4,128,128]{2,1,0:T(8,128)S(1)} %get-tuple-element.198.refs_3_.refs_6_), channel_id=1, source_target_pairs={{1,0},{2,1},{3,2},{4,3},{5,4},{6,5},{7,6},{8,7},{9,8},{10,9},{11,1... | collective-permute-start | bytes 786440 | tf_op jit(solution)/shard_map/ppermute | solution.py:258
  167.0 8.0 %collective-permute-start.20 = (f32[4,128,128]{2,1,0:T(8,128)S(1)}, f32[4,128,128]{2,1,0:T(8,128)S(1)}, u32[]{:S(2)}, u32[]{:S(2)}) collective-permute-start(f32[4,128,128]{2,1,0:T(8,128)S(1)} %get-tuple-element.207.refs_5_.refs_8_), channel_id=1, source_target_pairs={{0,1},{1,2},{2,3},{3,4},{4,5},{5,6},{6,7},{7,8},{8,9},{9,10},{10,1... | collective-permute-start | bytes 786440 | tf_op jit(solution)/shard_map/ppermute | solution.py:258
  169.4 11.2 %collective-permute-start.21 = (f32[4,128,128]{2,1,0:T(8,128)S(1)}, f32[4,128,128]{2,1,0:T(8,128)S(1)}, u32[]{:S(2)}, u32[]{:S(2)}) collective-permute-start(f32[4,128,128]{2,1,0:T(8,128)S(1)} %get-tuple-element.208.refs_3_.refs_6_), channel_id=1, source_target_pairs={{1,0},{2,1},{3,2},{4,3},{5,4},{6,5},{7,6},{8,7},{9,8},{10,9},{11,1... | collective-permute-start | bytes 786440 | tf_op jit(solution)/shard_map/ppermute | solution.py:258
  181.5 8.0 %collective-permute-start.22 = (f32[4,128,128]{2,1,0:T(8,128)S(1)}, f32[4,128,128]{2,1,0:T(8,128)S(1)}, u32[]{:S(2)}, u32[]{:S(2)}) collective-permute-start(f32[4,128,128]{2,1,0:T(8,128)S(1)} %get-tuple-element.217.refs_5_.refs_8_), channel_id=1, source_target_pairs={{0,1},{1,2},{2,3},{3,4},{4,5},{5,6},{6,7},{7,8},{8,9},{9,10},{10,1... | collective-permute-start | bytes 786440 | tf_op jit(solution)/shard_map/ppermute | solution.py:258
  183.9 11.4 %collective-permute-start.23 = (f32[4,128,128]{2,1,0:T(8,128)S(1)}, f32[4,128,128]{2,1,0:T(8,128)S(1)}, u32[]{:S(2)}, u32[]{:S(2)}) collective-permute-start(f32[4,128,128]{2,1,0:T(8,128)S(1)} %get-tuple-element.218.refs_3_.refs_6_), channel_id=1, source_target_pairs={{1,0},{2,1},{3,2},{4,3},{5,4},{6,5},{7,6},{8,7},{9,8},{10,9},{11,1... | collective-permute-start | bytes 786440 | tf_op jit(solution)/shard_map/ppermute | solution.py:258
  196.2 8.2 %collective-permute-start.24 = (f32[4,128,128]{2,1,0:T(8,128)S(1)}, f32[4,128,128]{2,1,0:T(8,128)S(1)}, u32[]{:S(2)}, u32[]{:S(2)}) collective-permute-start(f32[4,128,128]{2,1,0:T(8,128)S(1)} %get-tuple-element.227.refs_5_.refs_8_), channel_id=1, source_target_pairs={{0,1},{1,2},{2,3},{3,4},{4,5},{5,6},{6,7},{7,8},{8,9},{9,10},{10,1... | collective-permute-start | bytes 786440 | tf_op jit(solution)/shard_map/ppermute | solution.py:258
  198.5 11.3 %collective-permute-start.25 = (f32[4,128,128]{2,1,0:T(8,128)S(1)}, f32[4,128,128]{2,1,0:T(8,128)S(1)}, u32[]{:S(2)}, u32[]{:S(2)}) collective-permute-start(f32[4,128,128]{2,1,0:T(8,128)S(1)} %get-tuple-element.228.refs_3_.refs_6_), channel_id=1, source_target_pairs={{1,0},{2,1},{3,2},{4,3},{5,4},{6,5},{7,6},{8,7},{9,8},{10,9},{11,1... | collective-permute-start | bytes 786440 | tf_op jit(solution)/shard_map/ppermute | solution.py:258
  210.8 8.0 %collective-permute-start.26 = (f32[4,128,128]{2,1,0:T(8,128)S(1)}, f32[4,128,128]{2,1,0:T(8,128)S(1)}, u32[]{:S(2)}, u32[]{:S(2)}) collective-permute-start(f32[4,128,128]{2,1,0:T(8,128)S(1)} %get-tuple-element.237.refs_5_.refs_8_), channel_id=1, source_target_pairs={{0,1},{1,2},{2,3},{3,4},{4,5},{5,6},{6,7},{7,8},{8,9},{9,10},{10,1... | collective-permute-start | bytes 786440 | tf_op jit(solution)/shard_map/ppermute | solution.py:258
  213.1 11.4 %collective-permute-start.27 = (f32[4,128,128]{2,1,0:T(8,128)S(1)}, f32[4,128,128]{2,1,0:T(8,128)S(1)}, u32[]{:S(2)}, u32[]{:S(2)}) collective-permute-start(f32[4,128,128]{2,1,0:T(8,128)S(1)} %get-tuple-element.238.refs_3_.refs_6_), channel_id=1, source_target_pairs={{1,0},{2,1},{3,2},{4,3},{5,4},{6,5},{7,6},{8,7},{9,8},{10,9},{11,1... | collective-permute-start | bytes 786440 | tf_op jit(solution)/shard_map/ppermute | solution.py:258
  225.4 8.0 %collective-permute-start.28 = (f32[4,128,128]{2,1,0:T(8,128)S(1)}, f32[4,128,128]{2,1,0:T(8,128)S(1)}, u32[]{:S(2)}, u32[]{:S(2)}) collective-permute-start(f32[4,128,128]{2,1,0:T(8,128)S(1)} %get-tuple-element.247.refs_5_.refs_8_), channel_id=1, source_target_pairs={{0,1},{1,2},{2,3},{3,4},{4,5},{5,6},{6,7},{7,8},{8,9},{9,10},{10,1... | collective-permute-start | bytes 786440 | tf_op jit(solution)/shard_map/ppermute | solution.py:258
  227.7 11.4 %collective-permute-start.29 = (f32[4,128,128]{2,1,0:T(8,128)S(1)}, f32[4,128,128]{2,1,0:T(8,128)S(1)}, u32[]{:S(2)}, u32[]{:S(2)}) collective-permute-start(f32[4,128,128]{2,1,0:T(8,128)S(1)} %get-tuple-element.248.refs_3_.refs_6_), channel_id=1, source_target_pairs={{1,0},{2,1},{3,2},{4,3},{5,4},{6,5},{7,6},{8,7},{9,8},{10,9},{11,1... | collective-permute-start | bytes 786440 | tf_op jit(solution)/shard_map/ppermute | solution.py:258
  233.4 7.4 %copy-start.6 = (f32[8,128,128]{2,1,0:T(8,128)}, f32[8,128,128]{2,1,0:T(8,128)S(1)}, u32[]{:S(2)}) copy-start(f32[8,128,128]{2,1,0:T(8,128)S(1)} %get-tuple-element.258.refs_4_) | copy-start | bytes 1572868
  240.8 13.2 %collective-permute-start.30 = (f32[4,128,128]{2,1,0:T(8,128)}, f32[4,128,128]{2,1,0:T(8,128)}, u32[]{:S(2)}, u32[]{:S(2)}) collective-permute-start(f32[4,128,128]{2,1,0:T(8,128)} %get-tuple-element.259.refs_5_), channel_id=1, source_target_pairs={{0,1},{1,2},{2,3},{3,4},{4,5},{5,6},{6,7},{7,8},{8,9},{9,10},{10,1... | collective-permute-start | bytes 786440 | tf_op jit(solution)/shard_map/ppermute | solution.py:258
  243.8 11.3 %collective-permute-start.31 = (f32[4,128,128]{2,1,0:T(8,128)}, f32[4,128,128]{2,1,0:T(8,128)}, u32[]{:S(2)}, u32[]{:S(2)}) collective-permute-start(f32[4,128,128]{2,1,0:T(8,128)} %get-tuple-element.257.refs_3_), channel_id=1, source_target_pairs={{1,0},{2,1},{3,2},{4,3},{5,4},{6,5},{7,6},{8,7},{9,8},{10,9},{11,1... | collective-permute-start | bytes 786440 | tf_op jit(solution)/shard_map/ppermute | solution.py:258
  245.1 1.0 copy-start.5
  246.2 1.0 copy-start.7
  247.2 0.9 copy-start.11
  248.2 0.9 copy-start.13
  249.1 4.8 %copy-start.3 = (f32[8,128,128]{2,1,0:T(8,128)S(1)}, f32[8,128,128]{2,1,0:T(8,128)}, u32[]{:S(2)}) copy-start(f32[8,128,128]{2,1,0:T(8,128)} %copy-done.2) | copy-start | bytes 1572868
  255.1 1.3 copy-start.9
  256.7 2.0 collective-permute-start.32
  258.8 6.9 %collective-permute-start.33 = (f32[2,128,128]{2,1,0:T(8,128)S(1)}, f32[2,128,128]{2,1,0:T(8,128)S(1)}, u32[]{:S(2)}, u32[]{:S(2)}) collective-permute-start(f32[2,128,128]{2,1,0:T(8,128)S(1)} %get-tuple-element.290), channel_id=1, source_target_pairs={{0,32},{16,48},{32,64},{48,80},{64,96},{80,112},{96,0},{112,16},{1... | collective-permute-start | bytes 393224 | tf_op jit(solution)/shard_map/ppermute | solution.py:258
  260.0 9.2 %collective-permute-start.34 = (f32[2,128,128]{2,1,0:T(8,128)S(1)}, f32[2,128,128]{2,1,0:T(8,128)S(1)}, u32[]{:S(2)}, u32[]{:S(2)}) collective-permute-start(f32[2,128,128]{2,1,0:T(8,128)S(1)} %get-tuple-element.292), channel_id=1, source_target_pairs={{0,64},{16,80},{32,96},{48,112},{64,0},{80,16},{96,32},{112,48},{1... | collective-permute-start | bytes 393224 | tf_op jit(solution)/shard_map/ppermute | solution.py:258
  262.9 6.3 %collective-permute-start.35 = (f32[2,128,128]{2,1,0:T(8,128)S(1)}, f32[2,128,128]{2,1,0:T(8,128)S(1)}, u32[]{:S(2)}, u32[]{:S(2)}) collective-permute-start(f32[2,128,128]{2,1,0:T(8,128)S(1)} %get-tuple-element.291), channel_id=1, source_target_pairs={{0,96},{16,112},{32,0},{48,16},{64,32},{80,48},{96,64},{112,80},{1... | collective-permute-start | bytes 393224 | tf_op jit(solution)/shard_map/ppermute | solution.py:258
  269.3 9.8 %collective-permute-start.36 = (f32[2,128,128]{2,1,0:T(8,128)S(1)}, f32[2,128,128]{2,1,0:T(8,128)S(1)}, u32[]{:S(2)}, u32[]{:S(2)}) collective-permute-start(f32[2,128,128]{2,1,0:T(8,128)S(1)} %add_add_fusion), channel_id=1, source_target_pairs={{0,128},{16,144},{32,160},{48,176},{64,192},{80,208},{96,224},{112... | collective-permute-start | bytes 393224 | tf_op jit(solution)/shard_map/ppermute | solution.py:258
  279.1 7.7 %collective-permute-start.37 = (f32[2,128,128]{2,1,0:T(8,128)S(1)}, f32[2,128,128]{2,1,0:T(8,128)S(1)}, u32[]{:S(2)}, u32[]{:S(2)}) collective-permute-start(f32[2,128,128]{2,1,0:T(8,128)S(1)} %get-tuple-element.277), channel_id=1, source_target_pairs={{0,32},{16,48},{32,64},{48,80},{64,96},{80,112},{96,0},{112,16},{1... | collective-permute-start | bytes 393224 | tf_op jit(solution)/shard_map/ppermute | solution.py:258
  280.7 7.5 %collective-permute-start.38 = (f32[2,128,128]{2,1,0:T(8,128)S(1)}, f32[2,128,128]{2,1,0:T(8,128)S(1)}, u32[]{:S(2)}, u32[]{:S(2)}) collective-permute-start(f32[2,128,128]{2,1,0:T(8,128)S(1)} %get-tuple-element.277), channel_id=1, source_target_pairs={{0,64},{16,80},{32,96},{48,112},{64,0},{80,16},{96,32},{112,48},{1... | collective-permute-start | bytes 393224 | tf_op jit(solution)/shard_map/ppermute | solution.py:258
  283.5 5.1 %collective-permute-start.39 = (f32[2,128,128]{2,1,0:T(8,128)S(1)}, f32[2,128,128]{2,1,0:T(8,128)S(1)}, u32[]{:S(2)}, u32[]{:S(2)}) collective-permute-start(f32[2,128,128]{2,1,0:T(8,128)S(1)} %get-tuple-element.277), channel_id=1, source_target_pairs={{0,96},{16,112},{32,0},{48,16},{64,32},{80,48},{96,64},{112,80},{1... | collective-permute-start | bytes 393224 | tf_op jit(solution)/shard_map/ppermute | solution.py:258
  288.6 2.0 collective-permute-start.40
  290.7 18.2 %copy-start.16 = (f32[16,128,128]{2,1,0:T(8,128)S(1)}, f32[16,128,128]{2,1,0:T(8,128)}, u32[]{:S(2)}) copy-start(f32[16,128,128]{2,1,0:T(8,128)} %param.9) | copy-start | bytes 3145732
  292.0 6.4 %collective-permute-start.41 = (f32[8,128]{1,0:T(8,128)S(1)}, f32[8,128]{1,0:T(8,128)S(1)}, u32[]{:S(2)}, u32[]{:S(2)}) collective-permute-start(f32[8,128]{1,0:T(8,128)S(1)} %broadcast_in_dim.7), channel_id=1, source_target_pairs={{0,4},{1,5},{2,6},{3,7},{4,8},{5,9},{6,10},{7,11},{8,12},{9,13},{1... | collective-permute-start | bytes 12296 | tf_op jit(solution)/shard_map/ppermute | solution.py:258
  295.7 5.1 %collective-permute-start.42 = (f32[8,128]{1,0:T(8,128)S(1)}, f32[8,128]{1,0:T(8,128)S(1)}, u32[]{:S(2)}, u32[]{:S(2)}) collective-permute-start(f32[8,128]{1,0:T(8,128)S(1)} %broadcast_in_dim.7), channel_id=1, source_target_pairs={{0,8},{1,9},{2,10},{3,11},{4,12},{5,13},{6,14},{7,15},{8,0},{9,1},... | collective-permute-start | bytes 12296 | tf_op jit(solution)/shard_map/ppermute | solution.py:258
  295.7 5.1 %collective-permute-start.43 = (f32[8,128]{1,0:T(8,128)S(1)}, f32[8,128]{1,0:T(8,128)S(1)}, u32[]{:S(2)}, u32[]{:S(2)}) collective-permute-start(f32[8,128]{1,0:T(8,128)S(1)} %broadcast_in_dim.7), channel_id=1, source_target_pairs={{0,12},{1,13},{2,14},{3,15},{4,0},{5,1},{6,2},{7,3},{8,4},{9,5},{1... | collective-permute-start | bytes 12296 | tf_op jit(solution)/shard_map/ppermute | solution.py:258
  301.5 5.5 %collective-permute-start.44 = (f32[8,128]{1,0:T(8,128)S(1)}, f32[8,128]{1,0:T(8,128)S(1)}, u32[]{:S(2)}, u32[]{:S(2)}) collective-permute-start(f32[8,128]{1,0:T(8,128)S(1)} %maximum_maximum_fusion.1), channel_id=1, source_target_pairs={{0,1},{1,2},{2,3},{3,0},{4,5},{5,6},{6,7},{7,4},{8,9},{9,10},{10,1... | collective-permute-start | bytes 12296 | tf_op jit(solution)/shard_map/ppermute | solution.py:258
  303.2 4.5 %collective-permute-start.45 = (f32[8,128]{1,0:T(8,128)S(1)}, f32[8,128]{1,0:T(8,128)S(1)}, u32[]{:S(2)}, u32[]{:S(2)}) collective-permute-start(f32[8,128]{1,0:T(8,128)S(1)} %maximum_maximum_fusion.1), channel_id=1, source_target_pairs={{0,2},{1,3},{2,0},{3,1},{4,6},{5,7},{6,4},{7,5},{8,10},{9,11},{10,... | collective-permute-start | bytes 12296 | tf_op jit(solution)/shard_map/ppermute | solution.py:258
  303.2 4.5 %collective-permute-start.46 = (f32[8,128]{1,0:T(8,128)S(1)}, f32[8,128]{1,0:T(8,128)S(1)}, u32[]{:S(2)}, u32[]{:S(2)}) collective-permute-start(f32[8,128]{1,0:T(8,128)S(1)} %maximum_maximum_fusion.1), channel_id=1, source_target_pairs={{0,3},{1,0},{2,1},{3,2},{4,7},{5,4},{6,5},{7,6},{8,11},{9,8},{10,9... | collective-permute-start | bytes 12296 | tf_op jit(solution)/shard_map/ppermute | solution.py:258
  (4 other events, 2.9 us)

commit v2 on v1

--- a/solution.py
+++ b/solution.py
@@ -18,9 +18,10 @@
 EDGE = 4
 MID = ROWS - 2 * EDGE
 CHUNK = 32
+SLICE = 8
 VMEM = pl.BlockSpec(memory_space=pltpu.VMEM)
 SMEM = pl.BlockSpec(memory_space=pltpu.SMEM)
-LIMIT = 24 * 1024 * 1024
+LIMIT = 12 * 1024 * 1024
 
 
 def planes(count):
@@ -42,28 +43,54 @@
 
 
 def sort_kernel(first_ref, receivers_ref, lists_ref):
+    def body(j, counts):
+        plane = where_of(receivers_ref[0, j], first_ref)[0]
+        inside = (plane >= 0) & (plane < ROWS)
+        low = inside & (plane < EDGE)
+        high = inside & (plane >= ROWS - EDGE)
+        mid = inside & (plane >= EDGE) & (plane < ROWS - EDGE)
+        lists_ref[jnp.where(low, 0, 3), counts[0]] = j
+        lists_ref[jnp.where(mid, 1, 3), counts[1]] = j
+        lists_ref[jnp.where(high, 2, 3), counts[2]] = j
+        return tuple(c + x.astype(jnp.int32) for c, x in zip(counts, (low, mid, high)))
+
+    zero = jnp.int32(0)
+    counts = lax.fori_loop(0, REC, body, (zero, zero, zero), unroll=4)
     for region in range(3):
-        lists_ref[region, REC] = 0
-
-    def body(j, carry):
-        plane = (receivers_ref[0, j] - first_ref[0]) >> 14
-        inside = (plane >= 0) & (plane < ROWS)
-        region = jnp.where(plane < EDGE, 0, jnp.where(plane < ROWS - EDGE, 1, 2))
-
-        @pl.when(inside)
-        def _():
-            count = lists_ref[region, REC]
-            lists_ref[region, count] = j
-            lists_ref[region, REC] = count + 1
-
-        return carry
-
-    lax.fori_loop(0, REC, body, 0)
-
-
-def where_of(cell, first):
-    local = cell - first
-    return local >> 14, (local >> 7) & 127, local & 127
+        lists_ref[region, REC] = counts[region]
+
+
+def where_of(cell, first_ref):
+    local = cell - first_ref[0]
+    plane = local >> 14
+    plane = jnp.where(first_ref[1] == 1, ROWS - 1 - plane, plane)
+    return plane, (local >> 7) & 127, local & 127
+
+
+def cut_kernel(first_ref, whole_ref, low_ref, mid_ref, high_ref):
+    start = 0
+    for ref, count in ((low_ref, EDGE), (mid_ref, MID), (high_ref, EDGE)):
+
+        def body(i, carry, ref=ref, start=start):
+            plane = jnp.where(first_ref[1] == 1, ROWS - 1 - start - i, start + i)
+            ref[i] = whole_ref[plane]
+            return carry
+
+        lax.fori_loop(0, count, body, 0)
+        start += count
+
+
+def join_kernel(first_ref, grad_ref, a_low, a_mid, a_high, b_low, b_mid, b_high, out_ref):
+    start = 0
+    for a, b, count in ((a_low, b_low, EDGE), (a_mid, b_mid, MID), (a_high, b_high, EDGE)):
+
+        def body(i, carry, a=a, b=b, start=start):
+            plane = jnp.where(first_ref[1] == 1, ROWS - 1 - start - i, start + i)
+            out_ref[plane] = grad_ref[start + i] + a[i] * b[i]
+            return carry
+
+        lax.fori_loop(0, count, body, 0)
+        start += count
 
 
 def lanes_row():
@@ -71,7 +98,7 @@
 
 
 def add_source(first_ref, source_ref, wavelet_ref, tick, ref, low, count):
-    plane, row, lane = where_of(source_ref[0], first_ref[0])
+    plane, row, lane = where_of(source_ref[0], first_ref)
     plane = plane - low
 
     @pl.when((plane >= 0) & (plane < count))
@@ -84,7 +111,7 @@
 def add_residuals(first_ref, receivers_ref, lists_ref, res_ref, ref, region, low):
     def body(i, carry):
         j = lists_ref[region, i]
-        plane, row, lane = where_of(receivers_ref[0, j], first_ref[0])
+        plane, row, lane = where_of(receivers_ref[0, j], first_ref)
         spot = ref[plane - low, pl.ds(row, 1), :]
         ref[plane - low, pl.ds(row, 1), :] = spot + res_ref[pl.ds(j, 1), :]
         return carry
@@ -99,7 +126,7 @@
 
         def body(i, carry):
             j = lists_ref[region, i]
-            plane, row, lane = where_of(receivers_ref[0, j], first_ref[0])
+            plane, row, lane = where_of(receivers_ref[0, j], first_ref)
             spot = ref[plane - low, pl.ds(row, 1), :]
             value = spot - observed_ref[tick, j]
             res_ref[pl.ds(j, 1), :] = jnp.where(lanes_row() == lane, value, 0.0)
@@ -128,12 +155,12 @@
 
 def laplace_rows(pad_ref, plane, row, lane_weights):
     at = plane + EDGE
-    field = pad_ref[at, pl.ds(8 + row, CHUNK), :]
+    field = pad_ref[at, pl.ds(8 + row, SLICE), :]
     total = (3.0 * CENTRE) * field
     for index, weight in enumerate(COEFFS):
         k = index + 1
-        pair = pad_ref[at + k, pl.ds(8 + row, CHUNK), :] + pad_ref[at - k, pl.ds(8 + row, CHUNK), :]
-        pair = pair + (pad_ref[at, pl.ds(8 + row + k, CHUNK), :] + pad_ref[at, pl.ds(8 + row - k, CHUNK), :])
+        pair = pad_ref[at + k, pl.ds(8 + row, SLICE), :] + pad_ref[at - k, pl.ds(8 + row, SLICE), :]
+        pair = pair + (pad_ref[at, pl.ds(8 + row + k, SLICE), :] + pad_ref[at, pl.ds(8 + row - k, SLICE), :])
         total = total + weight * pair
         total = total + lane_weights[2 * index] * pltpu.roll(field, NZ - k, 1)
         total = total + lane_weights[2 * index + 1] * pltpu.roll(field, k, 1)
@@ -141,7 +168,7 @@
 
 
 def make_lane_weights():
-    lane = lax.broadcasted_iota(jnp.int32, (CHUNK, NZ), 1)
+    lane = lax.broadcasted_iota(jnp.int32, (SLICE, NZ), 1)
     out = []
     for index, weight in enumerate(COEFFS):
         k = index + 1
@@ -153,7 +180,9 @@
 def own_kernel(forward, tick, has_extra, *refs):
     refs = list(refs)
     take = lambda n: [refs.pop(0) for _ in range(n)]
-    first_ref, receivers_ref, lists_ref = take(3)
+    first_ref = take(1)[0]
+    if not forward or tick > 0:
+        receivers_ref, lists_ref = take(2)
     if forward:
         source_ref, wavelet_ref = take(2)
     observed = take(1)[0] if (forward and tick > 0) or (not forward and tick == STEPS - 1) else None
@@ -184,9 +213,9 @@
     for region, count in enumerate((EDGE, MID, EDGE)):
 
         def body(i, carry, region=region, low=low):
-            for row in range(0, NY, CHUNK):
+            for row in range(0, NY, SLICE):
                 field, total = laplace_rows(pad_ref, low + i, row, weights)
-                rows = pl.ds(row, CHUNK)
+                rows = pl.ds(row, SLICE)
                 value = 2.0 * field - old[region][i, rows, :] + model[region][i, rows, :] * total
                 outs[region][i, rows, :] = value
                 if forward:
@@ -194,7 +223,7 @@
                 elif has_extra:
                     grad_out[low + i, rows, :] = grad_in[low + i, rows, :] + field * image[region][i, rows, :]
                 elif grad_out is not None:
-                    grad_out[low + i, rows, :] = jnp.zeros((CHUNK, NZ), jnp.float32)
+                    grad_out[low + i, rows, :] = jnp.zeros((SLICE, NZ), jnp.float32)
             return carry
 
         lax.fori_loop(0, count, body, 0)
@@ -211,47 +240,45 @@
         add_residuals(first_ref, receivers_ref, lists_ref, res_in, next_mid, 1, EDGE)
 
 
-def edge_kernel(forward, tick, *refs):
+def edge_kernel(forward, tick, high, *refs):
     refs = list(refs)
     take = lambda n: [refs.pop(0) for _ in range(n)]
-    first_ref, receivers_ref, lists_ref = take(3)
+    first_ref = take(1)[0]
     if forward:
         source_ref, wavelet_ref = take(2)
-    before, after, base_lo, base_hi, model_lo, model_hi = take(6)
-    if forward:
-        part_lo, part_hi = take(2)
+    else:
+        receivers_ref, lists_ref = take(2)
+    halo, base, model = take(3)
+    if forward:
+        part = take(1)[0]
     else:
         res_ref = take(1)[0]
-    next_lo, next_hi = take(2)
-    if forward:
-        image_lo, image_hi = take(2)
+    take(1)
+    edge = take(1)[0]
+    if forward:
+        image = take(1)[0]
 
     def body(c, carry):
         rows = pl.ds(pl.multiple_of(c * CHUNK, CHUNK), CHUNK)
-        low = [before[i, rows, :] for i in range(EDGE)]
-        high = [after[i, rows, :] for i in range(EDGE)]
+        far = [halo[i, rows, :] for i in range(EDGE)]
+        if not high:
+            far = far[::-1]
         for j in range(EDGE):
-            extra = COEFFS[3] * low[j]
+            extra = COEFFS[3] * far[j]
             for k in range(j + 1, 4):
-                extra = extra + COEFFS[k - 1] * low[EDGE + j - k]
-            next_lo[j, rows, :] = base_lo[j, rows, :] + model_lo[j, rows, :] * extra
+                extra = extra + COEFFS[k - 1] * far[EDGE + j - k]
+            at = EDGE - 1 - j if high else j
+            edge[at, rows, :] = base[at, rows, :] + model[at, rows, :] * extra
             if forward:
-                image_lo[j, rows, :] = part_lo[j, rows, :] + extra
-            extra = COEFFS[3] * high[j]
-            for k in range(EDGE - j, 4):
-                extra = extra + COEFFS[k - 1] * high[j + k - EDGE]
-            next_hi[j, rows, :] = base_hi[j, rows, :] + model_hi[j, rows, :] * extra
-            if forward:
-                image_hi[j, rows, :] = part_hi[j, rows, :] + extra
+                image[at, rows, :] = part[at, rows, :] + extra
         return carry
 
     lax.fori_loop(0, NY // CHUNK, body, 0)
-    if forward:
-        add_source(first_ref, source_ref, wavelet_ref, tick, next_lo, 0, EDGE)
-        add_source(first_ref, source_ref, wavelet_ref, tick, next_hi, ROWS - EDGE, EDGE)
+    low = ROWS - EDGE if high else 0
+    if forward:
+        add_source(first_ref, source_ref, wavelet_ref, tick, edge, low, EDGE)
     else:
-        add_residuals(first_ref, receivers_ref, lists_ref, res_ref, next_lo, 0, 0)
-        add_residuals(first_ref, receivers_ref, lists_ref, res_ref, next_hi, 2, ROWS - EDGE)
+        add_residuals(first_ref, receivers_ref, lists_ref, res_ref, edge, 2 if high else 0, low)
 
 
 def swap(value, axis, pairs):
@@ -301,13 +328,27 @@
 
 
 def on_device(model_slab, wave_prev, wave_now, adjoint_next, adjoint_now, wavelet, source_cell, receiver_cells, observed):
-    cut = lambda a: (a[:EDGE], a[EDGE : ROWS - EDGE], a[ROWS - EDGE :])
-    up = [(i, i + 1) for i in range(15)]
-    down = [(i + 1, i) for i in range(15)]
-    first = (lax.axis_index("dom") * (ROWS * NY * NZ)).astype(jnp.int32).reshape(1)
+    ends = [(i, i ^ 1) for i in range(16)]
+    starts = [(i, i + 1 if i % 2 else i - 1) for i in range(1, 15)]
+    place = lax.axis_index("dom")
+
+    first = jnp.stack([place * (ROWS * NY * NZ), place % 2]).astype(jnp.int32)
+
+    def cut(a):
+        return call(
+            cut_kernel,
+            [planes(EDGE), planes(MID), planes(EDGE)],
+            [],
+            [SMEM, VMEM],
+            [VMEM] * 3,
+            1000,
+            2 * ROWS * NY * NZ * 4,
+            "cut",
+        )(first, a)
+
     lists = call(
         sort_kernel,
-        jax.ShapeDtypeStruct((3, REC + 128), jnp.int32),
+        jax.ShapeDtypeStruct((4, REC + 128), jnp.int32),
         [],
         [SMEM, SMEM],
         SMEM,
@@ -316,51 +357,66 @@
         "sort_receivers",
     )(first, receiver_cells)
     observed = observed[0]
-    where = (first, receiver_cells, lists)
     model = cut(model_slab)
     pad = [pltpu.VMEM((ROWS + 2 * EDGE, NY + 16, NZ), jnp.float32)]
     res_shape = jax.ShapeDtypeStruct((REC, NZ), jnp.float32)
     own_cost = dict(flops=ROWS * NY * NZ * 60, nbytes=8 * ROWS * NY * NZ * 4)
-    edge_cost = dict(flops=2 * EDGE * NY * NZ * 10, nbytes=6 * EDGE * NY * NZ * 4)
-
-    def halos(cur):
-        return swap(cur[2], "dom", up), swap(cur[0], "dom", down)
+    edge_cost = dict(flops=EDGE * NY * NZ * 10, nbytes=6 * EDGE * NY * NZ * 4)
+    ANY = pl.BlockSpec(memory_space=pl.ANY)
+    source = (first, source_cell, wavelet)
+    taken = (first, receiver_cells, lists)
+
+    def edges(forward, tick, sent, bases, parts):
+        outs = [None, None]
+        done = bases[0]
+        for high in (True, False):
+            side = 2 if high else 0
+            smem = source if forward else taken
+            outs[high] = call(
+                functools.partial(edge_kernel, forward, tick, high),
+                [planes(EDGE)] * (2 if forward else 1),
+                [],
+                [SMEM] * 3 + [VMEM] * 4 + [ANY],
+                [VMEM] * (2 if forward else 1),
+                name="edge_high" if high else "edge_low",
+                **edge_cost,
+            )(*smem, sent[high], bases[high], model[side], parts[high], done)
+            done = outs[high][0]
+        return outs
+
+    def halos(cur, tick):
+        low = swap(cur[0], "dom", starts)
+        high = swap(cur[2], "dom", ends)
+        return low, high
 
     old, cur = cut(wave_prev[0]), cut(wave_now[0])
     images, residuals = [], []
     for tick in range(STEPS):
-        before, after = halos(cur)
+        sent = halos(cur, tick)
         extra = (observed,) if tick > 0 else ()
+        smem = ((first, receiver_cells, lists) if tick > 0 else (first,)) + (source_cell, wavelet) + extra
         outs = [planes(MID), planes(EDGE), planes(EDGE), planes(EDGE), planes(MID), planes(EDGE)]
         outs += [res_shape] if tick > 0 else []
         result = call(
             functools.partial(own_kernel, True, tick, False),
             outs,
             pad,
-            [SMEM] * (5 + len(extra)) + [VMEM] * 9,
+            [SMEM] * len(smem) + [VMEM] * 9,
             [VMEM] * len(outs),
             name="own_forward",
             **own_cost,
-        )(*where, source_cell, wavelet, *extra, *cur, *old, *model)
+        )(*smem, *cur, *old, *model)
         mid, base_lo, base_hi, part_lo, image_mid, part_hi = result[:6]
         if tick > 0:
             residuals.append(result[6])
-        low, high, image_lo, image_hi = call(
-            functools.partial(edge_kernel, True, tick),
-            [planes(EDGE)] * 4,
-            [],
-            [SMEM] * 5 + [VMEM] * 8,
-            [VMEM] * 4,
-            name="edge_forward",
-            **edge_cost,
-        )(*where, source_cell, wavelet, before, after, base_lo, base_hi, model[0], model[2], part_lo, part_hi)
+        (low, image_lo), (high, image_hi) = edges(True, tick, sent, (base_lo, base_hi), (part_lo, part_hi))
         images.append((image_lo, image_mid, image_hi))
         old, cur = cur, (low, mid, high)
     last = cur
     old, cur = cut(adjoint_next[0]), cut(adjoint_now[0])
     grad = None
     for tick in reversed(range(STEPS)):
-        before, after = halos(cur)
+        sent = halos(cur, tick)
         top = tick == STEPS - 1
         extra = (observed,) if top else ()
         fields = last if top else (residuals[tick], *images[tick + 1], grad)
@@ -375,22 +431,23 @@
             [VMEM] * len(outs),
             name="own_adjoint",
             **own_cost,
-        )(*where, *extra, *cur, *old, *model, *fields)
+        )(*taken, *extra, *cur, *old, *model, *fields)
         mid, base_lo, base_hi = result[:3]
         if top:
             residuals.append(result[3])
         grad = result[-1]
-        low, high = call(
-            functools.partial(edge_kernel, False, tick),
-            [planes(EDGE)] * 2,
-            [],
-            [SMEM] * 3 + [VMEM] * 7,
-            [VMEM] * 2,
-            name="edge_adjoint",
-            **edge_cost,
-        )(*where, before, after, base_lo, base_hi, model[0], model[2], residuals[tick])
+        (low,), (high,) = edges(False, tick, sent, (base_lo, base_hi), (residuals[tick],) * 2)
         old, cur = cur, (low, mid, high)
-    grad = grad + jnp.concatenate([a * b for a, b in zip(cur, images[0])])
+    grad = call(
+        join_kernel,
+        planes(ROWS),
+        [],
+        [SMEM] + [VMEM] * 7,
+        VMEM,
+        2 * ROWS * NY * NZ,
+        4 * ROWS * NY * NZ * 4,
+        "join",
+    )(first, grad, *cur, *images[0])
     total = shot_sum(grad)
     peak = dom_max(jnp.max(jnp.abs(total)))
     direction = total / (peak + EPSILON)

time: 314 us -> 295 us (0.939)
  waiting for transfers between devices: 105 us -> 43.2 us
  starting transfers between devices: 94.5 us -> 128 us
  Pallas kernels: 94 us -> 106 us
    ppermute x47, waiting for transfers between devices: 105 us -> 43.2 us  [swap(): return lax.ppermute(value, axis, pairs)]
    ppermute x47, starting transfers between devices: 94.5 us -> 128 us  [swap(): return lax.ppermute(value, axis, pairs)]
    pallas_call x17 -> x39, Pallas kernels: 22.1 us -> 34.5 us  [the longest x32 23.7 us: edges(): call(functools.partial(edge_kernel, forward, tick, high), [planes(EDGE)]...]
    unnamed x42 -> x48, local copies, waits for them, and re-layouts: 6.06 us -> 9.02 us
  transfers between devices with their start and end apart: 47 -> 47, of which waited for: 25 -> 20; matrix products, arithmetic and copies ran while one was open for 0% -> 0% of each run, Pallas kernels for 26% -> 35%
where the time goes in v2:
time: 295 us; the launch traced here: 293 us
  starting transfers between devices  128 us (43%)
  Pallas kernels  106 us (36%)
  waiting for transfers between devices  43.2 us (15%)
  local copies, waits for them, and re-layouts  10.3 us (3%)
  other arithmetic  3.16 us (1%)
  between operations  2.97 us (1%)
    ppermute x47, starting transfers between devices, swap(): return lax.ppermute(value, axis, pairs)  128 us
    ppermute x47, waiting for transfers between devices, swap(): return lax.ppermute(value, axis, pairs)  43.2 us
    pallas_call x8, Pallas kernels, on_device(): call(functools.partial(own_kernel, True, tick, False), outs, pad, [SMEM]...  35.7 us
    pallas_call x8, Pallas kernels, on_device(): call(functools.partial(own_kernel, False, tick, not top), outs, pad, [SME...  35.5 us
    pallas_call x32, Pallas kernels, edges(): call(functools.partial(edge_kernel, forward, tick, high), [planes(EDGE)]...  23.7 us
    unnamed x48, local copies, waits for them, and re-layouts  9.02 us
    pallas_call x1, Pallas kernels, on_device(): call(sort_kernel, jax.ShapeDtypeStruct((4, REC + 128), jnp.int32), [], [S...  6.46 us
  transfers between devices with their start and end apart: 47, of which 20 were waited for; matrix products, arithmetic and copies ran while one was open for 0% of the time, Pallas kernels for 35%

profile of v2, /device:TPU:0, one launch (start us, length us, event | category | flops | bytes accessed | tf_op | source)
XLA Modules:
  0.0 293.2 jit_solution(13678293226393412170)
XLA Ops:
  0.7 1.3 copy-done.3
  6.5 4.1 %own_forward.8 = (f32[8,128,128]{2,1,0:T(8,128)S(1)}, f32[4,128,128]{2,1,0:T(8,128)S(1)}, f32[4,128,128]{2,1,0:T(8,128)S(1)}, f32[4,128,128]{2,1,0:T(8,128)S(1)}...) custom-call(s32[2]{0:T(128)S(1)} %pad_add_fusion.first_ref.refs_0_, s32[1]{0:T(128)S(6)} %copy.15.refs_1_.refs_3_, ...), custom_call_target="tpu_custom_call" | custom-call | flops 15728640 | bytes 8388608 | tf_op jit(solution)/shard_map/own_forward/pallas_call | solution.py:400
  12.1 5.1 %collective-permute-start.4 = (f32[4,128,128]{2,1,0:T(8,128)S(1)}, f32[4,128,128]{2,1,0:T(8,128)S(1)}, u32[]{:S(2)}, u32[]{:S(2)}) collective-permute-start(f32[4,128,128]{2,1,0:T(8,128)S(1)} %get-tuple-element.156.refs_7_.refs_8_.refs_11_), channel_id=1, source_target_pairs={{0,1},{1,0},{2,3},{3,2},{4,5},{5,4},{6,7},{7,6},{8,9},{9,8},{10,11... | collective-permute-start | bytes 786440 | tf_op jit(solution)/shard_map/ppermute | solution.py:285
  18.6 6.5 %sort_receivers.1.refs_2_ = s32[4,384]{1,0:T(4,128)S(1)} custom-call(s32[2]{0:T(128)S(1)} %pad_add_fusion.first_ref.refs_0_, s32[1,256]{1,0:T(1,128)S(1)} %copy-done.7), custom_call_target="tpu_custom_call" | custom-call | flops 1000 | bytes 4096 | tf_op jit(solution)/shard_map/sort_receivers/pallas_call | solution.py:349
  25.1 4.5 %own_forward.9 = (f32[8,128,128]{2,1,0:T(8,128)S(1)}, f32[4,128,128]{2,1,0:T(8,128)S(1)}, f32[4,128,128]{2,1,0:T(8,128)S(1)}, f32[4,128,128]{2,1,0:T(8,128)S(1)}...) custom-call(s32[2]{0:T(128)S(1)} %pad_add_fusion.first_ref.refs_0_, ...), custom_call_target="tpu_custom_call" | custom-call | flops 15728640 | bytes 8388608 | tf_op jit(solution)/shard_map/own_forward/pallas_call | solution.py:400
  30.5 4.5 %collective-permute-start.6 = (f32[4,128,128]{2,1,0:T(8,128)S(1)}, f32[4,128,128]{2,1,0:T(8,128)S(1)}, u32[]{:S(2)}, u32[]{:S(2)}) collective-permute-start(f32[4,128,128]{2,1,0:T(8,128)S(1)} %get-tuple-element.163.refs_7_.refs_8_.refs_11_), channel_id=1, source_target_pairs={{0,1},{1,0},{2,3},{3,2},{4,5},{5,4},{6,7},{7,6},{8,9},{9,8},{10,11... | collective-permute-start | bytes 786440 | tf_op jit(solution)/shard_map/ppermute | solution.py:285
  36.4 4.5 %own_forward.10 = (f32[8,128,128]{2,1,0:T(8,128)S(1)}, f32[4,128,128]{2,1,0:T(8,128)S(1)}, f32[4,128,128]{2,1,0:T(8,128)S(1)}, f32[4,128,128]{2,1,0:T(8,128)S(1)...) custom-call(s32[2]{0:T(128)S(1)} %pad_add_fusion.first_ref.refs_0_, ...), custom_call_target="tpu_custom_call" | custom-call | flops 15728640 | bytes 8388608 | tf_op jit(solution)/shard_map/own_forward/pallas_call | solution.py:400
  41.6 4.7 %collective-permute-start.8 = (f32[4,128,128]{2,1,0:T(8,128)S(1)}, f32[4,128,128]{2,1,0:T(8,128)S(1)}, u32[]{:S(2)}, u32[]{:S(2)}) collective-permute-start(f32[4,128,128]{2,1,0:T(8,128)S(1)} %get-tuple-element.170.refs_7_.refs_8_.refs_11_), channel_id=1, source_target_pairs={{0,1},{1,0},{2,3},{3,2},{4,5},{5,4},{6,7},{7,6},{8,9},{9,8},{10,11... | collective-permute-start | bytes 786440 | tf_op jit(solution)/shard_map/ppermute | solution.py:285
  47.6 4.5 %own_forward.11 = (f32[8,128,128]{2,1,0:T(8,128)S(1)}, f32[4,128,128]{2,1,0:T(8,128)S(1)}, f32[4,128,128]{2,1,0:T(8,128)S(1)}, f32[4,128,128]{2,1,0:T(8,128)S(1)...) custom-call(s32[2]{0:T(128)S(1)} %pad_add_fusion.first_ref.refs_0_, ...), custom_call_target="tpu_custom_call" | custom-call | flops 15728640 | bytes 8388608 | tf_op jit(solution)/shard_map/own_forward/pallas_call | solution.py:400
  52.1 2.5 collective-permute-done.8.refs_3_
  55.2 4.2 %collective-permute-start.10 = (f32[4,128,128]{2,1,0:T(8,128)S(1)}, f32[4,128,128]{2,1,0:T(8,128)S(1)}, u32[]{:S(2)}, u32[]{:S(2)}) collective-permute-start(f32[4,128,128]{2,1,0:T(8,128)S(1)} %get-tuple-element.177.refs_7_.refs_8_.refs_11_), channel_id=1, source_target_pairs={{0,1},{1,0},{2,3},{3,2},{4,5},{5,4},{6,7},{7,6},{8,9},{9,8},{10,11... | collective-permute-start | bytes 786440 | tf_op jit(solution)/shard_map/ppermute | solution.py:285
  60.8 4.5 %own_forward.12 = (f32[8,128,128]{2,1,0:T(8,128)S(1)}, f32[4,128,128]{2,1,0:T(8,128)S(1)}, f32[4,128,128]{2,1,0:T(8,128)S(1)}, f32[4,128,128]{2,1,0:T(8,128)S(1)...) custom-call(s32[2]{0:T(128)S(1)} %pad_add_fusion.first_ref.refs_0_, ...), custom_call_target="tpu_custom_call" | custom-call | flops 15728640 | bytes 8388608 | tf_op jit(solution)/shard_map/own_forward/pallas_call | solution.py:400
  65.3 1.6 collective-permute-done.10.refs_3_
  67.5 4.2 %collective-permute-start.12 = (f32[4,128,128]{2,1,0:T(8,128)S(1)}, f32[4,128,128]{2,1,0:T(8,128)S(1)}, u32[]{:S(2)}, u32[]{:S(2)}) collective-permute-start(f32[4,128,128]{2,1,0:T(8,128)S(1)} %get-tuple-element.184.refs_7_.refs_8_.refs_11_), channel_id=1, source_target_pairs={{0,1},{1,0},{2,3},{3,2},{4,5},{5,4},{6,7},{7,6},{8,9},{9,8},{10,11... | collective-permute-start | bytes 786440 | tf_op jit(solution)/shard_map/ppermute | solution.py:285
  73.0 4.5 %own_forward.13 = (f32[8,128,128]{2,1,0:T(8,128)S(1)}, f32[4,128,128]{2,1,0:T(8,128)S(1)}, f32[4,128,128]{2,1,0:T(8,128)S(1)}, f32[4,128,128]{2,1,0:T(8,128)S(1)...) custom-call(s32[2]{0:T(128)S(1)} %pad_add_fusion.first_ref.refs_0_, ...), custom_call_target="tpu_custom_call" | custom-call | flops 15728640 | bytes 8388608 | tf_op jit(solution)/shard_map/own_forward/pallas_call | solution.py:400
  79.1 6.1 %collective-permute-start.14 = (f32[4,128,128]{2,1,0:T(8,128)S(1)}, f32[4,128,128]{2,1,0:T(8,128)S(1)}, u32[]{:S(2)}, u32[]{:S(2)}) collective-permute-start(f32[4,128,128]{2,1,0:T(8,128)S(1)} %get-tuple-element.191.refs_7_.refs_8_.refs_11_), channel_id=1, source_target_pairs={{0,1},{1,0},{2,3},{3,2},{4,5},{5,4},{6,7},{7,6},{8,9},{9,8},{10,11... | collective-permute-start | bytes 786440 | tf_op jit(solution)/shard_map/ppermute | solution.py:285
  86.5 4.5 %own_forward.14 = (f32[8,128,128]{2,1,0:T(8,128)S(1)}, f32[4,128,128]{2,1,0:T(8,128)S(1)}, f32[4,128,128]{2,1,0:T(8,128)S(1)}, f32[4,128,128]{2,1,0:T(8,128)S(1)...) custom-call(s32[2]{0:T(128)S(1)} %pad_add_fusion.first_ref.refs_0_, ...), custom_call_target="tpu_custom_call" | custom-call | flops 15728640 | bytes 8388608 | tf_op jit(solution)/shard_map/own_forward/pallas_call | solution.py:400
  92.0 6.5 %collective-permute-start.16 = (f32[4,128,128]{2,1,0:T(8,128)S(1)}, f32[4,128,128]{2,1,0:T(8,128)S(1)}, u32[]{:S(2)}, u32[]{:S(2)}) collective-permute-start(f32[4,128,128]{2,1,0:T(8,128)S(1)} %get-tuple-element.198.refs_7_.refs_8_), channel_id=1, source_target_pairs={{0,1},{1,0},{2,3},{3,2},{4,5},{5,4},{6,7},{7,6},{8,9},{9,8},{10,11... | collective-permute-start | bytes 786440 | tf_op jit(solution)/shard_map/ppermute | solution.py:285
  100.6 6.6 %collective-permute-start.17 = (f32[4,128,128]{2,1,0:T(8,128)S(1)}, f32[4,128,128]{2,1,0:T(8,128)S(1)}, u32[]{:S(2)}, u32[]{:S(2)}) collective-permute-start(f32[4,128,128]{2,1,0:T(8,128)S(1)} %get-tuple-element.139.refs_6_.refs_8_), channel_id=1, source_target_pairs={{0,1},{1,0},{2,3},{3,2},{4,5},{5,4},{6,7},{7,6},{8,9},{9,8},{10,11... | collective-permute-start | bytes 786440 | tf_op jit(solution)/shard_map/ppermute | solution.py:285
  108.8 4.5 %own_forward.15 = (f32[8,128,128]{2,1,0:T(8,128)S(1)}, f32[4,128,128]{2,1,0:T(8,128)S(1)}, f32[4,128,128]{2,1,0:T(8,128)S(1)}, f32[4,128,128]{2,1,0:T(8,128)S(1)...) custom-call(s32[2]{0:T(128)S(1)} %pad_add_fusion.first_ref.refs_0_, ...), custom_call_target="tpu_custom_call" | custom-call | flops 15728640 | bytes 8388608 | tf_op jit(solution)/shard_map/own_forward/pallas_call | solution.py:400
  114.6 4.6 %own_adjoint.8 = (f32[8,128,128]{2,1,0:T(8,128)S(1)}, f32[4,128,128]{2,1,0:T(8,128)S(1)}, f32[4,128,128]{2,1,0:T(8,128)S(1)}, f32[256,128]{1,0:T(8,128)S(1)}, f32[16,128,128]{2,1,0:T(8,128)S(1)}) custom-call(s32[2]{0:T(128)S(1)} %pad_add_fusion.first_ref.refs_0_, s32[1,256]{1,0:T(1,128)S(1)} %copy-done.7, s32[4,384]{1,0:T(4,128)S(1)} %sort_receivers.1.refs_2_, ...), custom_call_target="tpu_custom_call" | custom-call | flops 15728640 | bytes 8388608 | tf_op jit(solution)/shard_map/own_adjoint/pallas_call | solution.py:426
  120.0 7.9 %collective-permute-start.19 = (f32[4,128,128]{2,1,0:T(8,128)S(1)}, f32[4,128,128]{2,1,0:T(8,128)S(1)}, u32[]{:S(2)}, u32[]{:S(2)}) collective-permute-start(f32[4,128,128]{2,1,0:T(8,128)S(1)} %edge_high.24.refs_7_.refs_5_.refs_8_), channel_id=1, source_target_pairs={{0,1},{1,0},{2,3},{3,2},{4,5},{5,4},{6,7},{7,6},{8,9},{9,8},{10,11... | collective-permute-start | bytes 786440 | tf_op jit(solution)/shard_map/ppermute | solution.py:285
  129.4 4.4 %own_adjoint.9 = (f32[8,128,128]{2,1,0:T(8,128)S(1)}, f32[4,128,128]{2,1,0:T(8,128)S(1)}, f32[4,128,128]{2,1,0:T(8,128)S(1)}, f32[16,128,128]{2,1,0:T(8,128)S(1)}) custom-call(s32[2]{0:T(128)S(1)} %pad_add_fusion.first_ref.refs_0_, s32[1,256]{1,0:T(1,128)S(1)} %copy-done.7, s32[4,384]{1,0:T(4,128)S(1)} %sort_receivers.1.refs_2_, ...), custom_call_target="tpu_custom_call" | custom-call | flops 15728640 | bytes 8388608 | tf_op jit(solution)/shard_map/own_adjoint/pallas_call | solution.py:426
  134.5 5.9 %collective-permute-start.21 = (f32[4,128,128]{2,1,0:T(8,128)S(1)}, f32[4,128,128]{2,1,0:T(8,128)S(1)}, u32[]{:S(2)}, u32[]{:S(2)}) collective-permute-start(f32[4,128,128]{2,1,0:T(8,128)S(1)} %edge_high.25.refs_7_.refs_5_.refs_8_), channel_id=1, source_target_pairs={{0,1},{1,0},{2,3},{3,2},{4,5},{5,4},{6,7},{7,6},{8,9},{9,8},{10,11... | collective-permute-start | bytes 786440 | tf_op jit(solution)/shard_map/ppermute | solution.py:285
  141.9 4.4 %own_adjoint.10 = (f32[8,128,128]{2,1,0:T(8,128)S(1)}, f32[4,128,128]{2,1,0:T(8,128)S(1)}, f32[4,128,128]{2,1,0:T(8,128)S(1)}, f32[16,128,128]{2,1,0:T(8,128)S(1)}) custom-call(s32[2]{0:T(128)S(1)} %pad_add_fusion.first_ref.refs_0_, s32[1,256]{1,0:T(1,128)S(1)} %copy-done.7, s32[4,384]{1,0:T(4,128)S(1)} %sort_receivers.1.refs_2_, ...), custom_call_target="tpu_custom_call" | custom-call | flops 15728640 | bytes 8388608 | tf_op jit(solution)/shard_map/own_adjoint/pallas_call | solution.py:426
  146.3 3.2 %collective-permute-done.21.refs_3_ = f32[4,128,128]{2,1,0:T(8,128)S(1)} collective-permute-done((f32[4,128,128]{2,1,0:T(8,128)S(1)}, f32[4,128,128]{2,1,0:T(8,128)S(1)}, u32[]{:S(2)}, u32[]{:S(2)}) %collective-permute-start.21) | collective-permute-done | bytes 262176 | tf_op jit(solution)/shard_map/ppermute | solution.py:285
  150.2 3.8 %collective-permute-start.23 = (f32[4,128,128]{2,1,0:T(8,128)S(1)}, f32[4,128,128]{2,1,0:T(8,128)S(1)}, u32[]{:S(2)}, u32[]{:S(2)}) collective-permute-start(f32[4,128,128]{2,1,0:T(8,128)S(1)} %edge_high.26.refs_7_.refs_5_.refs_8_), channel_id=1, source_target_pairs={{0,1},{1,0},{2,3},{3,2},{4,5},{5,4},{6,7},{7,6},{8,9},{9,8},{10,11... | collective-permute-start | bytes 786440 | tf_op jit(solution)/shard_map/ppermute | solution.py:285
  155.5 4.4 %own_adjoint.11 = (f32[8,128,128]{2,1,0:T(8,128)S(1)}, f32[4,128,128]{2,1,0:T(8,128)S(1)}, f32[4,128,128]{2,1,0:T(8,128)S(1)}, f32[16,128,128]{2,1,0:T(8,128)S(1)}) custom-call(s32[2]{0:T(128)S(1)} %pad_add_fusion.first_ref.refs_0_, s32[1,256]{1,0:T(1,128)S(1)} %copy-done.7, s32[4,384]{1,0:T(4,128)S(1)} %sort_receivers.1.refs_2_, ...), custom_call_target="tpu_custom_call" | custom-call | flops 15728640 | bytes 8388608 | tf_op jit(solution)/shard_map/own_adjoint/pallas_call | solution.py:426
  159.8 2.3 collective-permute-done.23.refs_3_
  162.9 5.0 %collective-permute-start.25 = (f32[4,128,128]{2,1,0:T(8,128)S(1)}, f32[4,128,128]{2,1,0:T(8,128)S(1)}, u32[]{:S(2)}, u32[]{:S(2)}) collective-permute-start(f32[4,128,128]{2,1,0:T(8,128)S(1)} %edge_high.27.refs_7_.refs_5_.refs_8_), channel_id=1, source_target_pairs={{0,1},{1,0},{2,3},{3,2},{4,5},{5,4},{6,7},{7,6},{8,9},{9,8},{10,11... | collective-permute-start | bytes 786440 | tf_op jit(solution)/shard_map/ppermute | solution.py:285
  169.4 4.4 %own_adjoint.12 = (f32[8,128,128]{2,1,0:T(8,128)S(1)}, f32[4,128,128]{2,1,0:T(8,128)S(1)}, f32[4,128,128]{2,1,0:T(8,128)S(1)}, f32[16,128,128]{2,1,0:T(8,128)S(1)}) custom-call(s32[2]{0:T(128)S(1)} %pad_add_fusion.first_ref.refs_0_, s32[1,256]{1,0:T(1,128)S(1)} %copy-done.7, s32[4,384]{1,0:T(4,128)S(1)} %sort_receivers.1.refs_2_, ...), custom_call_target="tpu_custom_call" | custom-call | flops 15728640 | bytes 8388608 | tf_op jit(solution)/shard_map/own_adjoint/pallas_call | solution.py:426
  173.7 3.1 %collective-permute-done.25.refs_3_ = f32[4,128,128]{2,1,0:T(8,128)S(1)} collective-permute-done((f32[4,128,128]{2,1,0:T(8,128)S(1)}, f32[4,128,128]{2,1,0:T(8,128)S(1)}, u32[]{:S(2)}, u32[]{:S(2)}) %collective-permute-start.25) | collective-permute-done | bytes 262176 | tf_op jit(solution)/shard_map/ppermute | solution.py:285
  177.6 5.0 %collective-permute-start.27 = (f32[4,128,128]{2,1,0:T(8,128)S(1)}, f32[4,128,128]{2,1,0:T(8,128)S(1)}, u32[]{:S(2)}, u32[]{:S(2)}) collective-permute-start(f32[4,128,128]{2,1,0:T(8,128)S(1)} %edge_high.28.refs_7_.refs_5_.refs_8_), channel_id=1, source_target_pairs={{0,1},{1,0},{2,3},{3,2},{4,5},{5,4},{6,7},{7,6},{8,9},{9,8},{10,11... | collective-permute-start | bytes 786440 | tf_op jit(solution)/shard_map/ppermute | solution.py:285
  184.1 4.4 %own_adjoint.13 = (f32[8,128,128]{2,1,0:T(8,128)S(1)}, f32[4,128,128]{2,1,0:T(8,128)S(1)}, f32[4,128,128]{2,1,0:T(8,128)S(1)}, f32[16,128,128]{2,1,0:T(8,128)S(1)}) custom-call(s32[2]{0:T(128)S(1)} %pad_add_fusion.first_ref.refs_0_, s32[1,256]{1,0:T(1,128)S(1)} %copy-done.7, s32[4,384]{1,0:T(4,128)S(1)} %sort_receivers.1.refs_2_, ...), custom_call_target="tpu_custom_call" | custom-call | flops 15728640 | bytes 8388608 | tf_op jit(solution)/shard_map/own_adjoint/pallas_call | solution.py:426
  188.5 2.4 collective-permute-done.27.refs_3_
  191.6 5.1 %collective-permute-start.29 = (f32[4,128,128]{2,1,0:T(8,128)S(1)}, f32[4,128,128]{2,1,0:T(8,128)S(1)}, u32[]{:S(2)}, u32[]{:S(2)}) collective-permute-start(f32[4,128,128]{2,1,0:T(8,128)S(1)} %edge_high.29.refs_7_.refs_5_.refs_8_), channel_id=1, source_target_pairs={{0,1},{1,0},{2,3},{3,2},{4,5},{5,4},{6,7},{7,6},{8,9},{9,8},{10,11... | collective-permute-start | bytes 786440 | tf_op jit(solution)/shard_map/ppermute | solution.py:285
  198.2 4.4 %own_adjoint.14 = (f32[8,128,128]{2,1,0:T(8,128)S(1)}, f32[4,128,128]{2,1,0:T(8,128)S(1)}, f32[4,128,128]{2,1,0:T(8,128)S(1)}, f32[16,128,128]{2,1,0:T(8,128)S(1)}) custom-call(s32[2]{0:T(128)S(1)} %pad_add_fusion.first_ref.refs_0_, s32[1,256]{1,0:T(1,128)S(1)} %copy-done.7, s32[4,384]{1,0:T(4,128)S(1)} %sort_receivers.1.refs_2_, ...), custom_call_target="tpu_custom_call" | custom-call | flops 15728640 | bytes 8388608 | tf_op jit(solution)/shard_map/own_adjoint/pallas_call | solution.py:426
  203.3 2.2 collective-permute-done.29.refs_3_
  206.3 5.8 %collective-permute-start.31 = (f32[4,128,128]{2,1,0:T(8,128)S(1)}, f32[4,128,128]{2,1,0:T(8,128)}, u32[]{:S(2)}, u32[]{:S(2)}) collective-permute-start(f32[4,128,128]{2,1,0:T(8,128)S(1)} %edge_high.30.refs_7_.refs_5_), channel_id=1, source_target_pairs={{0,1},{1,0},{2,3},{3,2},{4,5},{5,4},{6,7},{7,6},{8,9},{9,8},{10,11... | collective-permute-start | bytes 786440 | tf_op jit(solution)/shard_map/ppermute | solution.py:285
  212.1 1.5 edge_low.30.refs_3_
  213.6 1.3 collective-permute-start.30
  214.9 1.2 copy-done.2
  220.1 4.7 %own_adjoint.15 = (f32[8,128,128]{2,1,0:T(8,128)S(1)}, f32[4,128,128]{2,1,0:T(8,128)S(1)}, f32[4,128,128]{2,1,0:T(8,128)S(1)}, f32[16,128,128]{2,1,0:T(8,128)S(1)}) custom-call(s32[2]{0:T(128)S(1)} %pad_add_fusion.first_ref.refs_0_, s32[1,256]{1,0:T(1,128)S(1)} %copy-done.7, s32[4,384]{1,0:T(4,128)S(1)} %sort_receivers.1.refs_2_, ...), custom_call_target="tpu_custom_call" | custom-call | flops 15728640 | bytes 8388608 | tf_op jit(solution)/shard_map/own_adjoint/pallas_call | solution.py:426
  228.2 1.8 collective-permute-done.32
  230.1 4.5 %collective-permute-start.33 = (f32[2,128,128]{2,1,0:T(8,128)S(1)}, f32[2,128,128]{2,1,0:T(8,128)S(1)}, u32[]{:S(2)}, u32[]{:S(2)}) collective-permute-start(f32[2,128,128]{2,1,0:T(8,128)S(1)} %get-tuple-element.278), channel_id=1, source_target_pairs={{0,32},{16,48},{32,64},{48,80},{64,96},{80,112},{96,0},{112,16},{1... | collective-permute-start | bytes 393224 | tf_op jit(solution)/shard_map/ppermute | solution.py:285
  234.6 2.7 collective-permute-start.34
  237.4 2.3 collective-permute-done.33
  239.6 4.0 %collective-permute-done.34 = f32[2,128,128]{2,1,0:T(8,128)S(1)} collective-permute-done((f32[2,128,128]{2,1,0:T(8,128)S(1)}, f32[2,128,128]{2,1,0:T(8,128)S(1)}, u32[]{:S(2)}, u32[]{:S(2)}) %collective-permute-start.34) | collective-permute-done | bytes 131104 | tf_op jit(solution)/shard_map/ppermute | solution.py:285
  243.6 4.2 %collective-permute-start.36 = (f32[2,128,128]{2,1,0:T(8,128)S(1)}, f32[2,128,128]{2,1,0:T(8,128)S(1)}, u32[]{:S(2)}, u32[]{:S(2)}) collective-permute-start(f32[2,128,128]{2,1,0:T(8,128)S(1)} %add_add_fusion), channel_id=1, source_target_pairs={{0,128},{16,144},{32,160},{48,176},{64,192},{80,208},{96,224},{112... | collective-permute-start | bytes 393224 | tf_op jit(solution)/shard_map/ppermute | solution.py:285
  247.8 4.8 %collective-permute-done.36 = f32[2,128,128]{2,1,0:T(8,128)S(1)} collective-permute-done((f32[2,128,128]{2,1,0:T(8,128)S(1)}, f32[2,128,128]{2,1,0:T(8,128)S(1)}, u32[]{:S(2)}, u32[]{:S(2)}) %collective-permute-start.36) | collective-permute-done | bytes 131104 | tf_op jit(solution)/shard_map/ppermute | solution.py:285
  252.7 1.5 collective-permute-start.37
  254.1 2.7 collective-permute-start.38
  257.1 3.2 %collective-permute-done.37 = f32[2,128,128]{2,1,0:T(8,128)S(1)} collective-permute-done((f32[2,128,128]{2,1,0:T(8,128)S(1)}, f32[2,128,128]{2,1,0:T(8,128)S(1)}, u32[]{:S(2)}, u32[]{:S(2)}) %collective-permute-start.37) | collective-permute-done | bytes 131104 | tf_op jit(solution)/shard_map/ppermute | solution.py:285
  260.3 1.9 collective-permute-done.38
  262.4 1.9 collective-permute-done.40
  265.7 4.2 %collective-permute-start.41 = (f32[8,128]{1,0:T(8,128)S(1)}, f32[8,128]{1,0:T(8,128)S(1)}, u32[]{:S(2)}, u32[]{:S(2)}) collective-permute-start(f32[8,128]{1,0:T(8,128)S(1)} %broadcast_in_dim.7), channel_id=1, source_target_pairs={{0,4},{1,5},{2,6},{3,7},{4,8},{5,9},{6,10},{7,11},{8,12},{9,13},{1... | collective-permute-start | bytes 12296 | tf_op jit(solution)/shard_map/ppermute | solution.py:285
  269.9 5.9 %collective-permute-start.42 = (f32[8,128]{1,0:T(8,128)S(1)}, f32[8,128]{1,0:T(8,128)S(1)}, u32[]{:S(2)}, u32[]{:S(2)}) collective-permute-start(f32[8,128]{1,0:T(8,128)S(1)} %broadcast_in_dim.7), channel_id=1, source_target_pairs={{0,8},{1,9},{2,10},{3,11},{4,12},{5,13},{6,14},{7,15},{8,0},{9,1},... | collective-permute-start | bytes 12296 | tf_op jit(solution)/shard_map/ppermute | solution.py:285
  276.0 1.5 collective-permute-done.42
  277.5 2.0 collective-permute-done.43
  280.1 4.7 %collective-permute-start.44 = (f32[8,128]{1,0:T(8,128)S(1)}, f32[8,128]{1,0:T(8,128)S(1)}, u32[]{:S(2)}, u32[]{:S(2)}) collective-permute-start(f32[8,128]{1,0:T(8,128)S(1)} %maximum_maximum_fusion.1), channel_id=1, source_target_pairs={{0,1},{1,2},{2,3},{3,0},{4,5},{5,6},{6,7},{7,4},{8,9},{9,10},{10,1... | collective-permute-start | bytes 12296 | tf_op jit(solution)/shard_map/ppermute | solution.py:285
  284.8 1.5 collective-permute-start.45
  286.3 2.8 collective-permute-start.46
  289.3 1.2 collective-permute-done.46
  291.6 1.5 subtract_multiply_fusion
  (150 shorter events, 48.9 us)
Async XLA Ops:
  0.6 3.1 %copy-start = (f32[16,128,128]{2,1,0:T(8,128)S(1)}, f32[16,128,128]{2,1,0:T(8,128)}, u32[]{:S(2)}) copy-start(f32[16,128,128]{2,1,0:T(8,128)} %whole_ref.1) | copy-start | bytes 3145732
  0.7 1.3 copy-start.3
  2.0 2.4 copy-start.4
  2.7 7.8 %collective-permute-start.2 = (f32[4,128,128]{2,1,0:T(8,128)S(1)}, f32[4,128,128]{2,1,0:T(8,128)S(1)}, u32[]{:S(2)}, u32[]{:S(2)}) collective-permute-start(f32[4,128,128]{2,1,0:T(8,128)S(1)} %get-tuple-element.148.refs_5_.refs_11_), channel_id=1, source_target_pairs={{0,1},{1,0},{2,3},{3,2},{4,5},{5,4},{6,7},{7,6},{8,9},{9,8},{10,11... | collective-permute-start | bytes 786440 | tf_op jit(solution)/shard_map/ppermute | solution.py:285
  3.0 14.1 %collective-permute-start.1 = (f32[4,128,128]{2,1,0:T(8,128)S(1)}, f32[4,128,128]{2,1,0:T(8,128)S(1)}, u32[]{:S(2)}, u32[]{:S(2)}) collective-permute-start(f32[4,128,128]{2,1,0:T(8,128)S(1)} %get-tuple-element.146.refs_3_.refs_9_), channel_id=1, source_target_pairs={{1,2},{2,1},{3,4},{4,3},{5,6},{6,5},{7,8},{8,7},{9,10},{10,9},{11,... | collective-permute-start | bytes 786440 | tf_op jit(solution)/shard_map/ppermute | solution.py:285
  12.1 17.6 %collective-permute-start.4 = (f32[4,128,128]{2,1,0:T(8,128)S(1)}, f32[4,128,128]{2,1,0:T(8,128)S(1)}, u32[]{:S(2)}, u32[]{:S(2)}) collective-permute-start(f32[4,128,128]{2,1,0:T(8,128)S(1)} %get-tuple-element.156.refs_7_.refs_8_.refs_11_), channel_id=1, source_target_pairs={{0,1},{1,0},{2,3},{3,2},{4,5},{5,4},{6,7},{7,6},{8,9},{9,8},{10,11... | collective-permute-start | bytes 786440 | tf_op jit(solution)/shard_map/ppermute | solution.py:285
  17.8 11.9 %copy-start.18 = (f32[4,128,128]{2,1,0:T(8,128)}, f32[4,128,128]{2,1,0:T(8,128)S(1)}, u32[]{:S(2)}) copy-start(f32[4,128,128]{2,1,0:T(8,128)S(1)} %get-tuple-element.269.b_low) | copy-start | bytes 786436
  17.8 7.3 %copy-start.8 = (f32[1,8,256]{2,1,0:T(8,128)S(1)}, f32[1,8,256]{2,1,0:T(8,128)}, u32[]{:S(2)}) copy-start(f32[1,8,256]{2,1,0:T(8,128)} %param.17) | copy-start | bytes 24580
  17.8 17.2 %collective-permute-start.3 = (f32[4,128,128]{2,1,0:T(8,128)S(1)}, f32[4,128,128]{2,1,0:T(8,128)S(1)}, u32[]{:S(2)}, u32[]{:S(2)}) collective-permute-start(f32[4,128,128]{2,1,0:T(8,128)S(1)} %get-tuple-element.157.refs_6_.refs_9_), channel_id=1, source_target_pairs={{1,2},{2,1},{3,4},{4,3},{5,6},{6,5},{7,8},{8,7},{9,10},{10,9},{11,... | collective-permute-start | bytes 786440 | tf_op jit(solution)/shard_map/ppermute | solution.py:285
  30.5 5.2 %copy-start.20 = (f32[4,128,128]{2,1,0:T(8,128)}, f32[4,128,128]{2,1,0:T(8,128)S(1)}, u32[]{:S(2)}) copy-start(f32[4,128,128]{2,1,0:T(8,128)S(1)} %get-tuple-element.263.refs_15_) | copy-start | bytes 786436
  30.5 10.4 %collective-permute-start.6 = (f32[4,128,128]{2,1,0:T(8,128)S(1)}, f32[4,128,128]{2,1,0:T(8,128)S(1)}, u32[]{:S(2)}, u32[]{:S(2)}) collective-permute-start(f32[4,128,128]{2,1,0:T(8,128)S(1)} %get-tuple-element.163.refs_7_.refs_8_.refs_11_), channel_id=1, source_target_pairs={{0,1},{1,0},{2,3},{3,2},{4,5},{5,4},{6,7},{7,6},{8,9},{9,8},{10,11... | collective-permute-start | bytes 786440 | tf_op jit(solution)/shard_map/ppermute | solution.py:285
  35.7 5.2 %copy-start.22 = (f32[4,128,128]{2,1,0:T(8,128)}, f32[4,128,128]{2,1,0:T(8,128)S(1)}, u32[]{:S(2)}) copy-start(f32[4,128,128]{2,1,0:T(8,128)S(1)} %get-tuple-element.261.refs_13_) | copy-start | bytes 786436
  35.7 10.5 %collective-permute-start.5 = (f32[4,128,128]{2,1,0:T(8,128)S(1)}, f32[4,128,128]{2,1,0:T(8,128)S(1)}, u32[]{:S(2)}, u32[]{:S(2)}) collective-permute-start(f32[4,128,128]{2,1,0:T(8,128)S(1)} %get-tuple-element.164.refs_6_.refs_9_), channel_id=1, source_target_pairs={{1,2},{2,1},{3,4},{4,3},{5,6},{6,5},{7,8},{8,7},{9,10},{10,9},{11,... | collective-permute-start | bytes 786440 | tf_op jit(solution)/shard_map/ppermute | solution.py:285
  41.6 13.0 %collective-permute-start.8 = (f32[4,128,128]{2,1,0:T(8,128)S(1)}, f32[4,128,128]{2,1,0:T(8,128)S(1)}, u32[]{:S(2)}, u32[]{:S(2)}) collective-permute-start(f32[4,128,128]{2,1,0:T(8,128)S(1)} %get-tuple-element.170.refs_7_.refs_8_.refs_11_), channel_id=1, source_target_pairs={{0,1},{1,0},{2,3},{3,2},{4,5},{5,4},{6,7},{7,6},{8,9},{9,8},{10,11... | collective-permute-start | bytes 786440 | tf_op jit(solution)/shard_map/ppermute | solution.py:285
  46.9 12.6 %collective-permute-start.7 = (f32[4,128,128]{2,1,0:T(8,128)S(1)}, f32[4,128,128]{2,1,0:T(8,128)S(1)}, u32[]{:S(2)}, u32[]{:S(2)}) collective-permute-start(f32[4,128,128]{2,1,0:T(8,128)S(1)} %get-tuple-element.171.refs_6_.refs_9_), channel_id=1, source_target_pairs={{1,2},{2,1},{3,4},{4,3},{5,6},{6,5},{7,8},{8,7},{9,10},{10,9},{11,... | collective-permute-start | bytes 786440 | tf_op jit(solution)/shard_map/ppermute | solution.py:285
  55.2 11.7 %collective-permute-start.10 = (f32[4,128,128]{2,1,0:T(8,128)S(1)}, f32[4,128,128]{2,1,0:T(8,128)S(1)}, u32[]{:S(2)}, u32[]{:S(2)}) collective-permute-start(f32[4,128,128]{2,1,0:T(8,128)S(1)} %get-tuple-element.177.refs_7_.refs_8_.refs_11_), channel_id=1, source_target_pairs={{0,1},{1,0},{2,3},{3,2},{4,5},{5,4},{6,7},{7,6},{8,9},{9,8},{10,11... | collective-permute-start | bytes 786440 | tf_op jit(solution)/shard_map/ppermute | solution.py:285
  60.1 11.6 %collective-permute-start.9 = (f32[4,128,128]{2,1,0:T(8,128)S(1)}, f32[4,128,128]{2,1,0:T(8,128)S(1)}, u32[]{:S(2)}, u32[]{:S(2)}) collective-permute-start(f32[4,128,128]{2,1,0:T(8,128)S(1)} %get-tuple-element.178.refs_6_.refs_9_), channel_id=1, source_target_pairs={{1,2},{2,1},{3,4},{4,3},{5,6},{6,5},{7,8},{8,7},{9,10},{10,9},{11,... | collective-permute-start | bytes 786440 | tf_op jit(solution)/shard_map/ppermute | solution.py:285
  67.5 10.9 %collective-permute-start.12 = (f32[4,128,128]{2,1,0:T(8,128)S(1)}, f32[4,128,128]{2,1,0:T(8,128)S(1)}, u32[]{:S(2)}, u32[]{:S(2)}) collective-permute-start(f32[4,128,128]{2,1,0:T(8,128)S(1)} %get-tuple-element.184.refs_7_.refs_8_.refs_11_), channel_id=1, source_target_pairs={{0,1},{1,0},{2,3},{3,2},{4,5},{5,4},{6,7},{7,6},{8,9},{9,8},{10,11... | collective-permute-start | bytes 786440 | tf_op jit(solution)/shard_map/ppermute | solution.py:285
  72.4 12.8 %collective-permute-start.11 = (f32[4,128,128]{2,1,0:T(8,128)S(1)}, f32[4,128,128]{2,1,0:T(8,128)S(1)}, u32[]{:S(2)}, u32[]{:S(2)}) collective-permute-start(f32[4,128,128]{2,1,0:T(8,128)S(1)} %get-tuple-element.185.refs_6_.refs_9_), channel_id=1, source_target_pairs={{1,2},{2,1},{3,4},{4,3},{5,6},{6,5},{7,8},{8,7},{9,10},{10,9},{11,... | collective-permute-start | bytes 786440 | tf_op jit(solution)/shard_map/ppermute | solution.py:285
  79.1 12.3 %collective-permute-start.14 = (f32[4,128,128]{2,1,0:T(8,128)S(1)}, f32[4,128,128]{2,1,0:T(8,128)S(1)}, u32[]{:S(2)}, u32[]{:S(2)}) collective-permute-start(f32[4,128,128]{2,1,0:T(8,128)S(1)} %get-tuple-element.191.refs_7_.refs_8_.refs_11_), channel_id=1, source_target_pairs={{0,1},{1,0},{2,3},{3,2},{4,5},{5,4},{6,7},{7,6},{8,9},{9,8},{10,11... | collective-permute-start | bytes 786440 | tf_op jit(solution)/shard_map/ppermute | solution.py:285
  85.8 12.7 %collective-permute-start.13 = (f32[4,128,128]{2,1,0:T(8,128)S(1)}, f32[4,128,128]{2,1,0:T(8,128)S(1)}, u32[]{:S(2)}, u32[]{:S(2)}) collective-permute-start(f32[4,128,128]{2,1,0:T(8,128)S(1)} %get-tuple-element.192.refs_6_.refs_9_), channel_id=1, source_target_pairs={{1,2},{2,1},{3,4},{4,3},{5,6},{6,5},{7,8},{8,7},{9,10},{10,9},{11,... | collective-permute-start | bytes 786440 | tf_op jit(solution)/shard_map/ppermute | solution.py:285
  91.4 8.5 %copy-start.5 = (f32[1,16,128,128]{3,2,1,0:T(8,128)S(1)}, f32[1,16,128,128]{3,2,1,0:T(8,128)}, u32[]{:S(2)}) copy-start(f32[1,16,128,128]{3,2,1,0:T(8,128)} %param.13) | copy-start | bytes 3145732
  92.0 21.3 %collective-permute-start.16 = (f32[4,128,128]{2,1,0:T(8,128)S(1)}, f32[4,128,128]{2,1,0:T(8,128)S(1)}, u32[]{:S(2)}, u32[]{:S(2)}) collective-permute-start(f32[4,128,128]{2,1,0:T(8,128)S(1)} %get-tuple-element.198.refs_7_.refs_8_), channel_id=1, source_target_pairs={{0,1},{1,0},{2,3},{3,2},{4,5},{5,4},{6,7},{7,6},{8,9},{9,8},{10,11... | collective-permute-start | bytes 786440 | tf_op jit(solution)/shard_map/ppermute | solution.py:285
  98.5 9.5 %copy-start.6 = (f32[1,16,128,128]{3,2,1,0:T(8,128)S(1)}, f32[1,16,128,128]{3,2,1,0:T(8,128)}, u32[]{:S(2)}) copy-start(f32[1,16,128,128]{3,2,1,0:T(8,128)} %param.12) | copy-start | bytes 3145732
  99.2 14.8 %collective-permute-start.15 = (f32[4,128,128]{2,1,0:T(8,128)S(1)}, f32[4,128,128]{2,1,0:T(8,128)S(1)}, u32[]{:S(2)}, u32[]{:S(2)}) collective-permute-start(f32[4,128,128]{2,1,0:T(8,128)S(1)} %get-tuple-element.199.refs_6_), channel_id=1, source_target_pairs={{1,2},{2,1},{3,4},{4,3},{5,6},{6,5},{7,8},{8,7},{9,10},{10,9},{11,... | collective-permute-start | bytes 786440 | tf_op jit(solution)/shard_map/ppermute | solution.py:285
  100.6 18.7 %collective-permute-start.17 = (f32[4,128,128]{2,1,0:T(8,128)S(1)}, f32[4,128,128]{2,1,0:T(8,128)S(1)}, u32[]{:S(2)}, u32[]{:S(2)}) collective-permute-start(f32[4,128,128]{2,1,0:T(8,128)S(1)} %get-tuple-element.139.refs_6_.refs_8_), channel_id=1, source_target_pairs={{0,1},{1,0},{2,3},{3,2},{4,5},{5,4},{6,7},{7,6},{8,9},{9,8},{10,11... | collective-permute-start | bytes 786440 | tf_op jit(solution)/shard_map/ppermute | solution.py:285
  107.2 20.8 %collective-permute-start = (f32[4,128,128]{2,1,0:T(8,128)S(1)}, f32[4,128,128]{2,1,0:T(8,128)S(1)}, u32[]{:S(2)}, u32[]{:S(2)}) collective-permute-start(f32[4,128,128]{2,1,0:T(8,128)S(1)} %get-tuple-element.137.refs_4_.refs_6_), channel_id=1, source_target_pairs={{1,2},{2,1},{3,4},{4,3},{5,6},{6,5},{7,8},{8,7},{9,10},{10,9},{11,... | collective-permute-start | bytes 786440 | tf_op jit(solution)/shard_map/ppermute | solution.py:285
  120.0 13.8 %collective-permute-start.19 = (f32[4,128,128]{2,1,0:T(8,128)S(1)}, f32[4,128,128]{2,1,0:T(8,128)S(1)}, u32[]{:S(2)}, u32[]{:S(2)}) collective-permute-start(f32[4,128,128]{2,1,0:T(8,128)S(1)} %edge_high.24.refs_7_.refs_5_.refs_8_), channel_id=1, source_target_pairs={{0,1},{1,0},{2,3},{3,2},{4,5},{5,4},{6,7},{7,6},{8,9},{9,8},{10,11... | collective-permute-start | bytes 786440 | tf_op jit(solution)/shard_map/ppermute | solution.py:285
  128.7 11.7 %collective-permute-start.18 = (f32[4,128,128]{2,1,0:T(8,128)S(1)}, f32[4,128,128]{2,1,0:T(8,128)S(1)}, u32[]{:S(2)}, u32[]{:S(2)}) collective-permute-start(f32[4,128,128]{2,1,0:T(8,128)S(1)} %edge_low.24.refs_3_.refs_6_), channel_id=1, source_target_pairs={{1,2},{2,1},{3,4},{4,3},{5,6},{6,5},{7,8},{8,7},{9,10},{10,9},{11,... | collective-permute-start | bytes 786440 | tf_op jit(solution)/shard_map/ppermute | solution.py:285
  134.5 14.9 %collective-permute-start.21 = (f32[4,128,128]{2,1,0:T(8,128)S(1)}, f32[4,128,128]{2,1,0:T(8,128)S(1)}, u32[]{:S(2)}, u32[]{:S(2)}) collective-permute-start(f32[4,128,128]{2,1,0:T(8,128)S(1)} %edge_high.25.refs_7_.refs_5_.refs_8_), channel_id=1, source_target_pairs={{0,1},{1,0},{2,3},{3,2},{4,5},{5,4},{6,7},{7,6},{8,9},{9,8},{10,11... | collective-permute-start | bytes 786440 | tf_op jit(solution)/shard_map/ppermute | solution.py:285
  141.2 12.8 %collective-permute-start.20 = (f32[4,128,128]{2,1,0:T(8,128)S(1)}, f32[4,128,128]{2,1,0:T(8,128)S(1)}, u32[]{:S(2)}, u32[]{:S(2)}) collective-permute-start(f32[4,128,128]{2,1,0:T(8,128)S(1)} %edge_low.25.refs_3_.refs_6_), channel_id=1, source_target_pairs={{1,2},{2,1},{3,4},{4,3},{5,6},{6,5},{7,8},{8,7},{9,10},{10,9},{11,... | collective-permute-start | bytes 786440 | tf_op jit(solution)/shard_map/ppermute | solution.py:285
  150.2 11.9 %collective-permute-start.23 = (f32[4,128,128]{2,1,0:T(8,128)S(1)}, f32[4,128,128]{2,1,0:T(8,128)S(1)}, u32[]{:S(2)}, u32[]{:S(2)}) collective-permute-start(f32[4,128,128]{2,1,0:T(8,128)S(1)} %edge_high.26.refs_7_.refs_5_.refs_8_), channel_id=1, source_target_pairs={{0,1},{1,0},{2,3},{3,2},{4,5},{5,4},{6,7},{7,6},{8,9},{9,8},{10,11... | collective-permute-start | bytes 786440 | tf_op jit(solution)/shard_map/ppermute | solution.py:285
  154.8 13.1 %collective-permute-start.22 = (f32[4,128,128]{2,1,0:T(8,128)S(1)}, f32[4,128,128]{2,1,0:T(8,128)S(1)}, u32[]{:S(2)}, u32[]{:S(2)}) collective-permute-start(f32[4,128,128]{2,1,0:T(8,128)S(1)} %edge_low.26.refs_3_.refs_6_), channel_id=1, source_target_pairs={{1,2},{2,1},{3,4},{4,3},{5,6},{6,5},{7,8},{8,7},{9,10},{10,9},{11,... | collective-permute-start | bytes 786440 | tf_op jit(solution)/shard_map/ppermute | solution.py:285
  162.9 13.9 %collective-permute-start.25 = (f32[4,128,128]{2,1,0:T(8,128)S(1)}, f32[4,128,128]{2,1,0:T(8,128)S(1)}, u32[]{:S(2)}, u32[]{:S(2)}) collective-permute-start(f32[4,128,128]{2,1,0:T(8,128)S(1)} %edge_high.27.refs_7_.refs_5_.refs_8_), channel_id=1, source_target_pairs={{0,1},{1,0},{2,3},{3,2},{4,5},{5,4},{6,7},{7,6},{8,9},{9,8},{10,11... | collective-permute-start | bytes 786440 | tf_op jit(solution)/shard_map/ppermute | solution.py:285
  168.7 13.9 %collective-permute-start.24 = (f32[4,128,128]{2,1,0:T(8,128)S(1)}, f32[4,128,128]{2,1,0:T(8,128)S(1)}, u32[]{:S(2)}, u32[]{:S(2)}) collective-permute-start(f32[4,128,128]{2,1,0:T(8,128)S(1)} %edge_low.27.refs_3_.refs_6_), channel_id=1, source_target_pairs={{1,2},{2,1},{3,4},{4,3},{5,6},{6,5},{7,8},{8,7},{9,10},{10,9},{11,... | collective-permute-start | bytes 786440 | tf_op jit(solution)/shard_map/ppermute | solution.py:285
  177.6 13.3 %collective-permute-start.27 = (f32[4,128,128]{2,1,0:T(8,128)S(1)}, f32[4,128,128]{2,1,0:T(8,128)S(1)}, u32[]{:S(2)}, u32[]{:S(2)}) collective-permute-start(f32[4,128,128]{2,1,0:T(8,128)S(1)} %edge_high.28.refs_7_.refs_5_.refs_8_), channel_id=1, source_target_pairs={{0,1},{1,0},{2,3},{3,2},{4,5},{5,4},{6,7},{7,6},{8,9},{9,8},{10,11... | collective-permute-start | bytes 786440 | tf_op jit(solution)/shard_map/ppermute | solution.py:285
  183.4 13.3 %collective-permute-start.26 = (f32[4,128,128]{2,1,0:T(8,128)S(1)}, f32[4,128,128]{2,1,0:T(8,128)S(1)}, u32[]{:S(2)}, u32[]{:S(2)}) collective-permute-start(f32[4,128,128]{2,1,0:T(8,128)S(1)} %edge_low.28.refs_3_.refs_6_), channel_id=1, source_target_pairs={{1,2},{2,1},{3,4},{4,3},{5,6},{6,5},{7,8},{8,7},{9,10},{10,9},{11,... | collective-permute-start | bytes 786440 | tf_op jit(solution)/shard_map/ppermute | solution.py:285
  191.6 13.9 %collective-permute-start.29 = (f32[4,128,128]{2,1,0:T(8,128)S(1)}, f32[4,128,128]{2,1,0:T(8,128)S(1)}, u32[]{:S(2)}, u32[]{:S(2)}) collective-permute-start(f32[4,128,128]{2,1,0:T(8,128)S(1)} %edge_high.29.refs_7_.refs_5_.refs_8_), channel_id=1, source_target_pairs={{0,1},{1,0},{2,3},{3,2},{4,5},{5,4},{6,7},{7,6},{8,9},{9,8},{10,11... | collective-permute-start | bytes 786440 | tf_op jit(solution)/shard_map/ppermute | solution.py:285
  197.5 14.7 %collective-permute-start.28 = (f32[4,128,128]{2,1,0:T(8,128)S(1)}, f32[4,128,128]{2,1,0:T(8,128)S(1)}, u32[]{:S(2)}, u32[]{:S(2)}) collective-permute-start(f32[4,128,128]{2,1,0:T(8,128)S(1)} %edge_low.29.refs_3_.refs_6_), channel_id=1, source_target_pairs={{1,2},{2,1},{3,4},{4,3},{5,6},{6,5},{7,8},{8,7},{9,10},{10,9},{11,... | collective-permute-start | bytes 786440 | tf_op jit(solution)/shard_map/ppermute | solution.py:285
  203.3 10.3 %copy-start.1 = (f32[16,128,128]{2,1,0:T(8,128)}, f32[16,128,128]{2,1,0:T(8,128)S(1)}, u32[]{:S(2)}) copy-start(f32[16,128,128]{2,1,0:T(8,128)S(1)} %get-tuple-element.264.refs_16_) | copy-start | bytes 3145732
  206.3 18.5 %collective-permute-start.31 = (f32[4,128,128]{2,1,0:T(8,128)S(1)}, f32[4,128,128]{2,1,0:T(8,128)}, u32[]{:S(2)}, u32[]{:S(2)}) collective-permute-start(f32[4,128,128]{2,1,0:T(8,128)S(1)} %edge_high.30.refs_7_.refs_5_), channel_id=1, source_target_pairs={{0,1},{1,0},{2,3},{3,2},{4,5},{5,4},{6,7},{7,6},{8,9},{9,8},{10,11... | collective-permute-start | bytes 786440 | tf_op jit(solution)/shard_map/ppermute | solution.py:285
  213.6 12.3 %collective-permute-start.30 = (f32[4,128,128]{2,1,0:T(8,128)}, f32[4,128,128]{2,1,0:T(8,128)}, u32[]{:S(2)}, u32[]{:S(2)}) collective-permute-start(f32[4,128,128]{2,1,0:T(8,128)} %edge_low.30.refs_3_), channel_id=1, source_target_pairs={{1,2},{2,1},{3,4},{4,3},{5,6},{6,5},{7,8},{8,7},{9,10},{10,9},{11,... | collective-permute-start | bytes 786440 | tf_op jit(solution)/shard_map/ppermute | solution.py:285
  214.9 1.2 copy-start.2
  216.2 1.0 copy-start.12
  217.2 1.0 copy-start.14
  218.2 0.9 copy-start.21
  225.9 1.2 copy-start.10
  225.9 1.2 copy-start.17
  225.9 1.2 copy-start.19
  228.0 2.0 collective-permute-start.32
  230.1 9.5 %collective-permute-start.33 = (f32[2,128,128]{2,1,0:T(8,128)S(1)}, f32[2,128,128]{2,1,0:T(8,128)S(1)}, u32[]{:S(2)}, u32[]{:S(2)}) collective-permute-start(f32[2,128,128]{2,1,0:T(8,128)S(1)} %get-tuple-element.278), channel_id=1, source_target_pairs={{0,32},{16,48},{32,64},{48,80},{64,96},{80,112},{96,0},{112,16},{1... | collective-permute-start | bytes 393224 | tf_op jit(solution)/shard_map/ppermute | solution.py:285
  234.6 9.0 %collective-permute-start.34 = (f32[2,128,128]{2,1,0:T(8,128)S(1)}, f32[2,128,128]{2,1,0:T(8,128)S(1)}, u32[]{:S(2)}, u32[]{:S(2)}) collective-permute-start(f32[2,128,128]{2,1,0:T(8,128)S(1)} %get-tuple-element.280), channel_id=1, source_target_pairs={{0,64},{16,80},{32,96},{48,112},{64,0},{80,16},{96,32},{112,48},{1... | collective-permute-start | bytes 393224 | tf_op jit(solution)/shard_map/ppermute | solution.py:285
  237.3 6.3 %collective-permute-start.35 = (f32[2,128,128]{2,1,0:T(8,128)S(1)}, f32[2,128,128]{2,1,0:T(8,128)S(1)}, u32[]{:S(2)}, u32[]{:S(2)}) collective-permute-start(f32[2,128,128]{2,1,0:T(8,128)S(1)} %get-tuple-element.279), channel_id=1, source_target_pairs={{0,96},{16,112},{32,0},{48,16},{64,32},{80,48},{96,64},{112,80},{1... | collective-permute-start | bytes 393224 | tf_op jit(solution)/shard_map/ppermute | solution.py:285
  243.6 9.0 %collective-permute-start.36 = (f32[2,128,128]{2,1,0:T(8,128)S(1)}, f32[2,128,128]{2,1,0:T(8,128)S(1)}, u32[]{:S(2)}, u32[]{:S(2)}) collective-permute-start(f32[2,128,128]{2,1,0:T(8,128)S(1)} %add_add_fusion), channel_id=1, source_target_pairs={{0,128},{16,144},{32,160},{48,176},{64,192},{80,208},{96,224},{112... | collective-permute-start | bytes 393224 | tf_op jit(solution)/shard_map/ppermute | solution.py:285
  252.7 7.6 %collective-permute-start.37 = (f32[2,128,128]{2,1,0:T(8,128)S(1)}, f32[2,128,128]{2,1,0:T(8,128)S(1)}, u32[]{:S(2)}, u32[]{:S(2)}) collective-permute-start(f32[2,128,128]{2,1,0:T(8,128)S(1)} %get-tuple-element.275), channel_id=1, source_target_pairs={{0,32},{16,48},{32,64},{48,80},{64,96},{80,112},{96,0},{112,16},{1... | collective-permute-start | bytes 393224 | tf_op jit(solution)/shard_map/ppermute | solution.py:285
  254.1 8.0 %collective-permute-start.38 = (f32[2,128,128]{2,1,0:T(8,128)S(1)}, f32[2,128,128]{2,1,0:T(8,128)S(1)}, u32[]{:S(2)}, u32[]{:S(2)}) collective-permute-start(f32[2,128,128]{2,1,0:T(8,128)S(1)} %get-tuple-element.275), channel_id=1, source_target_pairs={{0,64},{16,80},{32,96},{48,112},{64,0},{80,16},{96,32},{112,48},{1... | collective-permute-start | bytes 393224 | tf_op jit(solution)/shard_map/ppermute | solution.py:285
  256.8 5.4 %collective-permute-start.39 = (f32[2,128,128]{2,1,0:T(8,128)S(1)}, f32[2,128,128]{2,1,0:T(8,128)S(1)}, u32[]{:S(2)}, u32[]{:S(2)}) collective-permute-start(f32[2,128,128]{2,1,0:T(8,128)S(1)} %get-tuple-element.275), channel_id=1, source_target_pairs={{0,96},{16,112},{32,0},{48,16},{64,32},{80,48},{96,64},{112,80},{1... | collective-permute-start | bytes 393224 | tf_op jit(solution)/shard_map/ppermute | solution.py:285
  262.3 2.0 collective-permute-start.40
  265.7 10.3 %collective-permute-start.41 = (f32[8,128]{1,0:T(8,128)S(1)}, f32[8,128]{1,0:T(8,128)S(1)}, u32[]{:S(2)}, u32[]{:S(2)}) collective-permute-start(f32[8,128]{1,0:T(8,128)S(1)} %broadcast_in_dim.7), channel_id=1, source_target_pairs={{0,4},{1,5},{2,6},{3,7},{4,8},{5,9},{6,10},{7,11},{8,12},{9,13},{1... | collective-permute-start | bytes 12296 | tf_op jit(solution)/shard_map/ppermute | solution.py:285
  269.9 7.6 %collective-permute-start.42 = (f32[8,128]{1,0:T(8,128)S(1)}, f32[8,128]{1,0:T(8,128)S(1)}, u32[]{:S(2)}, u32[]{:S(2)}) collective-permute-start(f32[8,128]{1,0:T(8,128)S(1)} %broadcast_in_dim.7), channel_id=1, source_target_pairs={{0,8},{1,9},{2,10},{3,11},{4,12},{5,13},{6,14},{7,15},{8,0},{9,1},... | collective-permute-start | bytes 12296 | tf_op jit(solution)/shard_map/ppermute | solution.py:285
  275.8 3.6 %collective-permute-start.43 = (f32[8,128]{1,0:T(8,128)S(1)}, f32[8,128]{1,0:T(8,128)S(1)}, u32[]{:S(2)}, u32[]{:S(2)}) collective-permute-start(f32[8,128]{1,0:T(8,128)S(1)} %broadcast_in_dim.7), channel_id=1, source_target_pairs={{0,12},{1,13},{2,14},{3,15},{4,0},{5,1},{6,2},{7,3},{8,4},{9,5},{1... | collective-permute-start | bytes 12296 | tf_op jit(solution)/shard_map/ppermute | solution.py:285
  280.1 9.0 %collective-permute-start.44 = (f32[8,128]{1,0:T(8,128)S(1)}, f32[8,128]{1,0:T(8,128)S(1)}, u32[]{:S(2)}, u32[]{:S(2)}) collective-permute-start(f32[8,128]{1,0:T(8,128)S(1)} %maximum_maximum_fusion.1), channel_id=1, source_target_pairs={{0,1},{1,2},{2,3},{3,0},{4,5},{5,6},{6,7},{7,4},{8,9},{9,10},{10,1... | collective-permute-start | bytes 12296 | tf_op jit(solution)/shard_map/ppermute | solution.py:285
  284.8 4.5 %collective-permute-start.45 = (f32[8,128]{1,0:T(8,128)S(1)}, f32[8,128]{1,0:T(8,128)S(1)}, u32[]{:S(2)}, u32[]{:S(2)}) collective-permute-start(f32[8,128]{1,0:T(8,128)S(1)} %maximum_maximum_fusion.1), channel_id=1, source_target_pairs={{0,2},{1,3},{2,0},{3,1},{4,6},{5,7},{6,4},{7,5},{8,10},{9,11},{10,... | collective-permute-start | bytes 12296 | tf_op jit(solution)/shard_map/ppermute | solution.py:285
  286.3 4.2 %collective-permute-start.46 = (f32[8,128]{1,0:T(8,128)S(1)}, f32[8,128]{1,0:T(8,128)S(1)}, u32[]{:S(2)}, u32[]{:S(2)}) collective-permute-start(f32[8,128]{1,0:T(8,128)S(1)} %maximum_maximum_fusion.1), channel_id=1, source_target_pairs={{0,3},{1,0},{2,1},{3,2},{4,7},{5,4},{6,5},{7,6},{8,11},{9,8},{10,9... | collective-permute-start | bytes 12296 | tf_op jit(solution)/shard_map/ppermute | solution.py:285
  (7 other events, 5.6 us)

commit v3 on v2

--- a/solution.py
+++ b/solution.py
@@ -19,6 +19,7 @@
 MID = ROWS - 2 * EDGE
 CHUNK = 32
 SLICE = 8
+EARLY = (4, 6)
 VMEM = pl.BlockSpec(memory_space=pltpu.VMEM)
 SMEM = pl.BlockSpec(memory_space=pltpu.SMEM)
 LIMIT = 12 * 1024 * 1024
@@ -42,22 +43,17 @@
     )
 
 
-def sort_kernel(first_ref, receivers_ref, lists_ref):
-    def body(j, counts):
-        plane = where_of(receivers_ref[0, j], first_ref)[0]
-        inside = (plane >= 0) & (plane < ROWS)
-        low = inside & (plane < EDGE)
-        high = inside & (plane >= ROWS - EDGE)
-        mid = inside & (plane >= EDGE) & (plane < ROWS - EDGE)
-        lists_ref[jnp.where(low, 0, 3), counts[0]] = j
-        lists_ref[jnp.where(mid, 1, 3), counts[1]] = j
-        lists_ref[jnp.where(high, 2, 3), counts[2]] = j
-        return tuple(c + x.astype(jnp.int32) for c, x in zip(counts, (low, mid, high)))
-
-    zero = jnp.int32(0)
-    counts = lax.fori_loop(0, REC, body, (zero, zero, zero), unroll=4)
-    for region in range(3):
-        lists_ref[region, REC] = counts[region]
+def sort_receivers(first, receivers):
+    plane = where_of(receivers, first)[0]
+    bounds = jnp.array([0, EDGE, ROWS - EDGE, ROWS], jnp.int32)
+    inside = (plane[None] >= bounds[:3, None]) & (plane[None] < bounds[1:, None])
+    order = jnp.arange(REC, dtype=jnp.int32)
+    ahead = inside[:, :, None] & (order[:, None] < order[None])[None]
+    rank = jnp.sum(ahead.astype(jnp.int32), 1)
+    hit = inside[:, :, None] & (rank[:, :, None] == order[None, None])
+    lists = jnp.sum(jnp.where(hit, order[None, :, None], 0), 1)
+    counts = jnp.sum(inside.astype(jnp.int32), 1)
+    return jnp.concatenate([lists, jnp.broadcast_to(counts[:, None], (3, 128))], 1)
 
 
 def where_of(cell, first_ref):
@@ -91,6 +87,26 @@
 
         lax.fori_loop(0, count, body, 0)
         start += count
+
+
+def largest_kernel(core_ref, half_ref, other_ref, total_ref, out_ref):
+    def body(i, best):
+        for ref, half in ((half_ref, core_ref[0]), (other_ref, 1 - core_ref[0])):
+            for row in range(0, NY, 8):
+                rows = pl.ds(row, 8)
+                value = ref[i, rows, :]
+                total_ref[half * 8 + i, rows, :] = value
+                best = jnp.maximum(best, jnp.abs(value))
+        return best
+
+    out_ref[...] = lax.fori_loop(0, 8, body, jnp.zeros((8, NZ), jnp.float32))
+
+
+def final_kernel(largest_ref, total_ref, model_ref, direction_ref, new_ref):
+    bottom = jnp.max(largest_ref[...]) + EPSILON
+    direction = total_ref[...] / bottom
+    direction_ref[...] = direction
+    new_ref[...] = model_ref[...] * (1.0 - STEP_FRACTION * direction)
 
 
 def lanes_row():
@@ -189,6 +205,8 @@
     cur = take(3)
     old = take(3)
     model = take(3)
+    if forward and tick in EARLY:
+        take(1)
     if not forward:
         if tick == STEPS - 1:
             last = take(3)
@@ -307,14 +325,19 @@
     for r in range(4):
         half = lax.dynamic_update_slice_in_dim(half, got[r], ((y - r) % 4) * 2, 0)
     other = swap(half, "shot", other_core)
-    first = jnp.where(core == 0, half, other)
-    second = jnp.where(core == 0, other, half)
-    return jnp.concatenate([first, second])
+    return call(
+        largest_kernel,
+        [planes(ROWS), jax.ShapeDtypeStruct((8, NZ), jnp.float32)],
+        [],
+        [SMEM, VMEM, VMEM],
+        [VMEM] * 2,
+        2 * ROWS * NY * NZ,
+        2 * ROWS * NY * NZ * 4,
+        "largest",
+    )(core.astype(jnp.int32).reshape(1), half, other)
 
 
 def dom_max(value):
-    value = jnp.broadcast_to(value, (8, 128))
-
     def along_x(r):
         return [(k, ((k // 4 + r) % 4) * 4 + k % 4) for k in range(16)]
 
@@ -324,7 +347,7 @@
     for turn in (along_x, along_z):
         got = [swap(value, "dom", turn(r)) for r in (1, 2, 3)]
         value = jnp.maximum(jnp.maximum(value, got[0]), jnp.maximum(got[1], got[2]))
-    return value[0, 0]
+    return value
 
 
 def on_device(model_slab, wave_prev, wave_now, adjoint_next, adjoint_now, wavelet, source_cell, receiver_cells, observed):
@@ -346,16 +369,7 @@
             "cut",
         )(first, a)
 
-    lists = call(
-        sort_kernel,
-        jax.ShapeDtypeStruct((4, REC + 128), jnp.int32),
-        [],
-        [SMEM, SMEM],
-        SMEM,
-        1000,
-        4096,
-        "sort_receivers",
-    )(first, receiver_cells)
+    lists = sort_receivers(first, receiver_cells[0])
     observed = observed[0]
     model = cut(model_slab)
     pad = [pltpu.VMEM((ROWS + 2 * EDGE, NY + 16, NZ), jnp.float32)]
@@ -390,6 +404,8 @@
         return low, high
 
     old, cur = cut(wave_prev[0]), cut(wave_now[0])
+    adjoint_old, adjoint_cur = cut(adjoint_next[0]), cut(adjoint_now[0])
+    adjoint_sent = [None, None]
     images, residuals = [], []
     for tick in range(STEPS):
         sent = halos(cur, tick)
@@ -401,23 +417,27 @@
             functools.partial(own_kernel, True, tick, False),
             outs,
             pad,
-            [SMEM] * len(smem) + [VMEM] * 9,
+            [SMEM] * len(smem) + [VMEM] * 9 + [ANY] * (tick in EARLY),
             [VMEM] * len(outs),
             name="own_forward",
             **own_cost,
-        )(*smem, *cur, *old, *model)
+        )(*smem, *cur, *old, *model, *([adjoint_sent[EARLY.index(tick)]] if tick in EARLY else []))
         mid, base_lo, base_hi, part_lo, image_mid, part_hi = result[:6]
+        if tick + 1 in EARLY:
+            side = EARLY.index(tick + 1)
+            edge, mid = lax.optimization_barrier((adjoint_cur[2 * side], mid))
+            adjoint_sent[side] = swap(edge, "dom", (starts, ends)[side])
         if tick > 0:
             residuals.append(result[6])
         (low, image_lo), (high, image_hi) = edges(True, tick, sent, (base_lo, base_hi), (part_lo, part_hi))
         images.append((image_lo, image_mid, image_hi))
         old, cur = cur, (low, mid, high)
     last = cur
-    old, cur = cut(adjoint_next[0]), cut(adjoint_now[0])
+    old, cur = adjoint_old, adjoint_cur
     grad = None
     for tick in reversed(range(STEPS)):
-        sent = halos(cur, tick)
         top = tick == STEPS - 1
+        sent = adjoint_sent if top else halos(cur, tick)
         extra = (observed,) if top else ()
         fields = last if top else (residuals[tick], *images[tick + 1], grad)
         outs = [planes(MID), planes(EDGE), planes(EDGE)]
@@ -448,11 +468,17 @@
         4 * ROWS * NY * NZ * 4,
         "join",
     )(first, grad, *cur, *images[0])
-    total = shot_sum(grad)
-    peak = dom_max(jnp.max(jnp.abs(total)))
-    direction = total / (peak + EPSILON)
-    new_model = model_slab * (1.0 - STEP_FRACTION * direction)
-    return direction, new_model
+    total, largest = shot_sum(grad)
+    block = pl.BlockSpec((EDGE, NY, NZ), lambda i: (i, 0, 0))
+    return pl.pallas_call(
+        final_kernel,
+        grid=(ROWS // EDGE,),
+        out_shape=[planes(ROWS)] * 2,
+        in_specs=[pl.BlockSpec((8, NZ), lambda i: (0, 0)), block, block],
+        out_specs=[block, block],
+        compiler_params=pltpu.CompilerParams(vmem_limit_bytes=LIMIT),
+        name="final",
+    )(dom_max(largest), total, model_slab)
 
 
 def solution(mesh):

time: 295 us -> 298 us (1.010)
  starting transfers between devices: 128 us -> 133 us
  waiting for transfers between devices: 43.2 us -> 46.8 us
  Pallas kernels: 106 us -> 103 us
    ppermute x47, starting transfers between devices: 128 us -> 133 us  [swap(): return lax.ppermute(value, axis, pairs)]
    pallas_call x1 -> x2, Pallas kernels: 6.46 us -> 2.36 us  [the longest x1 2.07 us: on_device(): pl.pallas_call(final_kernel, grid=(ROWS // EDGE,), out_shape=[planes(ROWS...]
    ppermute x47, waiting for transfers between devices: 43.2 us -> 46.8 us  [swap(): return lax.ppermute(value, axis, pairs)]
    unnamed x48 -> x52, local copies, waits for them, and re-layouts: 9.02 us -> 10.8 us
  transfers between devices with their start and end apart: 47 -> 47, of which waited for: 20 -> 23; matrix products, arithmetic and copies ran while one was open for 0% -> 0% of each run, Pallas kernels for 35% -> 31%
where the time goes in v3:
time: 298 us; the launch traced here: 296 us
  starting transfers between devices  133 us (45%)
  Pallas kernels  103 us (35%)
  waiting for transfers between devices  46.8 us (16%)
  local copies, waits for them, and re-layouts  11 us (4%)
    ppermute x47, starting transfers between devices, swap(): return lax.ppermute(value, axis, pairs)  133 us
    ppermute x47, waiting for transfers between devices, swap(): return lax.ppermute(value, axis, pairs)  46.8 us
    pallas_call x8, Pallas kernels, on_device(): call(functools.partial(own_kernel, True, tick, False), outs, pad, [SMEM]...  35.8 us
    pallas_call x8, Pallas kernels, on_device(): call(functools.partial(own_kernel, False, tick, not top), outs, pad, [SME...  35.3 us
    pallas_call x32, Pallas kernels, edges(): call(functools.partial(edge_kernel, forward, tick, high), [planes(EDGE)]...  24.9 us
    unnamed x52, local copies, waits for them, and re-layouts  10.8 us
  transfers between devices with their start and end apart: 47, of which 23 were waited for; matrix products, arithmetic and copies ran while one was open for 0% of the time, Pallas kernels for 31%

profile of v3, /device:TPU:0, one launch (start us, length us, event | category | flops | bytes accessed | tf_op | source)
XLA Modules:
  0.0 296.3 jit_solution(10406723739481198961)
XLA Ops:
  0.7 1.3 copy-done.3
  3.0 1.5 collective-permute-start
  5.3 1.2 copy-done.4
  8.6 4.1 %own_forward.8 = (f32[8,128,128]{2,1,0:T(8,128)S(1)}, f32[4,128,128]{2,1,0:T(8,128)S(1)}, f32[4,128,128]{2,1,0:T(8,128)S(1)}, f32[4,128,128]{2,1,0:T(8,128)S(1)}...) custom-call(s32[2]{0:T(128)S(1)} %pad_add_fusion.1.first_ref.refs_0_, s32[1]{0:T(128)S(6)} %copy.16.refs_1_.refs_3_, ...), custom_call_target="tpu_custom_call" | custom-call | flops 15728640 | bytes 8388608 | tf_op jit(solution)/shard_map/own_forward/pallas_call | solution.py:416
  14.6 4.5 %collective-permute-start.3 = (f32[4,128,128]{2,1,0:T(8,128)S(1)}, f32[4,128,128]{2,1,0:T(8,128)S(1)}, u32[]{:S(2)}, u32[]{:S(2)}) collective-permute-start(f32[4,128,128]{2,1,0:T(8,128)S(1)} %get-tuple-element.157.refs_7_.refs_8_.refs_11_), channel_id=1, source_target_pairs={{0,1},{1,0},{2,3},{3,2},{4,5},{5,4},{6,7},{7,6},{8,9},{9,8},{10,11... | collective-permute-start | bytes 786440 | tf_op jit(solution)/shard_map/ppermute | solution.py:303
  19.1 1.1 edge_low.16
  22.2 4.5 %own_forward.9 = (f32[8,128,128]{2,1,0:T(8,128)S(1)}, f32[4,128,128]{2,1,0:T(8,128)S(1)}, f32[4,128,128]{2,1,0:T(8,128)S(1)}, f32[4,128,128]{2,1,0:T(8,128)S(1)}...) custom-call(s32[2]{0:T(128)S(1)} %pad_add_fusion.1.first_ref.refs_0_, ...), custom_call_target="tpu_custom_call" | custom-call | flops 15728640 | bytes 8388608 | tf_op jit(solution)/shard_map/own_forward/pallas_call | solution.py:416
  27.5 3.4 %collective-permute-start.5 = (f32[4,128,128]{2,1,0:T(8,128)S(1)}, f32[4,128,128]{2,1,0:T(8,128)S(1)}, u32[]{:S(2)}, u32[]{:S(2)}) collective-permute-start(f32[4,128,128]{2,1,0:T(8,128)S(1)} %get-tuple-element.164.refs_7_.refs_8_.refs_11_), channel_id=1, source_target_pairs={{0,1},{1,0},{2,3},{3,2},{4,5},{5,4},{6,7},{7,6},{8,9},{9,8},{10,11... | collective-permute-start | bytes 786440 | tf_op jit(solution)/shard_map/ppermute | solution.py:303
  32.2 4.5 %own_forward.10 = (f32[8,128,128]{2,1,0:T(8,128)S(1)}, f32[4,128,128]{2,1,0:T(8,128)S(1)}, f32[4,128,128]{2,1,0:T(8,128)S(1)}, f32[4,128,128]{2,1,0:T(8,128)S(1)...) custom-call(s32[2]{0:T(128)S(1)} %pad_add_fusion.1.first_ref.refs_0_, ...), custom_call_target="tpu_custom_call" | custom-call | flops 15728640 | bytes 8388608 | tf_op jit(solution)/shard_map/own_forward/pallas_call | solution.py:416
  38.4 6.0 %collective-permute-start.8 = (f32[4,128,128]{2,1,0:T(8,128)S(1)}, f32[4,128,128]{2,1,0:T(8,128)S(1)}, u32[]{:S(2)}, u32[]{:S(2)}) collective-permute-start(f32[4,128,128]{2,1,0:T(8,128)S(1)} %get-tuple-element.171.refs_7_.refs_8_.refs_11_), channel_id=1, source_target_pairs={{0,1},{1,0},{2,3},{3,2},{4,5},{5,4},{6,7},{7,6},{8,9},{9,8},{10,11... | collective-permute-start | bytes 786440 | tf_op jit(solution)/shard_map/ppermute | solution.py:303
  46.5 4.5 %own_forward.11 = (f32[8,128,128]{2,1,0:T(8,128)S(1)}, f32[4,128,128]{2,1,0:T(8,128)S(1)}, f32[4,128,128]{2,1,0:T(8,128)S(1)}, f32[4,128,128]{2,1,0:T(8,128)S(1)...) custom-call(s32[2]{0:T(128)S(1)} %pad_add_fusion.1.first_ref.refs_0_, ...), custom_call_target="tpu_custom_call" | custom-call | flops 15728640 | bytes 8388608 | tf_op jit(solution)/shard_map/own_forward/pallas_call | solution.py:416
  52.4 10.7 %collective-permute-start.10 = (f32[4,128,128]{2,1,0:T(8,128)S(1)}, f32[4,128,128]{2,1,0:T(8,128)S(1)}, u32[]{:S(2)}, u32[]{:S(2)}) collective-permute-start(f32[4,128,128]{2,1,0:T(8,128)S(1)} %get-tuple-element.185.refs_7_.refs_8_.refs_11_), channel_id=1, source_target_pairs={{0,1},{1,0},{2,3},{3,2},{4,5},{5,4},{6,7},{7,6},{8,9},{9,8},{10,11... | collective-permute-start | bytes 786440 | tf_op jit(solution)/shard_map/ppermute | solution.py:303
  64.5 4.5 %own_forward.12 = (f32[8,128,128]{2,1,0:T(8,128)S(1)}, f32[4,128,128]{2,1,0:T(8,128)S(1)}, f32[4,128,128]{2,1,0:T(8,128)S(1)}, f32[4,128,128]{2,1,0:T(8,128)S(1)...) custom-call(s32[2]{0:T(128)S(1)} %pad_add_fusion.1.first_ref.refs_0_, ...), custom_call_target="tpu_custom_call" | custom-call | flops 15728640 | bytes 8388608 | tf_op jit(solution)/shard_map/own_forward/pallas_call | solution.py:416
  69.0 4.6 %collective-permute-done.10.refs_3_ = f32[4,128,128]{2,1,0:T(8,128)S(1)} collective-permute-done((f32[4,128,128]{2,1,0:T(8,128)S(1)}, f32[4,128,128]{2,1,0:T(8,128)S(1)}, u32[]{:S(2)}, u32[]{:S(2)}) %collective-permute-start.10) | collective-permute-done | bytes 262176 | tf_op jit(solution)/shard_map/ppermute | solution.py:303
  74.2 12.4 %collective-permute-start.12 = (f32[4,128,128]{2,1,0:T(8,128)S(1)}, f32[4,128,128]{2,1,0:T(8,128)S(1)}, u32[]{:S(2)}, u32[]{:S(2)}) collective-permute-start(f32[4,128,128]{2,1,0:T(8,128)S(1)} %get-tuple-element.192.refs_7_.refs_8_.refs_11_), channel_id=1, source_target_pairs={{0,1},{1,0},{2,3},{3,2},{4,5},{5,4},{6,7},{7,6},{8,9},{9,8},{10,11... | collective-permute-start | bytes 786440 | tf_op jit(solution)/shard_map/ppermute | solution.py:303
  87.9 4.5 %own_forward.13 = (f32[8,128,128]{2,1,0:T(8,128)S(1)}, f32[4,128,128]{2,1,0:T(8,128)S(1)}, f32[4,128,128]{2,1,0:T(8,128)S(1)}, f32[4,128,128]{2,1,0:T(8,128)S(1)...) custom-call(s32[2]{0:T(128)S(1)} %pad_add_fusion.1.first_ref.refs_0_, ...), custom_call_target="tpu_custom_call" | custom-call | flops 15728640 | bytes 8388608 | tf_op jit(solution)/shard_map/own_forward/pallas_call | solution.py:416
  92.5 1.6 collective-permute-start.14
  96.8 8.7 %collective-permute-done.14.refs_15_.refs_3_ = f32[4,128,128]{2,1,0:T(8,128)S(1)} collective-permute-done((f32[4,128,128]{2,1,0:T(8,128)S(1)}, f32[4,128,128]{2,1,0:T(8,128)S(1)}, u32[]{:S(2)}, u32[]{:S(2)}) %collective-permute-start.14) | collective-permute-done | bytes 262176 | tf_op jit(solution)/shard_map/ppermute | solution.py:303
  105.4 4.5 %own_forward.14 = (f32[8,128,128]{2,1,0:T(8,128)S(1)}, f32[4,128,128]{2,1,0:T(8,128)S(1)}, f32[4,128,128]{2,1,0:T(8,128)S(1)}, f32[4,128,128]{2,1,0:T(8,128)S(1)...) custom-call(s32[2]{0:T(128)S(1)} %pad_add_fusion.1.first_ref.refs_0_, ...), custom_call_target="tpu_custom_call" | custom-call | flops 15728640 | bytes 8388608 | tf_op jit(solution)/shard_map/own_forward/pallas_call | solution.py:416
  109.9 2.0 collective-permute-done.15.refs_3_
  114.9 4.5 %own_forward.15 = (f32[8,128,128]{2,1,0:T(8,128)S(1)}, f32[4,128,128]{2,1,0:T(8,128)S(1)}, f32[4,128,128]{2,1,0:T(8,128)S(1)}, f32[4,128,128]{2,1,0:T(8,128)S(1)...) custom-call(s32[2]{0:T(128)S(1)} %pad_add_fusion.1.first_ref.refs_0_, ...), custom_call_target="tpu_custom_call" | custom-call | flops 15728640 | bytes 8388608 | tf_op jit(solution)/shard_map/own_forward/pallas_call | solution.py:416
  119.4 2.8 collective-permute-done.17.refs_3_
  123.6 4.6 %own_adjoint.8 = (f32[8,128,128]{2,1,0:T(8,128)S(1)}, f32[4,128,128]{2,1,0:T(8,128)S(1)}, f32[4,128,128]{2,1,0:T(8,128)S(1)}, f32[256,128]{1,0:T(8,128)S(1)}, f32[16,128,128]{2,1,0:T(8,128)S(1)}) custom-call(s32[2]{0:T(128)S(1)} %pad_add_fusion.1.first_ref.refs_0_, s32[1,256]{1,0:T(1,128)S(1)} %copy-done.7, s32[3,384]{1,0:T(4,128)S(1)} %pad_add_fusion.refs_2_, ...), custom_call_target="tpu_custom_call" | custom-call | flops 15728640 | bytes 8388608 | tf_op jit(solution)/shard_map/own_adjoint/pallas_call | solution.py:446
  129.0 9.9 %collective-permute-start.19 = (f32[4,128,128]{2,1,0:T(8,128)S(1)}, f32[4,128,128]{2,1,0:T(8,128)S(1)}, u32[]{:S(2)}, u32[]{:S(2)}) collective-permute-start(f32[4,128,128]{2,1,0:T(8,128)S(1)} %edge_high.24.refs_7_.refs_5_.refs_8_), channel_id=1, source_target_pairs={{0,1},{1,0},{2,3},{3,2},{4,5},{5,4},{6,7},{7,6},{8,9},{9,8},{10,11... | collective-permute-start | bytes 786440 | tf_op jit(solution)/shard_map/ppermute | solution.py:303
  140.3 4.3 %own_adjoint.9 = (f32[8,128,128]{2,1,0:T(8,128)S(1)}, f32[4,128,128]{2,1,0:T(8,128)S(1)}, f32[4,128,128]{2,1,0:T(8,128)S(1)}, f32[16,128,128]{2,1,0:T(8,128)S(1)}) custom-call(s32[2]{0:T(128)S(1)} %pad_add_fusion.1.first_ref.refs_0_, s32[1,256]{1,0:T(1,128)S(1)} %copy-done.7, s32[3,384]{1,0:T(4,128)S(1)} %pad_add_fusion.refs_2_, ...), custom_call_target="tpu_custom_call" | custom-call | flops 15728640 | bytes 8388608 | tf_op jit(solution)/shard_map/own_adjoint/pallas_call | solution.py:446
  145.7 2.1 collective-permute-start.21
  149.2 4.3 %own_adjoint.10 = (f32[8,128,128]{2,1,0:T(8,128)S(1)}, f32[4,128,128]{2,1,0:T(8,128)S(1)}, f32[4,128,128]{2,1,0:T(8,128)S(1)}, f32[16,128,128]{2,1,0:T(8,128)S(1)}) custom-call(s32[2]{0:T(128)S(1)} %pad_add_fusion.1.first_ref.refs_0_, s32[1,256]{1,0:T(1,128)S(1)} %copy-done.7, s32[3,384]{1,0:T(4,128)S(1)} %pad_add_fusion.refs_2_, ...), custom_call_target="tpu_custom_call" | custom-call | flops 15728640 | bytes 8388608 | tf_op jit(solution)/shard_map/own_adjoint/pallas_call | solution.py:446
  153.6 1.7 collective-permute-done.21.refs_3_
  156.1 4.8 %collective-permute-start.23 = (f32[4,128,128]{2,1,0:T(8,128)S(1)}, f32[4,128,128]{2,1,0:T(8,128)S(1)}, u32[]{:S(2)}, u32[]{:S(2)}) collective-permute-start(f32[4,128,128]{2,1,0:T(8,128)S(1)} %edge_high.26.refs_7_.refs_5_.refs_8_), channel_id=1, source_target_pairs={{0,1},{1,0},{2,3},{3,2},{4,5},{5,4},{6,7},{7,6},{8,9},{9,8},{10,11... | collective-permute-start | bytes 786440 | tf_op jit(solution)/shard_map/ppermute | solution.py:303
  162.4 4.3 %own_adjoint.11 = (f32[8,128,128]{2,1,0:T(8,128)S(1)}, f32[4,128,128]{2,1,0:T(8,128)S(1)}, f32[4,128,128]{2,1,0:T(8,128)S(1)}, f32[16,128,128]{2,1,0:T(8,128)S(1)}) custom-call(s32[2]{0:T(128)S(1)} %pad_add_fusion.1.first_ref.refs_0_, s32[1,256]{1,0:T(1,128)S(1)} %copy-done.7, s32[3,384]{1,0:T(4,128)S(1)} %pad_add_fusion.refs_2_, ...), custom_call_target="tpu_custom_call" | custom-call | flops 15728640 | bytes 8388608 | tf_op jit(solution)/shard_map/own_adjoint/pallas_call | solution.py:446
  168.4 6.0 %collective-permute-start.25 = (f32[4,128,128]{2,1,0:T(8,128)S(1)}, f32[4,128,128]{2,1,0:T(8,128)S(1)}, u32[]{:S(2)}, u32[]{:S(2)}) collective-permute-start(f32[4,128,128]{2,1,0:T(8,128)S(1)} %edge_high.27.refs_7_.refs_5_.refs_8_), channel_id=1, source_target_pairs={{0,1},{1,0},{2,3},{3,2},{4,5},{5,4},{6,7},{7,6},{8,9},{9,8},{10,11... | collective-permute-start | bytes 786440 | tf_op jit(solution)/shard_map/ppermute | solution.py:303
  175.9 4.3 %own_adjoint.12 = (f32[8,128,128]{2,1,0:T(8,128)S(1)}, f32[4,128,128]{2,1,0:T(8,128)S(1)}, f32[4,128,128]{2,1,0:T(8,128)S(1)}, f32[16,128,128]{2,1,0:T(8,128)S(1)}) custom-call(s32[2]{0:T(128)S(1)} %pad_add_fusion.1.first_ref.refs_0_, s32[1,256]{1,0:T(1,128)S(1)} %copy-done.7, s32[3,384]{1,0:T(4,128)S(1)} %pad_add_fusion.refs_2_, ...), custom_call_target="tpu_custom_call" | custom-call | flops 15728640 | bytes 8388608 | tf_op jit(solution)/shard_map/own_adjoint/pallas_call | solution.py:446
  181.5 5.6 %collective-permute-start.27 = (f32[4,128,128]{2,1,0:T(8,128)S(1)}, f32[4,128,128]{2,1,0:T(8,128)S(1)}, u32[]{:S(2)}, u32[]{:S(2)}) collective-permute-start(f32[4,128,128]{2,1,0:T(8,128)S(1)} %edge_high.28.refs_7_.refs_5_.refs_8_), channel_id=1, source_target_pairs={{0,1},{1,0},{2,3},{3,2},{4,5},{5,4},{6,7},{7,6},{8,9},{9,8},{10,11... | collective-permute-start | bytes 786440 | tf_op jit(solution)/shard_map/ppermute | solution.py:303
  188.6 4.3 %own_adjoint.13 = (f32[8,128,128]{2,1,0:T(8,128)S(1)}, f32[4,128,128]{2,1,0:T(8,128)S(1)}, f32[4,128,128]{2,1,0:T(8,128)S(1)}, f32[16,128,128]{2,1,0:T(8,128)S(1)}) custom-call(s32[2]{0:T(128)S(1)} %pad_add_fusion.1.first_ref.refs_0_, s32[1,256]{1,0:T(1,128)S(1)} %copy-done.7, s32[3,384]{1,0:T(4,128)S(1)} %pad_add_fusion.refs_2_, ...), custom_call_target="tpu_custom_call" | custom-call | flops 15728640 | bytes 8388608 | tf_op jit(solution)/shard_map/own_adjoint/pallas_call | solution.py:446
  193.0 1.3 collective-permute-done.27.refs_3_
  195.1 6.4 %collective-permute-start.29 = (f32[4,128,128]{2,1,0:T(8,128)S(1)}, f32[4,128,128]{2,1,0:T(8,128)S(1)}, u32[]{:S(2)}, u32[]{:S(2)}) collective-permute-start(f32[4,128,128]{2,1,0:T(8,128)S(1)} %edge_high.29.refs_7_.refs_5_.refs_8_), channel_id=1, source_target_pairs={{0,1},{1,0},{2,3},{3,2},{4,5},{5,4},{6,7},{7,6},{8,9},{9,8},{10,11... | collective-permute-start | bytes 786440 | tf_op jit(solution)/shard_map/ppermute | solution.py:303
  203.0 4.3 %own_adjoint.14 = (f32[8,128,128]{2,1,0:T(8,128)S(1)}, f32[4,128,128]{2,1,0:T(8,128)S(1)}, f32[4,128,128]{2,1,0:T(8,128)S(1)}, f32[16,128,128]{2,1,0:T(8,128)S(1)}) custom-call(s32[2]{0:T(128)S(1)} %pad_add_fusion.1.first_ref.refs_0_, s32[1,256]{1,0:T(1,128)S(1)} %copy-done.7, s32[3,384]{1,0:T(4,128)S(1)} %pad_add_fusion.refs_2_, ...), custom_call_target="tpu_custom_call" | custom-call | flops 15728640 | bytes 8388608 | tf_op jit(solution)/shard_map/own_adjoint/pallas_call | solution.py:446
  209.4 7.2 %collective-permute-start.31 = (f32[4,128,128]{2,1,0:T(8,128)S(1)}, f32[4,128,128]{2,1,0:T(8,128)}, u32[]{:S(2)}, u32[]{:S(2)}) collective-permute-start(f32[4,128,128]{2,1,0:T(8,128)S(1)} %edge_high.30.refs_7_.refs_5_), channel_id=1, source_target_pairs={{0,1},{1,0},{2,3},{3,2},{4,5},{5,4},{6,7},{7,6},{8,9},{9,8},{10,11... | collective-permute-start | bytes 786440 | tf_op jit(solution)/shard_map/ppermute | solution.py:303
  216.6 1.5 edge_low.30.refs_3_
  218.1 1.3 collective-permute-start.30
  219.5 1.2 copy-done.2
  224.7 4.6 %own_adjoint.15 = (f32[8,128,128]{2,1,0:T(8,128)S(1)}, f32[4,128,128]{2,1,0:T(8,128)S(1)}, f32[4,128,128]{2,1,0:T(8,128)S(1)}, f32[16,128,128]{2,1,0:T(8,128)S(1)}) custom-call(s32[2]{0:T(128)S(1)} %pad_add_fusion.1.first_ref.refs_0_, s32[1,256]{1,0:T(1,128)S(1)} %copy-done.7, s32[3,384]{1,0:T(4,128)S(1)} %pad_add_fusion.refs_2_, ...), custom_call_target="tpu_custom_call" | custom-call | flops 15728640 | bytes 8388608 | tf_op jit(solution)/shard_map/own_adjoint/pallas_call | solution.py:446
  229.3 1.1 edge_high.31.refs_7_.a_high
  230.5 1.2 edge_low.31.a_low
  232.7 1.8 collective-permute-done.32
  234.9 2.7 collective-permute-start.34
  237.6 2.5 collective-permute-start.35
  240.2 4.3 %collective-permute-done.33 = f32[2,128,128]{2,1,0:T(8,128)S(1)} collective-permute-done((f32[2,128,128]{2,1,0:T(8,128)S(1)}, f32[2,128,128]{2,1,0:T(8,128)S(1)}, u32[]{:S(2)}, u32[]{:S(2)}) %collective-permute-start.33) | collective-permute-done | bytes 131104 | tf_op jit(solution)/shard_map/ppermute | solution.py:303
  245.1 3.2 %collective-permute-start.36 = (f32[2,128,128]{2,1,0:T(8,128)S(1)}, f32[2,128,128]{2,1,0:T(8,128)S(1)}, u32[]{:S(2)}, u32[]{:S(2)}) collective-permute-start(f32[2,128,128]{2,1,0:T(8,128)S(1)} %add_add_fusion), channel_id=1, source_target_pairs={{0,128},{16,144},{32,160},{48,176},{64,192},{80,208},{96,224},{112... | collective-permute-start | bytes 393224 | tf_op jit(solution)/shard_map/ppermute | solution.py:303
  248.3 5.8 %collective-permute-done.36 = f32[2,128,128]{2,1,0:T(8,128)S(1)} collective-permute-done((f32[2,128,128]{2,1,0:T(8,128)S(1)}, f32[2,128,128]{2,1,0:T(8,128)S(1)}, u32[]{:S(2)}, u32[]{:S(2)}) %collective-permute-start.36) | collective-permute-done | bytes 131104 | tf_op jit(solution)/shard_map/ppermute | solution.py:303
  254.1 2.0 collective-permute-start.37
  256.2 2.2 collective-permute-start.38
  258.3 1.1 collective-permute-start.39
  259.5 2.2 collective-permute-done.37
  261.7 1.4 collective-permute-done.38
  263.4 1.9 collective-permute-done.40.other_ref
  265.6 7.2 %collective-permute-start.41 = (f32[8,128]{1,0:T(8,128)S(1)}, f32[8,128]{1,0:T(8,128)S(1)}, u32[]{:S(2)}, u32[]{:S(2)}) collective-permute-start(f32[8,128]{1,0:T(8,128)S(1)} %get-tuple-element.282), channel_id=1, source_target_pairs={{0,4},{1,5},{2,6},{3,7},{4,8},{5,9},{6,10},{7,11},{8,12},{9,13},{1... | collective-permute-start | bytes 12296 | tf_op jit(solution)/shard_map/ppermute | solution.py:303
  272.8 8.5 %collective-permute-start.42 = (f32[8,128]{1,0:T(8,128)S(1)}, f32[8,128]{1,0:T(8,128)S(1)}, u32[]{:S(2)}, u32[]{:S(2)}) collective-permute-start(f32[8,128]{1,0:T(8,128)S(1)} %get-tuple-element.282), channel_id=1, source_target_pairs={{0,8},{1,9},{2,10},{3,11},{4,12},{5,13},{6,14},{7,15},{8,0},{9,1},... | collective-permute-start | bytes 12296 | tf_op jit(solution)/shard_map/ppermute | solution.py:303
  281.4 2.5 collective-permute-start.43
  283.9 1.3 collective-permute-done.43
  285.2 1.8 collective-permute-start.44
  287.1 3.5 %collective-permute-start.45 = (f32[8,128]{1,0:T(8,128)S(1)}, f32[8,128]{1,0:T(8,128)S(1)}, u32[]{:S(2)}, u32[]{:S(2)}) collective-permute-start(f32[8,128]{1,0:T(8,128)S(1)} %maximum_maximum_fusion.1), channel_id=1, source_target_pairs={{0,2},{1,3},{2,0},{3,1},{4,6},{5,7},{6,4},{7,5},{8,10},{9,11},{10,... | collective-permute-start | bytes 12296 | tf_op jit(solution)/shard_map/ppermute | solution.py:303
  292.1 2.0 collective-permute-done.46
  294.2 2.1 final.1
  (157 shorter events, 49.7 us)
Async XLA Ops:
  0.6 3.9 %copy-start = (f32[16,128,128]{2,1,0:T(8,128)S(1)}, f32[16,128,128]{2,1,0:T(8,128)}, u32[]{:S(2)}) copy-start(f32[16,128,128]{2,1,0:T(8,128)} %model_ref.1) | copy-start | bytes 3145732
  0.7 1.3 copy-start.3
  2.7 10.8 %collective-permute-start.1 = (f32[4,128,128]{2,1,0:T(8,128)S(1)}, f32[4,128,128]{2,1,0:T(8,128)}, u32[]{:S(2)}, u32[]{:S(2)}) collective-permute-start(f32[4,128,128]{2,1,0:T(8,128)S(1)} %get-tuple-element.146.refs_5_.refs_11_), channel_id=1, source_target_pairs={{0,1},{1,0},{2,3},{3,2},{4,5},{5,4},{6,7},{7,6},{8,9},{9,8},{10,11... | collective-permute-start | bytes 786440 | tf_op jit(solution)/shard_map/ppermute | solution.py:303
  3.0 1.5 copy-start.7
  3.0 16.1 %collective-permute-start = (f32[4,128,128]{2,1,0:T(8,128)S(1)}, f32[4,128,128]{2,1,0:T(8,128)}, u32[]{:S(2)}, u32[]{:S(2)}) collective-permute-start(f32[4,128,128]{2,1,0:T(8,128)S(1)} %get-tuple-element.144.refs_3_.refs_9_), channel_id=1, source_target_pairs={{1,2},{2,1},{3,4},{4,3},{5,6},{6,5},{7,8},{8,7},{9,10},{10,9},{11,... | collective-permute-start | bytes 786440 | tf_op jit(solution)/shard_map/ppermute | solution.py:303
  5.3 1.2 copy-start.4
  12.6 2.0 copy-start.9
  14.6 5.6 %copy-start.16 = (f32[4,128,128]{2,1,0:T(8,128)}, f32[4,128,128]{2,1,0:T(8,128)S(1)}, u32[]{:S(2)}) copy-start(f32[4,128,128]{2,1,0:T(8,128)S(1)} %get-tuple-element.281.b_high) | copy-start | bytes 786436
  14.6 12.1 %collective-permute-start.3 = (f32[4,128,128]{2,1,0:T(8,128)S(1)}, f32[4,128,128]{2,1,0:T(8,128)S(1)}, u32[]{:S(2)}, u32[]{:S(2)}) collective-permute-start(f32[4,128,128]{2,1,0:T(8,128)S(1)} %get-tuple-element.157.refs_7_.refs_8_.refs_11_), channel_id=1, source_target_pairs={{0,1},{1,0},{2,3},{3,2},{4,5},{5,4},{6,7},{7,6},{8,9},{9,8},{10,11... | collective-permute-start | bytes 786440 | tf_op jit(solution)/shard_map/ppermute | solution.py:303
  20.2 6.5 %copy-start.18 = (f32[4,128,128]{2,1,0:T(8,128)}, f32[4,128,128]{2,1,0:T(8,128)S(1)}, u32[]{:S(2)}) copy-start(f32[4,128,128]{2,1,0:T(8,128)S(1)} %get-tuple-element.279.b_low) | copy-start | bytes 786436
  20.2 10.7 %collective-permute-start.2 = (f32[4,128,128]{2,1,0:T(8,128)S(1)}, f32[4,128,128]{2,1,0:T(8,128)S(1)}, u32[]{:S(2)}, u32[]{:S(2)}) collective-permute-start(f32[4,128,128]{2,1,0:T(8,128)S(1)} %get-tuple-element.158.refs_6_.refs_9_), channel_id=1, source_target_pairs={{1,2},{2,1},{3,4},{4,3},{5,6},{6,5},{7,8},{8,7},{9,10},{10,9},{11,... | collective-permute-start | bytes 786440 | tf_op jit(solution)/shard_map/ppermute | solution.py:303
  27.5 4.0 %copy-start.20 = (f32[4,128,128]{2,1,0:T(8,128)}, f32[4,128,128]{2,1,0:T(8,128)S(1)}, u32[]{:S(2)}) copy-start(f32[4,128,128]{2,1,0:T(8,128)S(1)} %get-tuple-element.273.refs_15_) | copy-start | bytes 786436
  27.5 10.3 %collective-permute-start.5 = (f32[4,128,128]{2,1,0:T(8,128)S(1)}, f32[4,128,128]{2,1,0:T(8,128)S(1)}, u32[]{:S(2)}, u32[]{:S(2)}) collective-permute-start(f32[4,128,128]{2,1,0:T(8,128)S(1)} %get-tuple-element.164.refs_7_.refs_8_.refs_11_), channel_id=1, source_target_pairs={{0,1},{1,0},{2,3},{3,2},{4,5},{5,4},{6,7},{7,6},{8,9},{9,8},{10,11... | collective-permute-start | bytes 786440 | tf_op jit(solution)/shard_map/ppermute | solution.py:303
  31.6 5.2 %copy-start.22 = (f32[4,128,128]{2,1,0:T(8,128)}, f32[4,128,128]{2,1,0:T(8,128)S(1)}, u32[]{:S(2)}) copy-start(f32[4,128,128]{2,1,0:T(8,128)S(1)} %get-tuple-element.271.refs_13_) | copy-start | bytes 786436
  31.6 12.9 %collective-permute-start.4 = (f32[4,128,128]{2,1,0:T(8,128)S(1)}, f32[4,128,128]{2,1,0:T(8,128)S(1)}, u32[]{:S(2)}, u32[]{:S(2)}) collective-permute-start(f32[4,128,128]{2,1,0:T(8,128)S(1)} %get-tuple-element.165.refs_6_.refs_9_), channel_id=1, source_target_pairs={{1,2},{2,1},{3,4},{4,3},{5,6},{6,5},{7,8},{8,7},{9,10},{10,9},{11,... | collective-permute-start | bytes 786440 | tf_op jit(solution)/shard_map/ppermute | solution.py:303
  37.8 8.0 %copy-start.5 = (f32[1,16,128,128]{3,2,1,0:T(8,128)S(1)}, f32[1,16,128,128]{3,2,1,0:T(8,128)}, u32[]{:S(2)}) copy-start(f32[1,16,128,128]{3,2,1,0:T(8,128)} %param.14) | copy-start | bytes 3145732
  38.4 13.3 %collective-permute-start.8 = (f32[4,128,128]{2,1,0:T(8,128)S(1)}, f32[4,128,128]{2,1,0:T(8,128)S(1)}, u32[]{:S(2)}, u32[]{:S(2)}) collective-permute-start(f32[4,128,128]{2,1,0:T(8,128)S(1)} %get-tuple-element.171.refs_7_.refs_8_.refs_11_), channel_id=1, source_target_pairs={{0,1},{1,0},{2,3},{3,2},{4,5},{5,4},{6,7},{7,6},{8,9},{9,8},{10,11... | collective-permute-start | bytes 786440 | tf_op jit(solution)/shard_map/ppermute | solution.py:303
  45.1 18.0 %collective-permute-start.7 = (f32[4,128,128]{2,1,0:T(8,128)S(1)}, f32[4,128,128]{2,1,0:T(8,128)S(1)}, u32[]{:S(2)}, u32[]{:S(2)}) collective-permute-start(f32[4,128,128]{2,1,0:T(8,128)S(1)} %get-tuple-element.172.refs_6_.refs_9_), channel_id=1, source_target_pairs={{1,2},{2,1},{3,4},{4,3},{5,6},{6,5},{7,8},{8,7},{9,10},{10,9},{11,... | collective-permute-start | bytes 786440 | tf_op jit(solution)/shard_map/ppermute | solution.py:303
  51.1 13.4 %collective-permute-start.6 = (f32[4,128,128]{2,1,0:T(8,128)S(1)}, f32[4,128,128]{2,1,0:T(8,128)S(1)}, u32[]{:S(2)}, u32[]{:S(2)}) collective-permute-start(f32[4,128,128]{2,1,0:T(8,128)S(1)} %get-tuple-element.175.refs_4_.refs_6_), channel_id=1, source_target_pairs={{1,2},{2,1},{3,4},{4,3},{5,6},{6,5},{7,8},{8,7},{9,10},{10,9},{11,... | collective-permute-start | bytes 786440 | tf_op jit(solution)/shard_map/ppermute | solution.py:303
  52.4 21.2 %collective-permute-start.10 = (f32[4,128,128]{2,1,0:T(8,128)S(1)}, f32[4,128,128]{2,1,0:T(8,128)S(1)}, u32[]{:S(2)}, u32[]{:S(2)}) collective-permute-start(f32[4,128,128]{2,1,0:T(8,128)S(1)} %get-tuple-element.185.refs_7_.refs_8_.refs_11_), channel_id=1, source_target_pairs={{0,1},{1,0},{2,3},{3,2},{4,5},{5,4},{6,7},{7,6},{8,9},{9,8},{10,11... | collective-permute-start | bytes 786440 | tf_op jit(solution)/shard_map/ppermute | solution.py:303
  63.8 22.8 %collective-permute-start.9 = (f32[4,128,128]{2,1,0:T(8,128)S(1)}, f32[4,128,128]{2,1,0:T(8,128)S(1)}, u32[]{:S(2)}, u32[]{:S(2)}) collective-permute-start(f32[4,128,128]{2,1,0:T(8,128)S(1)} %get-tuple-element.186.refs_6_.refs_9_), channel_id=1, source_target_pairs={{1,2},{2,1},{3,4},{4,3},{5,6},{6,5},{7,8},{8,7},{9,10},{10,9},{11,... | collective-permute-start | bytes 786440 | tf_op jit(solution)/shard_map/ppermute | solution.py:303
  74.2 19.8 %collective-permute-start.12 = (f32[4,128,128]{2,1,0:T(8,128)S(1)}, f32[4,128,128]{2,1,0:T(8,128)S(1)}, u32[]{:S(2)}, u32[]{:S(2)}) collective-permute-start(f32[4,128,128]{2,1,0:T(8,128)S(1)} %get-tuple-element.192.refs_7_.refs_8_.refs_11_), channel_id=1, source_target_pairs={{0,1},{1,0},{2,3},{3,2},{4,5},{5,4},{6,7},{7,6},{8,9},{9,8},{10,11... | collective-permute-start | bytes 786440 | tf_op jit(solution)/shard_map/ppermute | solution.py:303
  87.2 8.2 %collective-permute-start.11 = (f32[4,128,128]{2,1,0:T(8,128)S(1)}, f32[4,128,128]{2,1,0:T(8,128)S(1)}, u32[]{:S(2)}, u32[]{:S(2)}) collective-permute-start(f32[4,128,128]{2,1,0:T(8,128)S(1)} %get-tuple-element.193.refs_6_.refs_9_), channel_id=1, source_target_pairs={{1,2},{2,1},{3,4},{4,3},{5,6},{6,5},{7,8},{8,7},{9,10},{10,9},{11,... | collective-permute-start | bytes 786440 | tf_op jit(solution)/shard_map/ppermute | solution.py:303
  92.5 12.9 %collective-permute-start.14 = (f32[4,128,128]{2,1,0:T(8,128)S(1)}, f32[4,128,128]{2,1,0:T(8,128)S(1)}, u32[]{:S(2)}, u32[]{:S(2)}) collective-permute-start(f32[4,128,128]{2,1,0:T(8,128)S(1)} %get-tuple-element.203.refs_6_.refs_8_), channel_id=1, source_target_pairs={{0,1},{1,0},{2,3},{3,2},{4,5},{5,4},{6,7},{7,6},{8,9},{9,8},{10,11... | collective-permute-start | bytes 786440 | tf_op jit(solution)/shard_map/ppermute | solution.py:303
  94.7 17.2 %collective-permute-start.15 = (f32[4,128,128]{2,1,0:T(8,128)S(1)}, f32[4,128,128]{2,1,0:T(8,128)S(1)}, u32[]{:S(2)}, u32[]{:S(2)}) collective-permute-start(f32[4,128,128]{2,1,0:T(8,128)S(1)} %get-tuple-element.199.refs_7_.refs_8_.refs_11_), channel_id=1, source_target_pairs={{0,1},{1,0},{2,3},{3,2},{4,5},{5,4},{6,7},{7,6},{8,9},{9,8},{10,11... | collective-permute-start | bytes 786440 | tf_op jit(solution)/shard_map/ppermute | solution.py:303
  96.1 16.6 %collective-permute-start.13 = (f32[4,128,128]{2,1,0:T(8,128)S(1)}, f32[4,128,128]{2,1,0:T(8,128)S(1)}, u32[]{:S(2)}, u32[]{:S(2)}) collective-permute-start(f32[4,128,128]{2,1,0:T(8,128)S(1)} %get-tuple-element.200.refs_6_.refs_9_), channel_id=1, source_target_pairs={{1,2},{2,1},{3,4},{4,3},{5,6},{6,5},{7,8},{8,7},{9,10},{10,9},{11,... | collective-permute-start | bytes 786440 | tf_op jit(solution)/shard_map/ppermute | solution.py:303
  111.9 2.3 copy-start.6
  112.5 9.7 %collective-permute-start.17 = (f32[4,128,128]{2,1,0:T(8,128)S(1)}, f32[4,128,128]{2,1,0:T(8,128)S(1)}, u32[]{:S(2)}, u32[]{:S(2)}) collective-permute-start(f32[4,128,128]{2,1,0:T(8,128)S(1)} %get-tuple-element.208.refs_7_.refs_8_), channel_id=1, source_target_pairs={{0,1},{1,0},{2,3},{3,2},{4,5},{5,4},{6,7},{7,6},{8,9},{9,8},{10,11... | collective-permute-start | bytes 786440 | tf_op jit(solution)/shard_map/ppermute | solution.py:303
  113.3 9.6 %collective-permute-start.16 = (f32[4,128,128]{2,1,0:T(8,128)S(1)}, f32[4,128,128]{2,1,0:T(8,128)S(1)}, u32[]{:S(2)}, u32[]{:S(2)}) collective-permute-start(f32[4,128,128]{2,1,0:T(8,128)S(1)} %get-tuple-element.209.refs_6_), channel_id=1, source_target_pairs={{1,2},{2,1},{3,4},{4,3},{5,6},{6,5},{7,8},{8,7},{9,10},{10,9},{11,... | collective-permute-start | bytes 786440 | tf_op jit(solution)/shard_map/ppermute | solution.py:303
  129.0 15.9 %collective-permute-start.19 = (f32[4,128,128]{2,1,0:T(8,128)S(1)}, f32[4,128,128]{2,1,0:T(8,128)S(1)}, u32[]{:S(2)}, u32[]{:S(2)}) collective-permute-start(f32[4,128,128]{2,1,0:T(8,128)S(1)} %edge_high.24.refs_7_.refs_5_.refs_8_), channel_id=1, source_target_pairs={{0,1},{1,0},{2,3},{3,2},{4,5},{5,4},{6,7},{7,6},{8,9},{9,8},{10,11... | collective-permute-start | bytes 786440 | tf_op jit(solution)/shard_map/ppermute | solution.py:303
  139.7 8.1 %collective-permute-start.18 = (f32[4,128,128]{2,1,0:T(8,128)S(1)}, f32[4,128,128]{2,1,0:T(8,128)S(1)}, u32[]{:S(2)}, u32[]{:S(2)}) collective-permute-start(f32[4,128,128]{2,1,0:T(8,128)S(1)} %edge_low.24.refs_3_.refs_6_), channel_id=1, source_target_pairs={{1,2},{2,1},{3,4},{4,3},{5,6},{6,5},{7,8},{8,7},{9,10},{10,9},{11,... | collective-permute-start | bytes 786440 | tf_op jit(solution)/shard_map/ppermute | solution.py:303
  145.7 9.6 %collective-permute-start.21 = (f32[4,128,128]{2,1,0:T(8,128)S(1)}, f32[4,128,128]{2,1,0:T(8,128)S(1)}, u32[]{:S(2)}, u32[]{:S(2)}) collective-permute-start(f32[4,128,128]{2,1,0:T(8,128)S(1)} %edge_high.25.refs_7_.refs_5_.refs_8_), channel_id=1, source_target_pairs={{0,1},{1,0},{2,3},{3,2},{4,5},{5,4},{6,7},{7,6},{8,9},{9,8},{10,11... | collective-permute-start | bytes 786440 | tf_op jit(solution)/shard_map/ppermute | solution.py:303
  148.5 12.4 %collective-permute-start.20 = (f32[4,128,128]{2,1,0:T(8,128)S(1)}, f32[4,128,128]{2,1,0:T(8,128)S(1)}, u32[]{:S(2)}, u32[]{:S(2)}) collective-permute-start(f32[4,128,128]{2,1,0:T(8,128)S(1)} %edge_low.25.refs_3_.refs_6_), channel_id=1, source_target_pairs={{1,2},{2,1},{3,4},{4,3},{5,6},{6,5},{7,8},{8,7},{9,10},{10,9},{11,... | collective-permute-start | bytes 786440 | tf_op jit(solution)/shard_map/ppermute | solution.py:303
  156.1 11.5 %collective-permute-start.23 = (f32[4,128,128]{2,1,0:T(8,128)S(1)}, f32[4,128,128]{2,1,0:T(8,128)S(1)}, u32[]{:S(2)}, u32[]{:S(2)}) collective-permute-start(f32[4,128,128]{2,1,0:T(8,128)S(1)} %edge_high.26.refs_7_.refs_5_.refs_8_), channel_id=1, source_target_pairs={{0,1},{1,0},{2,3},{3,2},{4,5},{5,4},{6,7},{7,6},{8,9},{9,8},{10,11... | collective-permute-start | bytes 786440 | tf_op jit(solution)/shard_map/ppermute | solution.py:303
  161.7 12.7 %collective-permute-start.22 = (f32[4,128,128]{2,1,0:T(8,128)S(1)}, f32[4,128,128]{2,1,0:T(8,128)S(1)}, u32[]{:S(2)}, u32[]{:S(2)}) collective-permute-start(f32[4,128,128]{2,1,0:T(8,128)S(1)} %edge_low.26.refs_3_.refs_6_), channel_id=1, source_target_pairs={{1,2},{2,1},{3,4},{4,3},{5,6},{6,5},{7,8},{8,7},{9,10},{10,9},{11,... | collective-permute-start | bytes 786440 | tf_op jit(solution)/shard_map/ppermute | solution.py:303
  168.4 12.4 %collective-permute-start.25 = (f32[4,128,128]{2,1,0:T(8,128)S(1)}, f32[4,128,128]{2,1,0:T(8,128)S(1)}, u32[]{:S(2)}, u32[]{:S(2)}) collective-permute-start(f32[4,128,128]{2,1,0:T(8,128)S(1)} %edge_high.27.refs_7_.refs_5_.refs_8_), channel_id=1, source_target_pairs={{0,1},{1,0},{2,3},{3,2},{4,5},{5,4},{6,7},{7,6},{8,9},{9,8},{10,11... | collective-permute-start | bytes 786440 | tf_op jit(solution)/shard_map/ppermute | solution.py:303
  175.2 12.0 %collective-permute-start.24 = (f32[4,128,128]{2,1,0:T(8,128)S(1)}, f32[4,128,128]{2,1,0:T(8,128)S(1)}, u32[]{:S(2)}, u32[]{:S(2)}) collective-permute-start(f32[4,128,128]{2,1,0:T(8,128)S(1)} %edge_low.27.refs_3_.refs_6_), channel_id=1, source_target_pairs={{1,2},{2,1},{3,4},{4,3},{5,6},{6,5},{7,8},{8,7},{9,10},{10,9},{11,... | collective-permute-start | bytes 786440 | tf_op jit(solution)/shard_map/ppermute | solution.py:303
  181.5 12.8 %collective-permute-start.27 = (f32[4,128,128]{2,1,0:T(8,128)S(1)}, f32[4,128,128]{2,1,0:T(8,128)S(1)}, u32[]{:S(2)}, u32[]{:S(2)}) collective-permute-start(f32[4,128,128]{2,1,0:T(8,128)S(1)} %edge_high.28.refs_7_.refs_5_.refs_8_), channel_id=1, source_target_pairs={{0,1},{1,0},{2,3},{3,2},{4,5},{5,4},{6,7},{7,6},{8,9},{9,8},{10,11... | collective-permute-start | bytes 786440 | tf_op jit(solution)/shard_map/ppermute | solution.py:303
  187.9 13.6 %collective-permute-start.26 = (f32[4,128,128]{2,1,0:T(8,128)S(1)}, f32[4,128,128]{2,1,0:T(8,128)S(1)}, u32[]{:S(2)}, u32[]{:S(2)}) collective-permute-start(f32[4,128,128]{2,1,0:T(8,128)S(1)} %edge_low.28.refs_3_.refs_6_), channel_id=1, source_target_pairs={{1,2},{2,1},{3,4},{4,3},{5,6},{6,5},{7,8},{8,7},{9,10},{10,9},{11,... | collective-permute-start | bytes 786440 | tf_op jit(solution)/shard_map/ppermute | solution.py:303
  195.1 13.6 %collective-permute-start.29 = (f32[4,128,128]{2,1,0:T(8,128)S(1)}, f32[4,128,128]{2,1,0:T(8,128)S(1)}, u32[]{:S(2)}, u32[]{:S(2)}) collective-permute-start(f32[4,128,128]{2,1,0:T(8,128)S(1)} %edge_high.29.refs_7_.refs_5_.refs_8_), channel_id=1, source_target_pairs={{0,1},{1,0},{2,3},{3,2},{4,5},{5,4},{6,7},{7,6},{8,9},{9,8},{10,11... | collective-permute-start | bytes 786440 | tf_op jit(solution)/shard_map/ppermute | solution.py:303
  202.3 14.3 %collective-permute-start.28 = (f32[4,128,128]{2,1,0:T(8,128)S(1)}, f32[4,128,128]{2,1,0:T(8,128)S(1)}, u32[]{:S(2)}, u32[]{:S(2)}) collective-permute-start(f32[4,128,128]{2,1,0:T(8,128)S(1)} %edge_low.29.refs_3_.refs_6_), channel_id=1, source_target_pairs={{1,2},{2,1},{3,4},{4,3},{5,6},{6,5},{7,8},{8,7},{9,10},{10,9},{11,... | collective-permute-start | bytes 786440 | tf_op jit(solution)/shard_map/ppermute | solution.py:303
  208.1 10.0 %copy-start.1 = (f32[16,128,128]{2,1,0:T(8,128)}, f32[16,128,128]{2,1,0:T(8,128)S(1)}, u32[]{:S(2)}) copy-start(f32[16,128,128]{2,1,0:T(8,128)S(1)} %get-tuple-element.274.refs_16_) | copy-start | bytes 3145732
  209.4 19.9 %collective-permute-start.31 = (f32[4,128,128]{2,1,0:T(8,128)S(1)}, f32[4,128,128]{2,1,0:T(8,128)}, u32[]{:S(2)}, u32[]{:S(2)}) collective-permute-start(f32[4,128,128]{2,1,0:T(8,128)S(1)} %edge_high.30.refs_7_.refs_5_), channel_id=1, source_target_pairs={{0,1},{1,0},{2,3},{3,2},{4,5},{5,4},{6,7},{7,6},{8,9},{9,8},{10,11... | collective-permute-start | bytes 786440 | tf_op jit(solution)/shard_map/ppermute | solution.py:303
  218.1 12.3 %collective-permute-start.30 = (f32[4,128,128]{2,1,0:T(8,128)}, f32[4,128,128]{2,1,0:T(8,128)}, u32[]{:S(2)}, u32[]{:S(2)}) collective-permute-start(f32[4,128,128]{2,1,0:T(8,128)} %edge_low.30.refs_3_), channel_id=1, source_target_pairs={{1,2},{2,1},{3,4},{4,3},{5,6},{6,5},{7,8},{8,7},{9,10},{10,9},{11,... | collective-permute-start | bytes 786440 | tf_op jit(solution)/shard_map/ppermute | solution.py:303
  219.5 1.2 copy-start.2
  220.7 1.0 copy-start.12
  230.4 1.2 copy-start.10
  230.4 1.2 copy-start.17
  230.4 1.2 copy-start.19
  232.5 2.0 collective-permute-start.32
  234.6 9.9 %collective-permute-start.33 = (f32[2,128,128]{2,1,0:T(8,128)S(1)}, f32[2,128,128]{2,1,0:T(8,128)S(1)}, u32[]{:S(2)}, u32[]{:S(2)}) collective-permute-start(f32[2,128,128]{2,1,0:T(8,128)S(1)} %get-tuple-element.288), channel_id=1, source_target_pairs={{0,32},{16,48},{32,64},{48,80},{64,96},{80,112},{96,0},{112,16},{1... | collective-permute-start | bytes 393224 | tf_op jit(solution)/shard_map/ppermute | solution.py:303
  234.9 9.5 %collective-permute-start.34 = (f32[2,128,128]{2,1,0:T(8,128)S(1)}, f32[2,128,128]{2,1,0:T(8,128)S(1)}, u32[]{:S(2)}, u32[]{:S(2)}) collective-permute-start(f32[2,128,128]{2,1,0:T(8,128)S(1)} %get-tuple-element.290), channel_id=1, source_target_pairs={{0,64},{16,80},{32,96},{48,112},{64,0},{80,16},{96,32},{112,48},{1... | collective-permute-start | bytes 393224 | tf_op jit(solution)/shard_map/ppermute | solution.py:303
  237.6 7.4 %collective-permute-start.35 = (f32[2,128,128]{2,1,0:T(8,128)S(1)}, f32[2,128,128]{2,1,0:T(8,128)S(1)}, u32[]{:S(2)}, u32[]{:S(2)}) collective-permute-start(f32[2,128,128]{2,1,0:T(8,128)S(1)} %get-tuple-element.289), channel_id=1, source_target_pairs={{0,96},{16,112},{32,0},{48,16},{64,32},{80,48},{96,64},{112,80},{1... | collective-permute-start | bytes 393224 | tf_op jit(solution)/shard_map/ppermute | solution.py:303
  245.1 9.0 %collective-permute-start.36 = (f32[2,128,128]{2,1,0:T(8,128)S(1)}, f32[2,128,128]{2,1,0:T(8,128)S(1)}, u32[]{:S(2)}, u32[]{:S(2)}) collective-permute-start(f32[2,128,128]{2,1,0:T(8,128)S(1)} %add_add_fusion), channel_id=1, source_target_pairs={{0,128},{16,144},{32,160},{48,176},{64,192},{80,208},{96,224},{112... | collective-permute-start | bytes 393224 | tf_op jit(solution)/shard_map/ppermute | solution.py:303
  254.1 7.6 %collective-permute-start.37 = (f32[2,128,128]{2,1,0:T(8,128)S(1)}, f32[2,128,128]{2,1,0:T(8,128)S(1)}, u32[]{:S(2)}, u32[]{:S(2)}) collective-permute-start(f32[2,128,128]{2,1,0:T(8,128)S(1)} %get-tuple-element.285), channel_id=1, source_target_pairs={{0,32},{16,48},{32,64},{48,80},{64,96},{80,112},{96,0},{112,16},{1... | collective-permute-start | bytes 393224 | tf_op jit(solution)/shard_map/ppermute | solution.py:303
  256.2 7.0 %collective-permute-start.38 = (f32[2,128,128]{2,1,0:T(8,128)S(1)}, f32[2,128,128]{2,1,0:T(8,128)S(1)}, u32[]{:S(2)}, u32[]{:S(2)}) collective-permute-start(f32[2,128,128]{2,1,0:T(8,128)S(1)} %get-tuple-element.285), channel_id=1, source_target_pairs={{0,64},{16,80},{32,96},{48,112},{64,0},{80,16},{96,32},{112,48},{1... | collective-permute-start | bytes 393224 | tf_op jit(solution)/shard_map/ppermute | solution.py:303
  258.3 5.0 %collective-permute-start.39 = (f32[2,128,128]{2,1,0:T(8,128)S(1)}, f32[2,128,128]{2,1,0:T(8,128)S(1)}, u32[]{:S(2)}, u32[]{:S(2)}) collective-permute-start(f32[2,128,128]{2,1,0:T(8,128)S(1)} %get-tuple-element.285), channel_id=1, source_target_pairs={{0,96},{16,112},{32,0},{48,16},{64,32},{80,48},{96,64},{112,80},{1... | collective-permute-start | bytes 393224 | tf_op jit(solution)/shard_map/ppermute | solution.py:303
  263.3 2.0 collective-permute-start.40
  265.6 18.3 %collective-permute-start.41 = (f32[8,128]{1,0:T(8,128)S(1)}, f32[8,128]{1,0:T(8,128)S(1)}, u32[]{:S(2)}, u32[]{:S(2)}) collective-permute-start(f32[8,128]{1,0:T(8,128)S(1)} %get-tuple-element.282), channel_id=1, source_target_pairs={{0,4},{1,5},{2,6},{3,7},{4,8},{5,9},{6,10},{7,11},{8,12},{9,13},{1... | collective-permute-start | bytes 12296 | tf_op jit(solution)/shard_map/ppermute | solution.py:303
  272.8 11.1 %collective-permute-start.42 = (f32[8,128]{1,0:T(8,128)S(1)}, f32[8,128]{1,0:T(8,128)S(1)}, u32[]{:S(2)}, u32[]{:S(2)}) collective-permute-start(f32[8,128]{1,0:T(8,128)S(1)} %get-tuple-element.282), channel_id=1, source_target_pairs={{0,8},{1,9},{2,10},{3,11},{4,12},{5,13},{6,14},{7,15},{8,0},{9,1},... | collective-permute-start | bytes 12296 | tf_op jit(solution)/shard_map/ppermute | solution.py:303
  281.4 3.9 %collective-permute-start.43 = (f32[8,128]{1,0:T(8,128)S(1)}, f32[8,128]{1,0:T(8,128)S(1)}, u32[]{:S(2)}, u32[]{:S(2)}) collective-permute-start(f32[8,128]{1,0:T(8,128)S(1)} %get-tuple-element.282), channel_id=1, source_target_pairs={{0,12},{1,13},{2,14},{3,15},{4,0},{5,1},{6,2},{7,3},{8,4},{9,5},{1... | collective-permute-start | bytes 12296 | tf_op jit(solution)/shard_map/ppermute | solution.py:303
  285.2 6.3 %collective-permute-start.44 = (f32[8,128]{1,0:T(8,128)S(1)}, f32[8,128]{1,0:T(8,128)S(1)}, u32[]{:S(2)}, u32[]{:S(2)}) collective-permute-start(f32[8,128]{1,0:T(8,128)S(1)} %maximum_maximum_fusion.1), channel_id=1, source_target_pairs={{0,1},{1,2},{2,3},{3,0},{4,5},{5,6},{6,7},{7,4},{8,9},{9,10},{10,1... | collective-permute-start | bytes 12296 | tf_op jit(solution)/shard_map/ppermute | solution.py:303
  287.1 5.1 %collective-permute-start.45 = (f32[8,128]{1,0:T(8,128)S(1)}, f32[8,128]{1,0:T(8,128)S(1)}, u32[]{:S(2)}, u32[]{:S(2)}) collective-permute-start(f32[8,128]{1,0:T(8,128)S(1)} %maximum_maximum_fusion.1), channel_id=1, source_target_pairs={{0,2},{1,3},{2,0},{3,1},{4,6},{5,7},{6,4},{7,5},{8,10},{9,11},{10,... | collective-permute-start | bytes 12296 | tf_op jit(solution)/shard_map/ppermute | solution.py:303
  290.6 3.6 %collective-permute-start.46 = (f32[8,128]{1,0:T(8,128)S(1)}, f32[8,128]{1,0:T(8,128)S(1)}, u32[]{:S(2)}, u32[]{:S(2)}) collective-permute-start(f32[8,128]{1,0:T(8,128)S(1)} %maximum_maximum_fusion.1), channel_id=1, source_target_pairs={{0,3},{1,0},{2,1},{3,2},{4,7},{5,4},{6,5},{7,6},{8,11},{9,8},{10,9... | collective-permute-start | bytes 12296 | tf_op jit(solution)/shard_map/ppermute | solution.py:303
  (9 other events, 7.3 us)

commit v4 on v2

--- a/solution.py
+++ b/solution.py
@@ -153,28 +153,34 @@
         start += count
 
 
-def laplace_rows(pad_ref, plane, row, lane_weights):
+def lane_matrix():
+    away = jnp.abs(lax.broadcasted_iota(jnp.int32, (NZ, NZ), 0) - lax.broadcasted_iota(jnp.int32, (NZ, NZ), 1))
+    out = jnp.zeros((NZ, NZ), jnp.float32)
+    for k, weight in enumerate((8064.0, -1008.0, 128.0, -9.0)):
+        out = jnp.where(away == k + 1, weight, out)
+    return out.astype(jnp.bfloat16)
+
+
+def lane_terms(plane, matrix):
+    total = None
+    for piece in range(3):
+        part = plane.astype(jnp.bfloat16)
+        plane = plane - part.astype(jnp.float32)
+        term = jnp.dot(part, matrix, preferred_element_type=jnp.float32)
+        total = term if total is None else total + term
+    return total * (1.0 / 5040.0)
+
+
+def laplace_rows(pad_ref, plane, row, along):
     at = plane + EDGE
     field = pad_ref[at, pl.ds(8 + row, SLICE), :]
-    total = (3.0 * CENTRE) * field
+    total = (3.0 * CENTRE) * field + along[row : row + SLICE]
     for index, weight in enumerate(COEFFS):
         k = index + 1
         pair = pad_ref[at + k, pl.ds(8 + row, SLICE), :] + pad_ref[at - k, pl.ds(8 + row, SLICE), :]
         pair = pair + (pad_ref[at, pl.ds(8 + row + k, SLICE), :] + pad_ref[at, pl.ds(8 + row - k, SLICE), :])
         total = total + weight * pair
-        total = total + lane_weights[2 * index] * pltpu.roll(field, NZ - k, 1)
-        total = total + lane_weights[2 * index + 1] * pltpu.roll(field, k, 1)
     return field, total
-
-
-def make_lane_weights():
-    lane = lax.broadcasted_iota(jnp.int32, (SLICE, NZ), 1)
-    out = []
-    for index, weight in enumerate(COEFFS):
-        k = index + 1
-        out.append(jnp.where(lane < NZ - k, weight, 0.0))
-        out.append(jnp.where(lane >= k, weight, 0.0))
-    return out
 
 
 def own_kernel(forward, tick, has_extra, *refs):
@@ -207,14 +213,15 @@
     pad_ref = take(1)[0]
 
     fill_padded(pad_ref, *cur)
-    weights = make_lane_weights()
+    matrix = lane_matrix()
     outs = (base_lo, next_mid, base_hi)
     low = 0
     for region, count in enumerate((EDGE, MID, EDGE)):
 
         def body(i, carry, region=region, low=low):
+            along = lane_terms(cur[region][i], matrix)
             for row in range(0, NY, SLICE):
-                field, total = laplace_rows(pad_ref, low + i, row, weights)
+                field, total = laplace_rows(pad_ref, low + i, row, along)
                 rows = pl.ds(row, SLICE)
                 value = 2.0 * field - old[region][i, rows, :] + model[region][i, rows, :] * total
                 outs[region][i, rows, :] = value

time: 295 us -> 293 us (level)
  starting transfers between devices: 128 us -> 138 us
  waiting for transfers between devices: 43.2 us -> 33.2 us
  Pallas kernels: 106 us -> 103 us
    ppermute x47, starting transfers between devices: 128 us -> 138 us  [swap(): return lax.ppermute(value, axis, pairs)]
    ppermute x47, waiting for transfers between devices: 43.2 us -> 33.2 us  [swap(): return lax.ppermute(value, axis, pairs)]
  transfers between devices with their start and end apart: 47 -> 47, of which waited for: 20 -> 23; matrix products, arithmetic and copies ran while one was open for 0% -> 0% of each run, Pallas kernels for 35% -> 35%
where the time goes in v4:
time: 293 us; the launch traced here: 290 us
  starting transfers between devices  138 us (47%)
  Pallas kernels  103 us (35%)
  waiting for transfers between devices  33.2 us (11%)
  local copies, waits for them, and re-layouts  10.3 us (4%)
  other arithmetic  3.16 us (1%)
  between operations  2.96 us (1%)
    ppermute x47, starting transfers between devices, swap(): return lax.ppermute(value, axis, pairs)  138 us
    pallas_call x8, Pallas kernels, on_device(): call(functools.partial(own_kernel, True, tick, False), outs, pad, [SMEM]...  34.4 us
    ppermute x47, waiting for transfers between devices, swap(): return lax.ppermute(value, axis, pairs)  33.2 us
    pallas_call x8, Pallas kernels, on_device(): call(functools.partial(own_kernel, False, tick, not top), outs, pad, [SME...  33.1 us
    pallas_call x32, Pallas kernels, edges(): call(functools.partial(edge_kernel, forward, tick, high), [planes(EDGE)]...  24.6 us
    unnamed x48, local copies, waits for them, and re-layouts  8.98 us
    pallas_call x1, Pallas kernels, on_device(): call(sort_kernel, jax.ShapeDtypeStruct((4, REC + 128), jnp.int32), [], [S...  6.46 us
  transfers between devices with their start and end apart: 47, of which 23 were waited for; matrix products, arithmetic and copies ran while one was open for 0% of the time, Pallas kernels for 35%

profile of v4, /device:TPU:0, one launch (start us, length us, event | category | flops | bytes accessed | tf_op | source)
XLA Modules:
  0.0 290.4 jit_solution(7483752686145677787)
XLA Ops:
  0.7 1.3 copy-done.3
  6.5 3.8 %own_forward.8 = (f32[8,128,128]{2,1,0:T(8,128)S(1)}, f32[4,128,128]{2,1,0:T(8,128)S(1)}, f32[4,128,128]{2,1,0:T(8,128)S(1)}, f32[4,128,128]{2,1,0:T(8,128)S(1)}...) custom-call(s32[2]{0:T(128)S(1)} %pad_add_fusion.first_ref.refs_0_, s32[1]{0:T(128)S(6)} %copy.15.refs_1_.refs_3_, ...), custom_call_target="tpu_custom_call" | custom-call | flops 15728640 | bytes 8388608 | tf_op jit(solution)/shard_map/own_forward/pallas_call | solution.py:407
  11.8 5.1 %collective-permute-start.4 = (f32[4,128,128]{2,1,0:T(8,128)S(1)}, f32[4,128,128]{2,1,0:T(8,128)S(1)}, u32[]{:S(2)}, u32[]{:S(2)}) collective-permute-start(f32[4,128,128]{2,1,0:T(8,128)S(1)} %get-tuple-element.156.refs_7_.refs_8_.refs_11_), channel_id=1, source_target_pairs={{0,1},{1,0},{2,3},{3,2},{4,5},{5,4},{6,7},{7,6},{8,9},{9,8},{10,11... | collective-permute-start | bytes 786440 | tf_op jit(solution)/shard_map/ppermute | solution.py:292
  18.4 6.5 %sort_receivers.1.refs_2_ = s32[4,384]{1,0:T(4,128)S(1)} custom-call(s32[2]{0:T(128)S(1)} %pad_add_fusion.first_ref.refs_0_, s32[1,256]{1,0:T(1,128)S(1)} %copy-done.7), custom_call_target="tpu_custom_call" | custom-call | flops 1000 | bytes 4096 | tf_op jit(solution)/shard_map/sort_receivers/pallas_call | solution.py:356
  24.9 4.4 %own_forward.9 = (f32[8,128,128]{2,1,0:T(8,128)S(1)}, f32[4,128,128]{2,1,0:T(8,128)S(1)}, f32[4,128,128]{2,1,0:T(8,128)S(1)}, f32[4,128,128]{2,1,0:T(8,128)S(1)}...) custom-call(s32[2]{0:T(128)S(1)} %pad_add_fusion.first_ref.refs_0_, ...), custom_call_target="tpu_custom_call" | custom-call | flops 15728640 | bytes 8388608 | tf_op jit(solution)/shard_map/own_forward/pallas_call | solution.py:407
  30.1 4.7 %collective-permute-start.6 = (f32[4,128,128]{2,1,0:T(8,128)S(1)}, f32[4,128,128]{2,1,0:T(8,128)S(1)}, u32[]{:S(2)}, u32[]{:S(2)}) collective-permute-start(f32[4,128,128]{2,1,0:T(8,128)S(1)} %get-tuple-element.163.refs_7_.refs_8_.refs_11_), channel_id=1, source_target_pairs={{0,1},{1,0},{2,3},{3,2},{4,5},{5,4},{6,7},{7,6},{8,9},{9,8},{10,11... | collective-permute-start | bytes 786440 | tf_op jit(solution)/shard_map/ppermute | solution.py:292
  36.2 4.4 %own_forward.10 = (f32[8,128,128]{2,1,0:T(8,128)S(1)}, f32[4,128,128]{2,1,0:T(8,128)S(1)}, f32[4,128,128]{2,1,0:T(8,128)S(1)}, f32[4,128,128]{2,1,0:T(8,128)S(1)...) custom-call(s32[2]{0:T(128)S(1)} %pad_add_fusion.first_ref.refs_0_, ...), custom_call_target="tpu_custom_call" | custom-call | flops 15728640 | bytes 8388608 | tf_op jit(solution)/shard_map/own_forward/pallas_call | solution.py:407
  41.2 4.6 %collective-permute-start.8 = (f32[4,128,128]{2,1,0:T(8,128)S(1)}, f32[4,128,128]{2,1,0:T(8,128)S(1)}, u32[]{:S(2)}, u32[]{:S(2)}) collective-permute-start(f32[4,128,128]{2,1,0:T(8,128)S(1)} %get-tuple-element.170.refs_7_.refs_8_.refs_11_), channel_id=1, source_target_pairs={{0,1},{1,0},{2,3},{3,2},{4,5},{5,4},{6,7},{7,6},{8,9},{9,8},{10,11... | collective-permute-start | bytes 786440 | tf_op jit(solution)/shard_map/ppermute | solution.py:292
  47.2 4.4 %own_forward.11 = (f32[8,128,128]{2,1,0:T(8,128)S(1)}, f32[4,128,128]{2,1,0:T(8,128)S(1)}, f32[4,128,128]{2,1,0:T(8,128)S(1)}, f32[4,128,128]{2,1,0:T(8,128)S(1)...) custom-call(s32[2]{0:T(128)S(1)} %pad_add_fusion.first_ref.refs_0_, ...), custom_call_target="tpu_custom_call" | custom-call | flops 15728640 | bytes 8388608 | tf_op jit(solution)/shard_map/own_forward/pallas_call | solution.py:407
  51.5 2.9 collective-permute-done.8.refs_3_
  55.0 4.2 %collective-permute-start.10 = (f32[4,128,128]{2,1,0:T(8,128)S(1)}, f32[4,128,128]{2,1,0:T(8,128)S(1)}, u32[]{:S(2)}, u32[]{:S(2)}) collective-permute-start(f32[4,128,128]{2,1,0:T(8,128)S(1)} %get-tuple-element.177.refs_7_.refs_8_.refs_11_), channel_id=1, source_target_pairs={{0,1},{1,0},{2,3},{3,2},{4,5},{5,4},{6,7},{7,6},{8,9},{9,8},{10,11... | collective-permute-start | bytes 786440 | tf_op jit(solution)/shard_map/ppermute | solution.py:292
  60.6 4.4 %own_forward.12 = (f32[8,128,128]{2,1,0:T(8,128)S(1)}, f32[4,128,128]{2,1,0:T(8,128)S(1)}, f32[4,128,128]{2,1,0:T(8,128)S(1)}, f32[4,128,128]{2,1,0:T(8,128)S(1)...) custom-call(s32[2]{0:T(128)S(1)} %pad_add_fusion.first_ref.refs_0_, ...), custom_call_target="tpu_custom_call" | custom-call | flops 15728640 | bytes 8388608 | tf_op jit(solution)/shard_map/own_forward/pallas_call | solution.py:407
  65.0 1.6 collective-permute-done.10.refs_3_
  67.3 6.4 %collective-permute-start.12 = (f32[4,128,128]{2,1,0:T(8,128)S(1)}, f32[4,128,128]{2,1,0:T(8,128)S(1)}, u32[]{:S(2)}, u32[]{:S(2)}) collective-permute-start(f32[4,128,128]{2,1,0:T(8,128)S(1)} %get-tuple-element.184.refs_7_.refs_8_.refs_11_), channel_id=1, source_target_pairs={{0,1},{1,0},{2,3},{3,2},{4,5},{5,4},{6,7},{7,6},{8,9},{9,8},{10,11... | collective-permute-start | bytes 786440 | tf_op jit(solution)/shard_map/ppermute | solution.py:292
  75.0 4.4 %own_forward.13 = (f32[8,128,128]{2,1,0:T(8,128)S(1)}, f32[4,128,128]{2,1,0:T(8,128)S(1)}, f32[4,128,128]{2,1,0:T(8,128)S(1)}, f32[4,128,128]{2,1,0:T(8,128)S(1)...) custom-call(s32[2]{0:T(128)S(1)} %pad_add_fusion.first_ref.refs_0_, ...), custom_call_target="tpu_custom_call" | custom-call | flops 15728640 | bytes 8388608 | tf_op jit(solution)/shard_map/own_forward/pallas_call | solution.py:407
  80.8 6.4 %collective-permute-start.14 = (f32[4,128,128]{2,1,0:T(8,128)S(1)}, f32[4,128,128]{2,1,0:T(8,128)S(1)}, u32[]{:S(2)}, u32[]{:S(2)}) collective-permute-start(f32[4,128,128]{2,1,0:T(8,128)S(1)} %get-tuple-element.191.refs_7_.refs_8_.refs_11_), channel_id=1, source_target_pairs={{0,1},{1,0},{2,3},{3,2},{4,5},{5,4},{6,7},{7,6},{8,9},{9,8},{10,11... | collective-permute-start | bytes 786440 | tf_op jit(solution)/shard_map/ppermute | solution.py:292
  88.6 4.4 %own_forward.14 = (f32[8,128,128]{2,1,0:T(8,128)S(1)}, f32[4,128,128]{2,1,0:T(8,128)S(1)}, f32[4,128,128]{2,1,0:T(8,128)S(1)}, f32[4,128,128]{2,1,0:T(8,128)S(1)...) custom-call(s32[2]{0:T(128)S(1)} %pad_add_fusion.first_ref.refs_0_, ...), custom_call_target="tpu_custom_call" | custom-call | flops 15728640 | bytes 8388608 | tf_op jit(solution)/shard_map/own_forward/pallas_call | solution.py:407
  94.4 7.5 %collective-permute-start.16 = (f32[4,128,128]{2,1,0:T(8,128)S(1)}, f32[4,128,128]{2,1,0:T(8,128)S(1)}, u32[]{:S(2)}, u32[]{:S(2)}) collective-permute-start(f32[4,128,128]{2,1,0:T(8,128)S(1)} %get-tuple-element.198.refs_7_.refs_8_), channel_id=1, source_target_pairs={{0,1},{1,0},{2,3},{3,2},{4,5},{5,4},{6,7},{7,6},{8,9},{9,8},{10,11... | collective-permute-start | bytes 786440 | tf_op jit(solution)/shard_map/ppermute | solution.py:292
  104.0 7.1 %collective-permute-start.17 = (f32[4,128,128]{2,1,0:T(8,128)S(1)}, f32[4,128,128]{2,1,0:T(8,128)S(1)}, u32[]{:S(2)}, u32[]{:S(2)}) collective-permute-start(f32[4,128,128]{2,1,0:T(8,128)S(1)} %get-tuple-element.139.refs_6_.refs_8_), channel_id=1, source_target_pairs={{0,1},{1,0},{2,3},{3,2},{4,5},{5,4},{6,7},{7,6},{8,9},{9,8},{10,11... | collective-permute-start | bytes 786440 | tf_op jit(solution)/shard_map/ppermute | solution.py:292
  112.5 4.4 %own_forward.15 = (f32[8,128,128]{2,1,0:T(8,128)S(1)}, f32[4,128,128]{2,1,0:T(8,128)S(1)}, f32[4,128,128]{2,1,0:T(8,128)S(1)}, f32[4,128,128]{2,1,0:T(8,128)S(1)...) custom-call(s32[2]{0:T(128)S(1)} %pad_add_fusion.first_ref.refs_0_, ...), custom_call_target="tpu_custom_call" | custom-call | flops 15728640 | bytes 8388608 | tf_op jit(solution)/shard_map/own_forward/pallas_call | solution.py:407
  118.4 4.4 %own_adjoint.8 = (f32[8,128,128]{2,1,0:T(8,128)S(1)}, f32[4,128,128]{2,1,0:T(8,128)S(1)}, f32[4,128,128]{2,1,0:T(8,128)S(1)}, f32[256,128]{1,0:T(8,128)S(1)}, f32[16,128,128]{2,1,0:T(8,128)S(1)}) custom-call(s32[2]{0:T(128)S(1)} %pad_add_fusion.first_ref.refs_0_, s32[1,256]{1,0:T(1,128)S(1)} %copy-done.7, s32[4,384]{1,0:T(4,128)S(1)} %sort_receivers.1.refs_2_, ...), custom_call_target="tpu_custom_call" | custom-call | flops 15728640 | bytes 8388608 | tf_op jit(solution)/shard_map/own_adjoint/pallas_call | solution.py:433
  123.9 6.0 %collective-permute-start.19 = (f32[4,128,128]{2,1,0:T(8,128)S(1)}, f32[4,128,128]{2,1,0:T(8,128)S(1)}, u32[]{:S(2)}, u32[]{:S(2)}) collective-permute-start(f32[4,128,128]{2,1,0:T(8,128)S(1)} %edge_high.24.refs_7_.refs_5_.refs_8_), channel_id=1, source_target_pairs={{0,1},{1,0},{2,3},{3,2},{4,5},{5,4},{6,7},{7,6},{8,9},{9,8},{10,11... | collective-permute-start | bytes 786440 | tf_op jit(solution)/shard_map/ppermute | solution.py:292
  131.4 4.1 %own_adjoint.9 = (f32[8,128,128]{2,1,0:T(8,128)S(1)}, f32[4,128,128]{2,1,0:T(8,128)S(1)}, f32[4,128,128]{2,1,0:T(8,128)S(1)}, f32[16,128,128]{2,1,0:T(8,128)S(1)}) custom-call(s32[2]{0:T(128)S(1)} %pad_add_fusion.first_ref.refs_0_, s32[1,256]{1,0:T(1,128)S(1)} %copy-done.7, s32[4,384]{1,0:T(4,128)S(1)} %sort_receivers.1.refs_2_, ...), custom_call_target="tpu_custom_call" | custom-call | flops 15728640 | bytes 8388608 | tf_op jit(solution)/shard_map/own_adjoint/pallas_call | solution.py:433
  137.0 4.5 %collective-permute-start.21 = (f32[4,128,128]{2,1,0:T(8,128)S(1)}, f32[4,128,128]{2,1,0:T(8,128)S(1)}, u32[]{:S(2)}, u32[]{:S(2)}) collective-permute-start(f32[4,128,128]{2,1,0:T(8,128)S(1)} %edge_high.25.refs_7_.refs_5_.refs_8_), channel_id=1, source_target_pairs={{0,1},{1,0},{2,3},{3,2},{4,5},{5,4},{6,7},{7,6},{8,9},{9,8},{10,11... | collective-permute-start | bytes 786440 | tf_op jit(solution)/shard_map/ppermute | solution.py:292
  143.0 4.1 %own_adjoint.10 = (f32[8,128,128]{2,1,0:T(8,128)S(1)}, f32[4,128,128]{2,1,0:T(8,128)S(1)}, f32[4,128,128]{2,1,0:T(8,128)S(1)}, f32[16,128,128]{2,1,0:T(8,128)S(1)}) custom-call(s32[2]{0:T(128)S(1)} %pad_add_fusion.first_ref.refs_0_, s32[1,256]{1,0:T(1,128)S(1)} %copy-done.7, s32[4,384]{1,0:T(4,128)S(1)} %sort_receivers.1.refs_2_, ...), custom_call_target="tpu_custom_call" | custom-call | flops 15728640 | bytes 8388608 | tf_op jit(solution)/shard_map/own_adjoint/pallas_call | solution.py:433
  147.1 2.1 collective-permute-done.21.refs_3_
  150.0 7.4 %collective-permute-start.23 = (f32[4,128,128]{2,1,0:T(8,128)S(1)}, f32[4,128,128]{2,1,0:T(8,128)S(1)}, u32[]{:S(2)}, u32[]{:S(2)}) collective-permute-start(f32[4,128,128]{2,1,0:T(8,128)S(1)} %edge_high.26.refs_7_.refs_5_.refs_8_), channel_id=1, source_target_pairs={{0,1},{1,0},{2,3},{3,2},{4,5},{5,4},{6,7},{7,6},{8,9},{9,8},{10,11... | collective-permute-start | bytes 786440 | tf_op jit(solution)/shard_map/ppermute | solution.py:292
  158.8 4.1 %own_adjoint.11 = (f32[8,128,128]{2,1,0:T(8,128)S(1)}, f32[4,128,128]{2,1,0:T(8,128)S(1)}, f32[4,128,128]{2,1,0:T(8,128)S(1)}, f32[16,128,128]{2,1,0:T(8,128)S(1)}) custom-call(s32[2]{0:T(128)S(1)} %pad_add_fusion.first_ref.refs_0_, s32[1,256]{1,0:T(1,128)S(1)} %copy-done.7, s32[4,384]{1,0:T(4,128)S(1)} %sort_receivers.1.refs_2_, ...), custom_call_target="tpu_custom_call" | custom-call | flops 15728640 | bytes 8388608 | tf_op jit(solution)/shard_map/own_adjoint/pallas_call | solution.py:433
  164.6 5.2 %collective-permute-start.25 = (f32[4,128,128]{2,1,0:T(8,128)S(1)}, f32[4,128,128]{2,1,0:T(8,128)S(1)}, u32[]{:S(2)}, u32[]{:S(2)}) collective-permute-start(f32[4,128,128]{2,1,0:T(8,128)S(1)} %edge_high.27.refs_7_.refs_5_.refs_8_), channel_id=1, source_target_pairs={{0,1},{1,0},{2,3},{3,2},{4,5},{5,4},{6,7},{7,6},{8,9},{9,8},{10,11... | collective-permute-start | bytes 786440 | tf_op jit(solution)/shard_map/ppermute | solution.py:292
  171.3 4.1 %own_adjoint.12 = (f32[8,128,128]{2,1,0:T(8,128)S(1)}, f32[4,128,128]{2,1,0:T(8,128)S(1)}, f32[4,128,128]{2,1,0:T(8,128)S(1)}, f32[16,128,128]{2,1,0:T(8,128)S(1)}) custom-call(s32[2]{0:T(128)S(1)} %pad_add_fusion.first_ref.refs_0_, s32[1,256]{1,0:T(1,128)S(1)} %copy-done.7, s32[4,384]{1,0:T(4,128)S(1)} %sort_receivers.1.refs_2_, ...), custom_call_target="tpu_custom_call" | custom-call | flops 15728640 | bytes 8388608 | tf_op jit(solution)/shard_map/own_adjoint/pallas_call | solution.py:433
  175.4 2.1 collective-permute-done.25.refs_3_
  178.3 7.4 %collective-permute-start.27 = (f32[4,128,128]{2,1,0:T(8,128)S(1)}, f32[4,128,128]{2,1,0:T(8,128)S(1)}, u32[]{:S(2)}, u32[]{:S(2)}) collective-permute-start(f32[4,128,128]{2,1,0:T(8,128)S(1)} %edge_high.28.refs_7_.refs_5_.refs_8_), channel_id=1, source_target_pairs={{0,1},{1,0},{2,3},{3,2},{4,5},{5,4},{6,7},{7,6},{8,9},{9,8},{10,11... | collective-permute-start | bytes 786440 | tf_op jit(solution)/shard_map/ppermute | solution.py:292
  187.1 4.1 %own_adjoint.13 = (f32[8,128,128]{2,1,0:T(8,128)S(1)}, f32[4,128,128]{2,1,0:T(8,128)S(1)}, f32[4,128,128]{2,1,0:T(8,128)S(1)}, f32[16,128,128]{2,1,0:T(8,128)S(1)}) custom-call(s32[2]{0:T(128)S(1)} %pad_add_fusion.first_ref.refs_0_, s32[1,256]{1,0:T(1,128)S(1)} %copy-done.7, s32[4,384]{1,0:T(4,128)S(1)} %sort_receivers.1.refs_2_, ...), custom_call_target="tpu_custom_call" | custom-call | flops 15728640 | bytes 8388608 | tf_op jit(solution)/shard_map/own_adjoint/pallas_call | solution.py:433
  192.9 5.4 %collective-permute-start.29 = (f32[4,128,128]{2,1,0:T(8,128)S(1)}, f32[4,128,128]{2,1,0:T(8,128)S(1)}, u32[]{:S(2)}, u32[]{:S(2)}) collective-permute-start(f32[4,128,128]{2,1,0:T(8,128)S(1)} %edge_high.29.refs_7_.refs_5_.refs_8_), channel_id=1, source_target_pairs={{0,1},{1,0},{2,3},{3,2},{4,5},{5,4},{6,7},{7,6},{8,9},{9,8},{10,11... | collective-permute-start | bytes 786440 | tf_op jit(solution)/shard_map/ppermute | solution.py:292
  199.8 4.1 %own_adjoint.14 = (f32[8,128,128]{2,1,0:T(8,128)S(1)}, f32[4,128,128]{2,1,0:T(8,128)S(1)}, f32[4,128,128]{2,1,0:T(8,128)S(1)}, f32[16,128,128]{2,1,0:T(8,128)S(1)}) custom-call(s32[2]{0:T(128)S(1)} %pad_add_fusion.first_ref.refs_0_, s32[1,256]{1,0:T(1,128)S(1)} %copy-done.7, s32[4,384]{1,0:T(4,128)S(1)} %sort_receivers.1.refs_2_, ...), custom_call_target="tpu_custom_call" | custom-call | flops 15728640 | bytes 8388608 | tf_op jit(solution)/shard_map/own_adjoint/pallas_call | solution.py:433
  204.7 1.1 collective-permute-done.29.refs_3_
  206.6 8.2 %collective-permute-start.31 = (f32[4,128,128]{2,1,0:T(8,128)S(1)}, f32[4,128,128]{2,1,0:T(8,128)}, u32[]{:S(2)}, u32[]{:S(2)}) collective-permute-start(f32[4,128,128]{2,1,0:T(8,128)S(1)} %edge_high.30.refs_7_.refs_5_), channel_id=1, source_target_pairs={{0,1},{1,0},{2,3},{3,2},{4,5},{5,4},{6,7},{7,6},{8,9},{9,8},{10,11... | collective-permute-start | bytes 786440 | tf_op jit(solution)/shard_map/ppermute | solution.py:292
  214.7 1.5 edge_low.30.refs_3_
  216.2 1.3 collective-permute-start.30
  217.6 1.2 copy-done.2
  222.8 4.3 %own_adjoint.15 = (f32[8,128,128]{2,1,0:T(8,128)S(1)}, f32[4,128,128]{2,1,0:T(8,128)S(1)}, f32[4,128,128]{2,1,0:T(8,128)S(1)}, f32[16,128,128]{2,1,0:T(8,128)S(1)}) custom-call(s32[2]{0:T(128)S(1)} %pad_add_fusion.first_ref.refs_0_, s32[1,256]{1,0:T(1,128)S(1)} %copy-done.7, s32[4,384]{1,0:T(4,128)S(1)} %sort_receivers.1.refs_2_, ...), custom_call_target="tpu_custom_call" | custom-call | flops 15728640 | bytes 8388608 | tf_op jit(solution)/shard_map/own_adjoint/pallas_call | solution.py:433
  227.1 1.1 edge_high.31.refs_7_.a_high
  228.3 1.2 edge_low.31.a_low
  230.5 1.8 collective-permute-done.32
  232.5 1.6 collective-permute-start.33
  234.1 2.5 collective-permute-start.34
  236.6 1.7 collective-permute-start.35
  239.3 3.6 %collective-permute-done.34 = f32[2,128,128]{2,1,0:T(8,128)S(1)} collective-permute-done((f32[2,128,128]{2,1,0:T(8,128)S(1)}, f32[2,128,128]{2,1,0:T(8,128)S(1)}, u32[]{:S(2)}, u32[]{:S(2)}) %collective-permute-start.34) | collective-permute-done | bytes 131104 | tf_op jit(solution)/shard_map/ppermute | solution.py:292
  243.0 5.1 %collective-permute-start.36 = (f32[2,128,128]{2,1,0:T(8,128)S(1)}, f32[2,128,128]{2,1,0:T(8,128)S(1)}, u32[]{:S(2)}, u32[]{:S(2)}) collective-permute-start(f32[2,128,128]{2,1,0:T(8,128)S(1)} %add_add_fusion), channel_id=1, source_target_pairs={{0,128},{16,144},{32,160},{48,176},{64,192},{80,208},{96,224},{112... | collective-permute-start | bytes 393224 | tf_op jit(solution)/shard_map/ppermute | solution.py:292
  248.1 3.9 %collective-permute-done.36 = f32[2,128,128]{2,1,0:T(8,128)S(1)} collective-permute-done((f32[2,128,128]{2,1,0:T(8,128)S(1)}, f32[2,128,128]{2,1,0:T(8,128)S(1)}, u32[]{:S(2)}, u32[]{:S(2)}) %collective-permute-start.36) | collective-permute-done | bytes 131104 | tf_op jit(solution)/shard_map/ppermute | solution.py:292
  252.0 1.6 collective-permute-start.37
  253.6 2.5 collective-permute-start.38
  256.1 1.6 collective-permute-start.39
  257.6 1.5 collective-permute-done.37
  259.1 1.4 collective-permute-done.38
  261.2 1.9 collective-permute-done.40
  264.5 5.1 %collective-permute-start.41 = (f32[8,128]{1,0:T(8,128)S(1)}, f32[8,128]{1,0:T(8,128)S(1)}, u32[]{:S(2)}, u32[]{:S(2)}) collective-permute-start(f32[8,128]{1,0:T(8,128)S(1)} %broadcast_in_dim.7), channel_id=1, source_target_pairs={{0,4},{1,5},{2,6},{3,7},{4,8},{5,9},{6,10},{7,11},{8,12},{9,13},{1... | collective-permute-start | bytes 12296 | tf_op jit(solution)/shard_map/ppermute | solution.py:292
  269.6 3.3 %collective-permute-start.42 = (f32[8,128]{1,0:T(8,128)S(1)}, f32[8,128]{1,0:T(8,128)S(1)}, u32[]{:S(2)}, u32[]{:S(2)}) collective-permute-start(f32[8,128]{1,0:T(8,128)S(1)} %broadcast_in_dim.7), channel_id=1, source_target_pairs={{0,8},{1,9},{2,10},{3,11},{4,12},{5,13},{6,14},{7,15},{8,0},{9,1},... | collective-permute-start | bytes 12296 | tf_op jit(solution)/shard_map/ppermute | solution.py:292
  272.8 1.6 collective-permute-start.43
  274.7 1.8 collective-permute-done.43
  277.1 5.2 %collective-permute-start.44 = (f32[8,128]{1,0:T(8,128)S(1)}, f32[8,128]{1,0:T(8,128)S(1)}, u32[]{:S(2)}, u32[]{:S(2)}) collective-permute-start(f32[8,128]{1,0:T(8,128)S(1)} %maximum_maximum_fusion.1), channel_id=1, source_target_pairs={{0,1},{1,2},{2,3},{3,0},{4,5},{5,6},{6,7},{7,4},{8,9},{9,10},{10,1... | collective-permute-start | bytes 12296 | tf_op jit(solution)/shard_map/ppermute | solution.py:292
  282.3 1.3 collective-permute-start.45
  283.6 2.8 collective-permute-start.46
  288.9 1.5 subtract_multiply_fusion
  (150 shorter events, 52.8 us)
Async XLA Ops:
  0.6 3.1 %copy-start = (f32[16,128,128]{2,1,0:T(8,128)S(1)}, f32[16,128,128]{2,1,0:T(8,128)}, u32[]{:S(2)}) copy-start(f32[16,128,128]{2,1,0:T(8,128)} %whole_ref.1) | copy-start | bytes 3145732
  0.7 1.3 copy-start.3
  2.0 2.4 copy-start.4
  2.7 7.6 %collective-permute-start.2 = (f32[4,128,128]{2,1,0:T(8,128)S(1)}, f32[4,128,128]{2,1,0:T(8,128)S(1)}, u32[]{:S(2)}, u32[]{:S(2)}) collective-permute-start(f32[4,128,128]{2,1,0:T(8,128)S(1)} %get-tuple-element.148.refs_5_.refs_11_), channel_id=1, source_target_pairs={{0,1},{1,0},{2,3},{3,2},{4,5},{5,4},{6,7},{7,6},{8,9},{9,8},{10,11... | collective-permute-start | bytes 786440 | tf_op jit(solution)/shard_map/ppermute | solution.py:292
  3.0 13.9 %collective-permute-start.1 = (f32[4,128,128]{2,1,0:T(8,128)S(1)}, f32[4,128,128]{2,1,0:T(8,128)S(1)}, u32[]{:S(2)}, u32[]{:S(2)}) collective-permute-start(f32[4,128,128]{2,1,0:T(8,128)S(1)} %get-tuple-element.146.refs_3_.refs_9_), channel_id=1, source_target_pairs={{1,2},{2,1},{3,4},{4,3},{5,6},{6,5},{7,8},{8,7},{9,10},{10,9},{11,... | collective-permute-start | bytes 786440 | tf_op jit(solution)/shard_map/ppermute | solution.py:292
  11.8 17.4 %collective-permute-start.4 = (f32[4,128,128]{2,1,0:T(8,128)S(1)}, f32[4,128,128]{2,1,0:T(8,128)S(1)}, u32[]{:S(2)}, u32[]{:S(2)}) collective-permute-start(f32[4,128,128]{2,1,0:T(8,128)S(1)} %get-tuple-element.156.refs_7_.refs_8_.refs_11_), channel_id=1, source_target_pairs={{0,1},{1,0},{2,3},{3,2},{4,5},{5,4},{6,7},{7,6},{8,9},{9,8},{10,11... | collective-permute-start | bytes 786440 | tf_op jit(solution)/shard_map/ppermute | solution.py:292
  17.6 11.7 %copy-start.18 = (f32[4,128,128]{2,1,0:T(8,128)}, f32[4,128,128]{2,1,0:T(8,128)S(1)}, u32[]{:S(2)}) copy-start(f32[4,128,128]{2,1,0:T(8,128)S(1)} %get-tuple-element.269.b_low) | copy-start | bytes 786436
  17.6 7.3 %copy-start.8 = (f32[1,8,256]{2,1,0:T(8,128)S(1)}, f32[1,8,256]{2,1,0:T(8,128)}, u32[]{:S(2)}) copy-start(f32[1,8,256]{2,1,0:T(8,128)} %param.17) | copy-start | bytes 24580
  17.6 17.2 %collective-permute-start.3 = (f32[4,128,128]{2,1,0:T(8,128)S(1)}, f32[4,128,128]{2,1,0:T(8,128)S(1)}, u32[]{:S(2)}, u32[]{:S(2)}) collective-permute-start(f32[4,128,128]{2,1,0:T(8,128)S(1)} %get-tuple-element.157.refs_6_.refs_9_), channel_id=1, source_target_pairs={{1,2},{2,1},{3,4},{4,3},{5,6},{6,5},{7,8},{8,7},{9,10},{10,9},{11,... | collective-permute-start | bytes 786440 | tf_op jit(solution)/shard_map/ppermute | solution.py:292
  30.1 5.4 %copy-start.20 = (f32[4,128,128]{2,1,0:T(8,128)}, f32[4,128,128]{2,1,0:T(8,128)S(1)}, u32[]{:S(2)}) copy-start(f32[4,128,128]{2,1,0:T(8,128)S(1)} %get-tuple-element.263.refs_15_) | copy-start | bytes 786436
  30.1 10.5 %collective-permute-start.6 = (f32[4,128,128]{2,1,0:T(8,128)S(1)}, f32[4,128,128]{2,1,0:T(8,128)S(1)}, u32[]{:S(2)}, u32[]{:S(2)}) collective-permute-start(f32[4,128,128]{2,1,0:T(8,128)S(1)} %get-tuple-element.163.refs_7_.refs_8_.refs_11_), channel_id=1, source_target_pairs={{0,1},{1,0},{2,3},{3,2},{4,5},{5,4},{6,7},{7,6},{8,9},{9,8},{10,11... | collective-permute-start | bytes 786440 | tf_op jit(solution)/shard_map/ppermute | solution.py:292
  35.5 5.1 %copy-start.22 = (f32[4,128,128]{2,1,0:T(8,128)}, f32[4,128,128]{2,1,0:T(8,128)S(1)}, u32[]{:S(2)}) copy-start(f32[4,128,128]{2,1,0:T(8,128)S(1)} %get-tuple-element.261.refs_13_) | copy-start | bytes 786436
  35.5 10.3 %collective-permute-start.5 = (f32[4,128,128]{2,1,0:T(8,128)S(1)}, f32[4,128,128]{2,1,0:T(8,128)S(1)}, u32[]{:S(2)}, u32[]{:S(2)}) collective-permute-start(f32[4,128,128]{2,1,0:T(8,128)S(1)} %get-tuple-element.164.refs_6_.refs_9_), channel_id=1, source_target_pairs={{1,2},{2,1},{3,4},{4,3},{5,6},{6,5},{7,8},{8,7},{9,10},{10,9},{11,... | collective-permute-start | bytes 786440 | tf_op jit(solution)/shard_map/ppermute | solution.py:292
  41.2 13.2 %collective-permute-start.8 = (f32[4,128,128]{2,1,0:T(8,128)S(1)}, f32[4,128,128]{2,1,0:T(8,128)S(1)}, u32[]{:S(2)}, u32[]{:S(2)}) collective-permute-start(f32[4,128,128]{2,1,0:T(8,128)S(1)} %get-tuple-element.170.refs_7_.refs_8_.refs_11_), channel_id=1, source_target_pairs={{0,1},{1,0},{2,3},{3,2},{4,5},{5,4},{6,7},{7,6},{8,9},{9,8},{10,11... | collective-permute-start | bytes 786440 | tf_op jit(solution)/shard_map/ppermute | solution.py:292
  46.5 12.8 %collective-permute-start.7 = (f32[4,128,128]{2,1,0:T(8,128)S(1)}, f32[4,128,128]{2,1,0:T(8,128)S(1)}, u32[]{:S(2)}, u32[]{:S(2)}) collective-permute-start(f32[4,128,128]{2,1,0:T(8,128)S(1)} %get-tuple-element.171.refs_6_.refs_9_), channel_id=1, source_target_pairs={{1,2},{2,1},{3,4},{4,3},{5,6},{6,5},{7,8},{8,7},{9,10},{10,9},{11,... | collective-permute-start | bytes 786440 | tf_op jit(solution)/shard_map/ppermute | solution.py:292
  55.0 11.6 %collective-permute-start.10 = (f32[4,128,128]{2,1,0:T(8,128)S(1)}, f32[4,128,128]{2,1,0:T(8,128)S(1)}, u32[]{:S(2)}, u32[]{:S(2)}) collective-permute-start(f32[4,128,128]{2,1,0:T(8,128)S(1)} %get-tuple-element.177.refs_7_.refs_8_.refs_11_), channel_id=1, source_target_pairs={{0,1},{1,0},{2,3},{3,2},{4,5},{5,4},{6,7},{7,6},{8,9},{9,8},{10,11... | collective-permute-start | bytes 786440 | tf_op jit(solution)/shard_map/ppermute | solution.py:292
  59.9 13.8 %collective-permute-start.9 = (f32[4,128,128]{2,1,0:T(8,128)S(1)}, f32[4,128,128]{2,1,0:T(8,128)S(1)}, u32[]{:S(2)}, u32[]{:S(2)}) collective-permute-start(f32[4,128,128]{2,1,0:T(8,128)S(1)} %get-tuple-element.178.refs_6_.refs_9_), channel_id=1, source_target_pairs={{1,2},{2,1},{3,4},{4,3},{5,6},{6,5},{7,8},{8,7},{9,10},{10,9},{11,... | collective-permute-start | bytes 786440 | tf_op jit(solution)/shard_map/ppermute | solution.py:292
  67.3 12.9 %collective-permute-start.12 = (f32[4,128,128]{2,1,0:T(8,128)S(1)}, f32[4,128,128]{2,1,0:T(8,128)S(1)}, u32[]{:S(2)}, u32[]{:S(2)}) collective-permute-start(f32[4,128,128]{2,1,0:T(8,128)S(1)} %get-tuple-element.184.refs_7_.refs_8_.refs_11_), channel_id=1, source_target_pairs={{0,1},{1,0},{2,3},{3,2},{4,5},{5,4},{6,7},{7,6},{8,9},{9,8},{10,11... | collective-permute-start | bytes 786440 | tf_op jit(solution)/shard_map/ppermute | solution.py:292
  74.3 12.9 %collective-permute-start.11 = (f32[4,128,128]{2,1,0:T(8,128)S(1)}, f32[4,128,128]{2,1,0:T(8,128)S(1)}, u32[]{:S(2)}, u32[]{:S(2)}) collective-permute-start(f32[4,128,128]{2,1,0:T(8,128)S(1)} %get-tuple-element.185.refs_6_.refs_9_), channel_id=1, source_target_pairs={{1,2},{2,1},{3,4},{4,3},{5,6},{6,5},{7,8},{8,7},{9,10},{10,9},{11,... | collective-permute-start | bytes 786440 | tf_op jit(solution)/shard_map/ppermute | solution.py:292
  80.8 13.0 %collective-permute-start.14 = (f32[4,128,128]{2,1,0:T(8,128)S(1)}, f32[4,128,128]{2,1,0:T(8,128)S(1)}, u32[]{:S(2)}, u32[]{:S(2)}) collective-permute-start(f32[4,128,128]{2,1,0:T(8,128)S(1)} %get-tuple-element.191.refs_7_.refs_8_.refs_11_), channel_id=1, source_target_pairs={{0,1},{1,0},{2,3},{3,2},{4,5},{5,4},{6,7},{7,6},{8,9},{9,8},{10,11... | collective-permute-start | bytes 786440 | tf_op jit(solution)/shard_map/ppermute | solution.py:292
  87.9 14.1 %collective-permute-start.13 = (f32[4,128,128]{2,1,0:T(8,128)S(1)}, f32[4,128,128]{2,1,0:T(8,128)S(1)}, u32[]{:S(2)}, u32[]{:S(2)}) collective-permute-start(f32[4,128,128]{2,1,0:T(8,128)S(1)} %get-tuple-element.192.refs_6_.refs_9_), channel_id=1, source_target_pairs={{1,2},{2,1},{3,4},{4,3},{5,6},{6,5},{7,8},{8,7},{9,10},{10,9},{11,... | collective-permute-start | bytes 786440 | tf_op jit(solution)/shard_map/ppermute | solution.py:292
  93.8 9.5 %copy-start.5 = (f32[1,16,128,128]{3,2,1,0:T(8,128)S(1)}, f32[1,16,128,128]{3,2,1,0:T(8,128)}, u32[]{:S(2)}) copy-start(f32[1,16,128,128]{3,2,1,0:T(8,128)} %param.13) | copy-start | bytes 3145732
  94.4 22.4 %collective-permute-start.16 = (f32[4,128,128]{2,1,0:T(8,128)S(1)}, f32[4,128,128]{2,1,0:T(8,128)S(1)}, u32[]{:S(2)}, u32[]{:S(2)}) collective-permute-start(f32[4,128,128]{2,1,0:T(8,128)S(1)} %get-tuple-element.198.refs_7_.refs_8_), channel_id=1, source_target_pairs={{0,1},{1,0},{2,3},{3,2},{4,5},{5,4},{6,7},{7,6},{8,9},{9,8},{10,11... | collective-permute-start | bytes 786440 | tf_op jit(solution)/shard_map/ppermute | solution.py:292
  102.0 9.8 %copy-start.6 = (f32[1,16,128,128]{3,2,1,0:T(8,128)S(1)}, f32[1,16,128,128]{3,2,1,0:T(8,128)}, u32[]{:S(2)}) copy-start(f32[1,16,128,128]{3,2,1,0:T(8,128)} %param.12) | copy-start | bytes 3145732
  102.6 14.9 %collective-permute-start.15 = (f32[4,128,128]{2,1,0:T(8,128)S(1)}, f32[4,128,128]{2,1,0:T(8,128)S(1)}, u32[]{:S(2)}, u32[]{:S(2)}) collective-permute-start(f32[4,128,128]{2,1,0:T(8,128)S(1)} %get-tuple-element.199.refs_6_), channel_id=1, source_target_pairs={{1,2},{2,1},{3,4},{4,3},{5,6},{6,5},{7,8},{8,7},{9,10},{10,9},{11,... | collective-permute-start | bytes 786440 | tf_op jit(solution)/shard_map/ppermute | solution.py:292
  104.0 19.0 %collective-permute-start.17 = (f32[4,128,128]{2,1,0:T(8,128)S(1)}, f32[4,128,128]{2,1,0:T(8,128)S(1)}, u32[]{:S(2)}, u32[]{:S(2)}) collective-permute-start(f32[4,128,128]{2,1,0:T(8,128)S(1)} %get-tuple-element.139.refs_6_.refs_8_), channel_id=1, source_target_pairs={{0,1},{1,0},{2,3},{3,2},{4,5},{5,4},{6,7},{7,6},{8,9},{9,8},{10,11... | collective-permute-start | bytes 786440 | tf_op jit(solution)/shard_map/ppermute | solution.py:292
  111.1 18.8 %collective-permute-start = (f32[4,128,128]{2,1,0:T(8,128)S(1)}, f32[4,128,128]{2,1,0:T(8,128)S(1)}, u32[]{:S(2)}, u32[]{:S(2)}) collective-permute-start(f32[4,128,128]{2,1,0:T(8,128)S(1)} %get-tuple-element.137.refs_4_.refs_6_), channel_id=1, source_target_pairs={{1,2},{2,1},{3,4},{4,3},{5,6},{6,5},{7,8},{8,7},{9,10},{10,9},{11,... | collective-permute-start | bytes 786440 | tf_op jit(solution)/shard_map/ppermute | solution.py:292
  123.9 12.3 %collective-permute-start.19 = (f32[4,128,128]{2,1,0:T(8,128)S(1)}, f32[4,128,128]{2,1,0:T(8,128)S(1)}, u32[]{:S(2)}, u32[]{:S(2)}) collective-permute-start(f32[4,128,128]{2,1,0:T(8,128)S(1)} %edge_high.24.refs_7_.refs_5_.refs_8_), channel_id=1, source_target_pairs={{0,1},{1,0},{2,3},{3,2},{4,5},{5,4},{6,7},{7,6},{8,9},{9,8},{10,11... | collective-permute-start | bytes 786440 | tf_op jit(solution)/shard_map/ppermute | solution.py:292
  130.7 10.8 %collective-permute-start.18 = (f32[4,128,128]{2,1,0:T(8,128)S(1)}, f32[4,128,128]{2,1,0:T(8,128)S(1)}, u32[]{:S(2)}, u32[]{:S(2)}) collective-permute-start(f32[4,128,128]{2,1,0:T(8,128)S(1)} %edge_low.24.refs_3_.refs_6_), channel_id=1, source_target_pairs={{1,2},{2,1},{3,4},{4,3},{5,6},{6,5},{7,8},{8,7},{9,10},{10,9},{11,... | collective-permute-start | bytes 786440 | tf_op jit(solution)/shard_map/ppermute | solution.py:292
  137.0 12.2 %collective-permute-start.21 = (f32[4,128,128]{2,1,0:T(8,128)S(1)}, f32[4,128,128]{2,1,0:T(8,128)S(1)}, u32[]{:S(2)}, u32[]{:S(2)}) collective-permute-start(f32[4,128,128]{2,1,0:T(8,128)S(1)} %edge_high.25.refs_7_.refs_5_.refs_8_), channel_id=1, source_target_pairs={{0,1},{1,0},{2,3},{3,2},{4,5},{5,4},{6,7},{7,6},{8,9},{9,8},{10,11... | collective-permute-start | bytes 786440 | tf_op jit(solution)/shard_map/ppermute | solution.py:292
  142.3 15.0 %collective-permute-start.20 = (f32[4,128,128]{2,1,0:T(8,128)S(1)}, f32[4,128,128]{2,1,0:T(8,128)S(1)}, u32[]{:S(2)}, u32[]{:S(2)}) collective-permute-start(f32[4,128,128]{2,1,0:T(8,128)S(1)} %edge_low.25.refs_3_.refs_6_), channel_id=1, source_target_pairs={{1,2},{2,1},{3,4},{4,3},{5,6},{6,5},{7,8},{8,7},{9,10},{10,9},{11,... | collective-permute-start | bytes 786440 | tf_op jit(solution)/shard_map/ppermute | solution.py:292
  150.0 13.9 %collective-permute-start.23 = (f32[4,128,128]{2,1,0:T(8,128)S(1)}, f32[4,128,128]{2,1,0:T(8,128)S(1)}, u32[]{:S(2)}, u32[]{:S(2)}) collective-permute-start(f32[4,128,128]{2,1,0:T(8,128)S(1)} %edge_high.26.refs_7_.refs_5_.refs_8_), channel_id=1, source_target_pairs={{0,1},{1,0},{2,3},{3,2},{4,5},{5,4},{6,7},{7,6},{8,9},{9,8},{10,11... | collective-permute-start | bytes 786440 | tf_op jit(solution)/shard_map/ppermute | solution.py:292
  158.1 11.7 %collective-permute-start.22 = (f32[4,128,128]{2,1,0:T(8,128)S(1)}, f32[4,128,128]{2,1,0:T(8,128)S(1)}, u32[]{:S(2)}, u32[]{:S(2)}) collective-permute-start(f32[4,128,128]{2,1,0:T(8,128)S(1)} %edge_low.26.refs_3_.refs_6_), channel_id=1, source_target_pairs={{1,2},{2,1},{3,4},{4,3},{5,6},{6,5},{7,8},{8,7},{9,10},{10,9},{11,... | collective-permute-start | bytes 786440 | tf_op jit(solution)/shard_map/ppermute | solution.py:292
  164.6 12.9 %collective-permute-start.25 = (f32[4,128,128]{2,1,0:T(8,128)S(1)}, f32[4,128,128]{2,1,0:T(8,128)S(1)}, u32[]{:S(2)}, u32[]{:S(2)}) collective-permute-start(f32[4,128,128]{2,1,0:T(8,128)S(1)} %edge_high.27.refs_7_.refs_5_.refs_8_), channel_id=1, source_target_pairs={{0,1},{1,0},{2,3},{3,2},{4,5},{5,4},{6,7},{7,6},{8,9},{9,8},{10,11... | collective-permute-start | bytes 786440 | tf_op jit(solution)/shard_map/ppermute | solution.py:292
  170.6 15.0 %collective-permute-start.24 = (f32[4,128,128]{2,1,0:T(8,128)S(1)}, f32[4,128,128]{2,1,0:T(8,128)S(1)}, u32[]{:S(2)}, u32[]{:S(2)}) collective-permute-start(f32[4,128,128]{2,1,0:T(8,128)S(1)} %edge_low.27.refs_3_.refs_6_), channel_id=1, source_target_pairs={{1,2},{2,1},{3,4},{4,3},{5,6},{6,5},{7,8},{8,7},{9,10},{10,9},{11,... | collective-permute-start | bytes 786440 | tf_op jit(solution)/shard_map/ppermute | solution.py:292
  178.3 13.9 %collective-permute-start.27 = (f32[4,128,128]{2,1,0:T(8,128)S(1)}, f32[4,128,128]{2,1,0:T(8,128)S(1)}, u32[]{:S(2)}, u32[]{:S(2)}) collective-permute-start(f32[4,128,128]{2,1,0:T(8,128)S(1)} %edge_high.28.refs_7_.refs_5_.refs_8_), channel_id=1, source_target_pairs={{0,1},{1,0},{2,3},{3,2},{4,5},{5,4},{6,7},{7,6},{8,9},{9,8},{10,11... | collective-permute-start | bytes 786440 | tf_op jit(solution)/shard_map/ppermute | solution.py:292
  186.4 11.8 %collective-permute-start.26 = (f32[4,128,128]{2,1,0:T(8,128)S(1)}, f32[4,128,128]{2,1,0:T(8,128)S(1)}, u32[]{:S(2)}, u32[]{:S(2)}) collective-permute-start(f32[4,128,128]{2,1,0:T(8,128)S(1)} %edge_low.28.refs_3_.refs_6_), channel_id=1, source_target_pairs={{1,2},{2,1},{3,4},{4,3},{5,6},{6,5},{7,8},{8,7},{9,10},{10,9},{11,... | collective-permute-start | bytes 786440 | tf_op jit(solution)/shard_map/ppermute | solution.py:292
  192.9 12.9 %collective-permute-start.29 = (f32[4,128,128]{2,1,0:T(8,128)S(1)}, f32[4,128,128]{2,1,0:T(8,128)S(1)}, u32[]{:S(2)}, u32[]{:S(2)}) collective-permute-start(f32[4,128,128]{2,1,0:T(8,128)S(1)} %edge_high.29.refs_7_.refs_5_.refs_8_), channel_id=1, source_target_pairs={{0,1},{1,0},{2,3},{3,2},{4,5},{5,4},{6,7},{7,6},{8,9},{9,8},{10,11... | collective-permute-start | bytes 786440 | tf_op jit(solution)/shard_map/ppermute | solution.py:292
  199.1 15.6 %collective-permute-start.28 = (f32[4,128,128]{2,1,0:T(8,128)S(1)}, f32[4,128,128]{2,1,0:T(8,128)S(1)}, u32[]{:S(2)}, u32[]{:S(2)}) collective-permute-start(f32[4,128,128]{2,1,0:T(8,128)S(1)} %edge_low.29.refs_3_.refs_6_), channel_id=1, source_target_pairs={{1,2},{2,1},{3,4},{4,3},{5,6},{6,5},{7,8},{8,7},{9,10},{10,9},{11,... | collective-permute-start | bytes 786440 | tf_op jit(solution)/shard_map/ppermute | solution.py:292
  204.7 11.6 %copy-start.1 = (f32[16,128,128]{2,1,0:T(8,128)}, f32[16,128,128]{2,1,0:T(8,128)S(1)}, u32[]{:S(2)}) copy-start(f32[16,128,128]{2,1,0:T(8,128)S(1)} %get-tuple-element.264.refs_16_) | copy-start | bytes 3145732
  206.6 20.6 %collective-permute-start.31 = (f32[4,128,128]{2,1,0:T(8,128)S(1)}, f32[4,128,128]{2,1,0:T(8,128)}, u32[]{:S(2)}, u32[]{:S(2)}) collective-permute-start(f32[4,128,128]{2,1,0:T(8,128)S(1)} %edge_high.30.refs_7_.refs_5_), channel_id=1, source_target_pairs={{0,1},{1,0},{2,3},{3,2},{4,5},{5,4},{6,7},{7,6},{8,9},{9,8},{10,11... | collective-permute-start | bytes 786440 | tf_op jit(solution)/shard_map/ppermute | solution.py:292
  216.2 12.1 %collective-permute-start.30 = (f32[4,128,128]{2,1,0:T(8,128)}, f32[4,128,128]{2,1,0:T(8,128)}, u32[]{:S(2)}, u32[]{:S(2)}) collective-permute-start(f32[4,128,128]{2,1,0:T(8,128)} %edge_low.30.refs_3_), channel_id=1, source_target_pairs={{1,2},{2,1},{3,4},{4,3},{5,6},{6,5},{7,8},{8,7},{9,10},{10,9},{11,... | collective-permute-start | bytes 786440 | tf_op jit(solution)/shard_map/ppermute | solution.py:292
  217.6 1.2 copy-start.2
  218.8 1.0 copy-start.12
  219.8 1.0 copy-start.14
  220.9 0.9 copy-start.21
  228.2 1.3 copy-start.10
  228.3 1.3 copy-start.17
  228.3 1.3 copy-start.19
  230.4 2.0 collective-permute-start.32
  232.5 6.8 %collective-permute-start.33 = (f32[2,128,128]{2,1,0:T(8,128)S(1)}, f32[2,128,128]{2,1,0:T(8,128)S(1)}, u32[]{:S(2)}, u32[]{:S(2)}) collective-permute-start(f32[2,128,128]{2,1,0:T(8,128)S(1)} %get-tuple-element.278), channel_id=1, source_target_pairs={{0,32},{16,48},{32,64},{48,80},{64,96},{80,112},{96,0},{112,16},{1... | collective-permute-start | bytes 393224 | tf_op jit(solution)/shard_map/ppermute | solution.py:292
  234.1 8.8 %collective-permute-start.34 = (f32[2,128,128]{2,1,0:T(8,128)S(1)}, f32[2,128,128]{2,1,0:T(8,128)S(1)}, u32[]{:S(2)}, u32[]{:S(2)}) collective-permute-start(f32[2,128,128]{2,1,0:T(8,128)S(1)} %get-tuple-element.280), channel_id=1, source_target_pairs={{0,64},{16,80},{32,96},{48,112},{64,0},{80,16},{96,32},{112,48},{1... | collective-permute-start | bytes 393224 | tf_op jit(solution)/shard_map/ppermute | solution.py:292
  236.6 6.3 %collective-permute-start.35 = (f32[2,128,128]{2,1,0:T(8,128)S(1)}, f32[2,128,128]{2,1,0:T(8,128)S(1)}, u32[]{:S(2)}, u32[]{:S(2)}) collective-permute-start(f32[2,128,128]{2,1,0:T(8,128)S(1)} %get-tuple-element.279), channel_id=1, source_target_pairs={{0,96},{16,112},{32,0},{48,16},{64,32},{80,48},{96,64},{112,80},{1... | collective-permute-start | bytes 393224 | tf_op jit(solution)/shard_map/ppermute | solution.py:292
  243.0 9.0 %collective-permute-start.36 = (f32[2,128,128]{2,1,0:T(8,128)S(1)}, f32[2,128,128]{2,1,0:T(8,128)S(1)}, u32[]{:S(2)}, u32[]{:S(2)}) collective-permute-start(f32[2,128,128]{2,1,0:T(8,128)S(1)} %add_add_fusion), channel_id=1, source_target_pairs={{0,128},{16,144},{32,160},{48,176},{64,192},{80,208},{96,224},{112... | collective-permute-start | bytes 393224 | tf_op jit(solution)/shard_map/ppermute | solution.py:292
  252.0 7.1 %collective-permute-start.37 = (f32[2,128,128]{2,1,0:T(8,128)S(1)}, f32[2,128,128]{2,1,0:T(8,128)S(1)}, u32[]{:S(2)}, u32[]{:S(2)}) collective-permute-start(f32[2,128,128]{2,1,0:T(8,128)S(1)} %get-tuple-element.275), channel_id=1, source_target_pairs={{0,32},{16,48},{32,64},{48,80},{64,96},{80,112},{96,0},{112,16},{1... | collective-permute-start | bytes 393224 | tf_op jit(solution)/shard_map/ppermute | solution.py:292
  253.6 7.0 %collective-permute-start.38 = (f32[2,128,128]{2,1,0:T(8,128)S(1)}, f32[2,128,128]{2,1,0:T(8,128)S(1)}, u32[]{:S(2)}, u32[]{:S(2)}) collective-permute-start(f32[2,128,128]{2,1,0:T(8,128)S(1)} %get-tuple-element.275), channel_id=1, source_target_pairs={{0,64},{16,80},{32,96},{48,112},{64,0},{80,16},{96,32},{112,48},{1... | collective-permute-start | bytes 393224 | tf_op jit(solution)/shard_map/ppermute | solution.py:292
  256.1 5.0 %collective-permute-start.39 = (f32[2,128,128]{2,1,0:T(8,128)S(1)}, f32[2,128,128]{2,1,0:T(8,128)S(1)}, u32[]{:S(2)}, u32[]{:S(2)}) collective-permute-start(f32[2,128,128]{2,1,0:T(8,128)S(1)} %get-tuple-element.275), channel_id=1, source_target_pairs={{0,96},{16,112},{32,0},{48,16},{64,32},{80,48},{96,64},{112,80},{1... | collective-permute-start | bytes 393224 | tf_op jit(solution)/shard_map/ppermute | solution.py:292
  261.1 2.0 collective-permute-start.40
  264.5 9.9 %collective-permute-start.41 = (f32[8,128]{1,0:T(8,128)S(1)}, f32[8,128]{1,0:T(8,128)S(1)}, u32[]{:S(2)}, u32[]{:S(2)}) collective-permute-start(f32[8,128]{1,0:T(8,128)S(1)} %broadcast_in_dim.7), channel_id=1, source_target_pairs={{0,4},{1,5},{2,6},{3,7},{4,8},{5,9},{6,10},{7,11},{8,12},{9,13},{1... | collective-permute-start | bytes 12296 | tf_op jit(solution)/shard_map/ppermute | solution.py:292
  269.6 5.1 %collective-permute-start.42 = (f32[8,128]{1,0:T(8,128)S(1)}, f32[8,128]{1,0:T(8,128)S(1)}, u32[]{:S(2)}, u32[]{:S(2)}) collective-permute-start(f32[8,128]{1,0:T(8,128)S(1)} %broadcast_in_dim.7), channel_id=1, source_target_pairs={{0,8},{1,9},{2,10},{3,11},{4,12},{5,13},{6,14},{7,15},{8,0},{9,1},... | collective-permute-start | bytes 12296 | tf_op jit(solution)/shard_map/ppermute | solution.py:292
  272.8 3.6 %collective-permute-start.43 = (f32[8,128]{1,0:T(8,128)S(1)}, f32[8,128]{1,0:T(8,128)S(1)}, u32[]{:S(2)}, u32[]{:S(2)}) collective-permute-start(f32[8,128]{1,0:T(8,128)S(1)} %broadcast_in_dim.7), channel_id=1, source_target_pairs={{0,12},{1,13},{2,14},{3,15},{4,0},{5,1},{6,2},{7,3},{8,4},{9,5},{1... | collective-permute-start | bytes 12296 | tf_op jit(solution)/shard_map/ppermute | solution.py:292
  277.1 9.3 %collective-permute-start.44 = (f32[8,128]{1,0:T(8,128)S(1)}, f32[8,128]{1,0:T(8,128)S(1)}, u32[]{:S(2)}, u32[]{:S(2)}) collective-permute-start(f32[8,128]{1,0:T(8,128)S(1)} %maximum_maximum_fusion.1), channel_id=1, source_target_pairs={{0,1},{1,2},{2,3},{3,0},{4,5},{5,6},{6,7},{7,4},{8,9},{9,10},{10,1... | collective-permute-start | bytes 12296 | tf_op jit(solution)/shard_map/ppermute | solution.py:292
  282.3 4.5 %collective-permute-start.45 = (f32[8,128]{1,0:T(8,128)S(1)}, f32[8,128]{1,0:T(8,128)S(1)}, u32[]{:S(2)}, u32[]{:S(2)}) collective-permute-start(f32[8,128]{1,0:T(8,128)S(1)} %maximum_maximum_fusion.1), channel_id=1, source_target_pairs={{0,2},{1,3},{2,0},{3,1},{4,6},{5,7},{6,4},{7,5},{8,10},{9,11},{10,... | collective-permute-start | bytes 12296 | tf_op jit(solution)/shard_map/ppermute | solution.py:292
  283.6 4.2 %collective-permute-start.46 = (f32[8,128]{1,0:T(8,128)S(1)}, f32[8,128]{1,0:T(8,128)S(1)}, u32[]{:S(2)}, u32[]{:S(2)}) collective-permute-start(f32[8,128]{1,0:T(8,128)S(1)} %maximum_maximum_fusion.1), channel_id=1, source_target_pairs={{0,3},{1,0},{2,1},{3,2},{4,7},{5,4},{6,5},{7,6},{8,11},{9,8},{10,9... | collective-permute-start | bytes 12296 | tf_op jit(solution)/shard_map/ppermute | solution.py:292
  (7 other events, 5.6 us)
